TPU v7x, 32 devices: a whole 2x2x4 slice. The times are simulated.
32 devices in a mesh: req: 4 (over y, core), seq: 4 (over z), tp: 2 (over x).
Axes of the slice: x: 2, y: 2, z: 4, core: 2. Of those that a mesh axis runs over, the one named last changes fastest.
Arguments:
- x_short: bfloat16 [32, 32, 1024], P(('req', 'seq')), may hold values from -6 to 6
- x_long: bfloat16 [4, 32, 1024], P('req'), may hold values from -6 to 6
- parents: int32 [32, 32], P(('req', 'seq')), may hold values from 0 to 30, as said below
- long_parents: int32 [4, 32], P('req'), may hold values from 0 to 30, as said below
- short_len: int32 [32], P(('req', 'seq')), may hold values from 1 to 512
- long_len: int32 [4], P('req'), may hold values from 1 to 1024
- doc_ids: int32 [32], replicated, may hold values from 0 to 31
- long_doc: int32 [4], replicated, may hold values from 0 to 31
- short_kv: bfloat16 [32, 2, 512, 1024], P(('req', 'seq'), None, None, 'tp'), as said below
- long_kv: bfloat16 [4, 2, 1024, 1024], P('req', None, 'seq', 'tp'), as said below
- enc_kv: bfloat16 [2, 32, 1024, 1024], P(None, None, ('req', 'seq'), 'tp'), as said below
- w_qkv: bfloat16 [3, 1024, 1024], P(None, None, 'tp'), may hold values from -0.1875 to 0.1875
- w_out: bfloat16 [1024, 1024], P('tp'), may hold values from -0.1875 to 0.1875
- w_cross_q: bfloat16 [1024, 1024], P(None, 'tp'), may hold values from -0.1875 to 0.1875
- w_cross_out: bfloat16 [1024, 1024], P('tp'), may hold values from -0.1875 to 0.1875
- w_up: bfloat16 [1024, 4096], P(None, 'tp'), may hold values from -0.1875 to 0.1875
- w_down: bfloat16 [4096, 1024], P('tp'), may hold values from -0.09375 to 0.09375
Outputs:
- y_short: bfloat16 [32, 32, 1024], P(('req', 'seq'))
- y_long: bfloat16 [4, 32, 1024], P('req')
Inputs may be any that keep to these rules, and one draw needn't show every extreme that they name: parents[r, 0] is 0 and is ignored; for node i > 0, parents[r, i] lies in 0 to i - 1; the last node's parent is node 30. long_parents[r, 0] is 0 and is ignored; for node i > 0, long_parents[r, i] lies in 0 to i - 1; the last node's parent is node 30. `short_kv`: entries lie within -68 to 68. `long_kv`: entries lie within -68 to 68. `enc_kv`: entries lie within -68 to 68.
All inputs are finite; a program needn't handle non-finite values.
Results may differ from a plain program's by a relative error of at most 0.035.
Values may be sent and summed in bfloat16 or wider, within the bound.
No kernel may reach another device: no remote copies, remote signals or barrier semaphores. Data moves between devices by JAX's collectives and lax.ppermute only.
A program may use at most 192 MiB of HBM per device.

v0:
```python
import jax
import jax.numpy as jnp
from jax import lax
from jax.sharding import PartitionSpec as P

HD = 64


MASKED_SCORE = -1e30
NORM_EPSILON = 1e-05
PRECISE = lax.Precision.HIGHEST


def ancestry(parents):
    node_ids = jnp.arange(parents.shape[-1], dtype=jnp.int32)
    parent_hot = (parents[..., :, None] == node_ids[None, None, :]).astype(jnp.float32)
    parent_hot = parent_hot * (node_ids[:, None] > 0).astype(jnp.float32)
    closure = jnp.eye(parents.shape[-1], dtype=jnp.float32)[None] + parent_hot
    path_span = 1
    while path_span < parents.shape[-1]:
        closure = jnp.minimum(jnp.einsum("rij,rjk->rik", closure, closure, precision=PRECISE), 1.0)
        path_span = path_span * 2
    return closure > 0.5


def partial_softmax(queries, key_rows, value_rows, allowed):
    scores = jnp.einsum(
        "nhe,che->hnc", queries, key_rows, preferred_element_type=jnp.float32
    ) * HD ** (-0.5)
    scores = jnp.where(allowed, scores, MASKED_SCORE)
    maxima = jnp.max(scores, axis=-1)
    weights = jnp.where(allowed, jnp.exp(scores - maxima[..., None]), 0.0)
    totals = jnp.sum(weights, axis=-1)
    weighted = jnp.einsum(
        "hnc,che->hne", weights, value_rows.astype(jnp.float32), precision=PRECISE
    )
    return (maxima, totals, weighted)


def combine(state_one, state_two):
    joint_max = jnp.maximum(state_one[0], state_two[0])
    scale_one = jnp.exp(state_one[0] - joint_max)
    scale_two = jnp.exp(state_two[0] - joint_max)
    return (
        joint_max,
        state_one[1] * scale_one + state_two[1] * scale_two,
        state_one[2] * scale_one[..., None] + state_two[2] * scale_two[..., None],
    )


def finish(partial_state):
    result = partial_state[2] / partial_state[1][..., None]
    return jnp.transpose(result, (1, 0, 2)).reshape(result.shape[1], -1).astype(jnp.bfloat16)


def normalize(row_values):
    centered = row_values - jnp.mean(row_values, axis=-1, keepdims=True)
    return centered * lax.rsqrt(
        jnp.mean(centered * centered, axis=-1, keepdims=True) + NORM_EPSILON
    )


def cross_partial(query_rows, key_rows, value_rows):
    scores = jnp.einsum(
        "unhe,uphe->unhp", query_rows, key_rows, preferred_element_type=jnp.float32
    ) * HD ** (-0.5)
    maxima = jnp.max(scores, axis=-1)
    weights = jnp.exp(scores - maxima[..., None])
    totals = jnp.sum(weights, axis=-1)
    weighted = jnp.einsum(
        "unhp,uphe->unhe", weights, value_rows.astype(jnp.float32), precision=PRECISE
    )
    return (weighted, maxima, totals)


def head_sums(partial_rows):
    return lax.psum(partial_rows.astype(jnp.bfloat16), "tp").astype(jnp.float32)


def long_output(own_rows):
    return lax.all_gather(own_rows, "seq", axis=0, tiled=True)


def local(
    x_short,
    x_long,
    parents,
    long_parents,
    short_len,
    long_len,
    doc_ids,
    long_doc,
    short_kv,
    long_kv,
    enc_kv,
    w_qkv,
    w_out,
    w_cross_q,
    w_cross_out,
    w_up,
    w_down,
):
    req_local, drafts, model_width = x_short.shape
    local_width = w_qkv.shape[2]
    local_heads = local_width // HD
    seq_count = lax.axis_size("seq")
    seq_index = lax.axis_index("seq")
    row_share = drafts // seq_count
    inputs = jnp.concatenate([x_short, x_long], 0)
    flat_rows = inputs.reshape(-1, model_width)
    projected = [
        jnp.dot(flat_rows, w_qkv[member], preferred_element_type=jnp.float32)
        .astype(jnp.bfloat16)
        .reshape(req_local + 1, drafts, local_heads, HD)
        for member in range(3)
    ]
    queries, key_rows, value_rows = projected
    short_tree = ancestry(parents)
    long_tree = ancestry(long_parents)[0]

    def short_attend(query_rows, draft_keys, draft_values, cache_kv, length, tree_mask):
        cache_span = cache_kv.shape[1]
        cache_keys = cache_kv[0].reshape(cache_span, local_heads, HD)
        cache_values = cache_kv[1].reshape(cache_span, local_heads, HD)
        valid_keys = jnp.arange(cache_span, dtype=jnp.int32) < length
        cache_part = partial_softmax(
            query_rows, cache_keys, cache_values, valid_keys[None, None, :]
        )
        draft_part = partial_softmax(query_rows, draft_keys, draft_values, tree_mask[None])
        return finish(combine(cache_part, draft_part))

    short_out = jax.vmap(short_attend)(
        queries[:req_local],
        key_rows[:req_local],
        value_rows[:req_local],
        short_kv,
        short_len,
        short_tree,
    )
    long_query = queries[req_local]
    long_key = key_rows[req_local]
    long_value = value_rows[req_local]
    length = long_len[0]
    first_row = seq_index * row_share
    query_share = lax.dynamic_slice_in_dim(long_query, first_row, row_share, 0)
    tree_share = lax.dynamic_slice_in_dim(long_tree, first_row, row_share, 0)
    initial = (
        jnp.full((local_heads, row_share), MASKED_SCORE, jnp.float32),
        jnp.zeros((local_heads, row_share), jnp.float32),
        jnp.zeros((local_heads, row_share, HD), jnp.float32),
    )
    block_piece = lax.all_gather(long_kv, "seq", axis=2, tiled=True)
    piece_rows = block_piece.shape[2]

    def update(kept_state):
        block_keys = block_piece[0, 0].reshape(piece_rows, local_heads, HD)
        block_values = block_piece[0, 1].reshape(piece_rows, local_heads, HD)
        valid_keys = jnp.arange(piece_rows, dtype=jnp.int32) < length
        return combine(
            kept_state,
            partial_softmax(query_share, block_keys, block_values, valid_keys[None, None, :]),
        )

    def keep_state(kept_state):
        return kept_state

    cache_state = lax.cond(jnp.int32(0) < length, update, keep_state, initial)
    long_rows = finish(
        combine(cache_state, partial_softmax(query_share, long_key, long_value, tree_share[None]))
    )
    long_input = lax.dynamic_slice_in_dim(x_long[0], first_row, row_share, 0)
    short_rows = req_local * drafts
    attn_rows = jnp.concatenate([short_out.reshape(short_rows, local_width), long_rows], 0)
    residual = jnp.concatenate([x_short.reshape(short_rows, model_width), long_input], 0).astype(
        jnp.float32
    )
    attn_sum = head_sums(jnp.dot(attn_rows, w_out, preferred_element_type=jnp.float32))
    hidden_one = normalize(residual + attn_sum).astype(jnp.bfloat16)
    cross_queries = jnp.dot(hidden_one, w_cross_q, preferred_element_type=jnp.float32).astype(
        jnp.bfloat16
    )
    row_count = cross_queries.shape[0]
    gathered = lax.all_gather(cross_queries, ("req", "seq"), axis=0, tiled=True)
    device_count = gathered.shape[0] // row_count
    block_devices = 1
    while (
        block_devices * 2 <= device_count
        and device_count % (block_devices * 2) == 0
        and (block_devices * 2 * row_count <= 1024)
    ):
        block_devices = block_devices * 2
    block_count = device_count // block_devices
    all_queries = gathered.reshape(block_count, block_devices, row_count, local_heads, HD)
    short_queries = all_queries[:, :, :short_rows].reshape(
        block_count, block_devices * req_local, drafts, local_heads, HD
    )
    long_queries = all_queries[:, :, short_rows:]
    short_docs = doc_ids.reshape(block_count, block_devices * req_local)
    long_docs = long_doc[jnp.arange(device_count, dtype=jnp.int32) // seq_count].reshape(
        block_count, block_devices
    )
    enc_keys = enc_kv[0].reshape(enc_kv.shape[1], enc_kv.shape[2], local_heads, HD)
    enc_values = enc_kv[1].reshape(enc_kv.shape[1], enc_kv.shape[2], local_heads, HD)

    def cross_block(block_inputs):
        query_short, query_long, doc_short, doc_long = block_inputs
        part_short = cross_partial(query_short, enc_keys[doc_short], enc_values[doc_short])
        part_long = cross_partial(query_long, enc_keys[doc_long], enc_values[doc_long])
        return tuple(
            (
                jnp.concatenate(
                    [
                        short_piece.reshape((block_devices, short_rows) + short_piece.shape[2:]),
                        long_piece,
                    ],
                    1,
                )
                for short_piece, long_piece in zip(part_short, part_long)
            )
        )

    block_parts = lax.map(cross_block, (short_queries, long_queries, short_docs, long_docs))
    sent_weighted, sent_maxima, sent_totals = tuple(
        (member.reshape((device_count,) + member.shape[2:]) for member in block_parts)
    )
    got_weighted, got_maxima, got_totals = (
        lax.all_to_all(
            sent_weighted.astype(jnp.bfloat16),
            ("req", "seq"),
            split_axis=0,
            concat_axis=0,
            tiled=True,
        ).astype(sent_weighted.dtype),
        lax.all_to_all(
            sent_maxima.astype(jnp.bfloat16),
            ("req", "seq"),
            split_axis=0,
            concat_axis=0,
            tiled=True,
        ).astype(sent_maxima.dtype),
        lax.all_to_all(
            sent_totals.astype(jnp.bfloat16),
            ("req", "seq"),
            split_axis=0,
            concat_axis=0,
            tiled=True,
        ).astype(sent_totals.dtype),
    )
    joint_max = jnp.max(got_maxima, axis=0)
    factor = jnp.exp(got_maxima - joint_max)
    cross_total = jnp.sum(got_totals * factor, axis=0)
    cross_accum = jnp.sum(got_weighted * factor[..., None], axis=0)
    cross_rows = (
        (cross_accum / cross_total[..., None]).reshape(row_count, local_width).astype(jnp.bfloat16)
    )
    cross_sum = head_sums(jnp.dot(cross_rows, w_cross_out, preferred_element_type=jnp.float32))
    hidden_two = normalize(hidden_one.astype(jnp.float32) + cross_sum).astype(jnp.bfloat16)
    upward = jnp.dot(hidden_two, w_up, preferred_element_type=jnp.float32)
    activated = jax.nn.gelu(upward, approximate=False).astype(jnp.bfloat16)
    downward = head_sums(jnp.dot(activated, w_down, preferred_element_type=jnp.float32))
    final_rows = normalize(hidden_two.astype(jnp.float32) + downward).astype(jnp.bfloat16)
    y_short = final_rows[:short_rows].reshape(req_local, drafts, model_width)
    y_long = long_output(final_rows[short_rows:])
    return (y_short, y_long.reshape(1, drafts, model_width))


def solution(mesh):
    in_specs = (
        P(("req", "seq"), None, None),
        P("req", None, None),
        P(("req", "seq"), None),
        P("req", None),
        P(("req", "seq")),
        P("req"),
        P(),
        P(),
        P(("req", "seq"), None, None, "tp"),
        P("req", None, "seq", "tp"),
        P(None, None, ("req", "seq"), "tp"),
        P(None, None, "tp"),
        P("tp", None),
        P(None, "tp"),
        P("tp", None),
        P(None, "tp"),
        P("tp", None),
    )
    out_specs = (P(("req", "seq"), None, None), P("req", None, None))
    return jax.shard_map(local, mesh=mesh, in_specs=in_specs, out_specs=out_specs, check_vma=False)
```

profile of v0, /device:TPU:0, one launch (start us, length us, event | category | flops | bytes accessed | tf_op | source)
XLA Modules:
  0.0 357.2 jit_solution(7681512146877946131)
XLA Ops:
  16.5 2.7 fusion.181
  27.3 31.3 %all-gather.3.cloned.1.call-done = bf16[1,2,1024,512]{2,3,1,0:T(8,128)(2,1)} async-done(((bf16[1,2,256,512]{2,3,1,0:T(8,128)(2,1)}), bf16[1,2,1024,512]{2,3,1,0:T(8,128)(2,1)}) %all-gather.3.cloned.1.call-update) | async-done | bytes 2097168 | tf_op jit(solution)/shard_map/all_gather | solution.py:152
  58.6 5.2 %conditional.1 = (f32[8,8]{1,0:T(8,128)}, f32[8,8]{1,0:T(8,128)S(1)}, f32[8,8,64]{2,1,0:T(8,128)S(1)}) conditional(s32[]{:T(128)} %convert_element_type.161, () %tuple.20, (s32[]{:T(128)}, bf16[1,2,1024,512]{2,3,1,0:T(8,128)(2,1)}, bf16[8,8,64]{2,0,1:T(8,128)(2,1)S(1)}) %tuple.21), branch_computations={%region_4.5_spmd, %region_5.8_spmd} | conditional | flops 59254144 | bytes 7110172 | solution.py:167
  66.9 19.1 %all-reduce.4.cloned.1.call-done = bf16[72,1024]{1,0:T(8,128)(2,1)} async-done(((bf16[72,1024]{1,0:T(8,128)(2,1)}), bf16[72,1024]{1,0:T(8,128)(2,1)}) %all-reduce.4.cloned.1.call-update) | async-done | bytes 147472 | tf_op jit(solution)/shard_map/psum | solution.py:77
  90.2 4.0 %fusion.180 = (bf16[1,32,64,512]{3,2,1,0:T(8,128)(2,1)S(1)}, bf16[1,32,64,512]{3,2,1,0:T(8,128)(2,1)}) fusion(bf16[2,32,64,512]{3,2,1,0:T(8,128)(2,1)} %param.31), kind=kLoop, calls=%fused_computation.278 | loop fusion | bytes 8388608 | tf_op jit(solution)/shard_map/slice | solution.py:202
  94.2 6.2 %reshape_squeeze.6 = bf16[32,64,8,64]{3,2,1,0:T(8,128)(2,1)} reshape(bf16[1,32,64,512]{3,2,1,0:T(8,128)(2,1)} %get-tuple-element.155) | data formatting | bytes 4194304 | tf_op jit(solution)/shard_map/reshape;squeeze | solution.py:203
  100.4 3.6 %reshape_squeeze.7 = bf16[32,64,8,64]{3,2,1,0:T(8,128)(2,1)} reshape(bf16[1,32,64,512]{3,2,1,0:T(8,128)(2,1)S(1)} %get-tuple-element.154) | data formatting | bytes 4194304 | tf_op jit(solution)/shard_map/reshape;squeeze | solution.py:202
  104.8 23.9 %all-gather.5.cloned.1.call-done = bf16[1152,512]{1,0:T(8,128)(2,1)} async-done(((bf16[72,512]{1,0:T(8,128)(2,1)}), bf16[1152,512]{1,0:T(8,128)(2,1)}) %all-gather.5.cloned.1.call-update) | async-done | bytes 1179664 | tf_op jit(solution)/shard_map/all_gather | solution.py:183
  128.7 2.4 copy.149
  131.1 5.0 %reshape.466 = bf16[2,8,72,8,64]{2,1,0,4,3:T(8,128)(2,1)S(1)} reshape(bf16[1152,512]{0,1:T(8,128)(2,1)} %copy.149) | data formatting | bytes 2359296 | tf_op jit(solution)/shard_map/reshape | solution.py:193
  138.1 3.2 copy.152
  141.3 3.1 copy.150
  144.4 59.8 %while.14 = (s32[]{:T(128)}, bf16[2,8,72,8,64]{4,3,2,1,0:T(8,128)(2,1)}, bf16[2,8,72,8]{2,3,1,0:T(8,128)(2,1)}, bf16[2,8,72,8]{2,3,1,0:T(8,128)(2,1)}, s32[2,16]...) while((s32[]{:T(128)}, ...), condition=%wide.region_18.19_spmd, body=%wide.region_13.18_spmd.sunk | while | flops 267449408 | bytes 31043756 | solution.py:222
  144.7 5.1 %gather_fusion.2 = bf16[16,64,8,64]{3,2,1,0:T(8,128)(2,1)} fusion(bf16[32,64,8,64]{3,2,1,0:T(8,128)(2,1)} %get-tuple-element.273, s32[1024]{0:T(1024)S(1)} %pad_clamp_fusion.6), kind=kCustom, calls=%fused_computation.1.clone.1 | custom fusion | bytes 2097216 | tf_op jit(solution)/shard_map/while/body/eval_jaxpr/gather | solution.py:207
  154.1 2.9 gather_fusion.1
  159.9 4.3 %gather_fusion.3 = bf16[16,64,8,64]{3,2,1,0:T(8,128)(2,1)} fusion(bf16[32,64,8,64]{3,2,1,0:T(8,128)(2,1)} %get-tuple-element.272, s32[1024]{0:T(1024)S(1)} %pad_clamp_fusion.6), kind=kCustom, calls=%fused_computation.clone.1 | custom fusion | bytes 2097216 | tf_op jit(solution)/shard_map/while/body/eval_jaxpr/gather | solution.py:207
  164.2 3.7 %fusion.238 = bf16[16,32,8,64]{3,1,2,0:T(8,128)(2,1)S(1)} fusion(f32[16,8,64,32]{2,3,1,0:T(8,128)S(1)} %get-tuple-element.235, bf16[16,64,8,64]{3,2,1,0:T(8,128)(2,1)} %gather_fusion.3, f32[16,32,8]{1,2,0:T(8,128)S(1)} %get-tuple-element.236), kind=kOutput, calls=%fused_computation.30.clone.1 | convolution fusion | flops 201850880 | bytes 2637824 | tf_op jit(solution)/shard_map/while/body/eval_jaxpr/unhp,uphe->unhe/dot_general | solution.py:70
  168.4 2.9 gather_fusion
  174.4 5.1 %gather_fusion.2 = bf16[16,64,8,64]{3,2,1,0:T(8,128)(2,1)} fusion(bf16[32,64,8,64]{3,2,1,0:T(8,128)(2,1)} %get-tuple-element.273, s32[1024]{0:T(1024)S(1)} %pad_clamp_fusion.6), kind=kCustom, calls=%fused_computation.1.clone.1 | custom fusion | bytes 2097216 | tf_op jit(solution)/shard_map/while/body/eval_jaxpr/gather | solution.py:207
  183.9 2.9 gather_fusion.1
  189.7 4.3 %gather_fusion.3 = bf16[16,64,8,64]{3,2,1,0:T(8,128)(2,1)} fusion(bf16[32,64,8,64]{3,2,1,0:T(8,128)(2,1)} %get-tuple-element.272, s32[1024]{0:T(1024)S(1)} %pad_clamp_fusion.6), kind=kCustom, calls=%fused_computation.clone.1 | custom fusion | bytes 2097216 | tf_op jit(solution)/shard_map/while/body/eval_jaxpr/gather | solution.py:207
  194.0 3.7 %fusion.238 = bf16[16,32,8,64]{3,1,2,0:T(8,128)(2,1)S(1)} fusion(f32[16,8,64,32]{2,3,1,0:T(8,128)S(1)} %get-tuple-element.235, bf16[16,64,8,64]{3,2,1,0:T(8,128)(2,1)} %gather_fusion.3, f32[16,32,8]{1,2,0:T(8,128)S(1)} %get-tuple-element.236), kind=kOutput, calls=%fused_computation.30.clone.1 | convolution fusion | flops 201850880 | bytes 2637824 | tf_op jit(solution)/shard_map/while/body/eval_jaxpr/unhp,uphe->unhe/dot_general | solution.py:70
  198.2 2.9 gather_fusion
  204.2 10.2 %all_to_all.15 = bf16[16,72,8]{1,2,0:T(8,128)(2,1)S(1)} all-to-all(bf16[16,72,8]{1,2,0:T(8,128)(2,1)} %bitcast.209), channel_id=1, replica_groups=mesh['req'=4,'seq'=4,'tp'=2] {'req','seq'}, dimensions={0} | all-to-all | bytes 36864 | tf_op jit(solution)/shard_map/all_to_all | solution.py:234
  214.3 3.4 all-to-all-start.2
  217.8 4.4 %copy.153 = bf16[2,8,72,8,64]{2,4,3,1,0:T(8,128)(2,1)} copy(bf16[2,8,72,8,64]{4,3,2,1,0:T(8,128)(2,1)} %get-tuple-element.71) | data formatting | bytes 2359296 | tf_op jit(solution)/shard_map/convert_element_type | solution.py:228
  224.2 3.9 %all-to-all-start = ((bf16[16,72,8,64]{1,3,2,0:T(8,128)(2,1)}), bf16[16,72,8,64]{1,3,2,0:T(8,128)(2,1)S(1)}, u32[]{:S(2)}, u32[]{:S(2)}) async-start(bf16[16,72,8,64]{1,3,2,0:T(8,128)(2,1)} %bitcast.36), calls=%async_computation | async-start | bytes 4194304 | tf_op jit(solution)/shard_map/all_to_all | solution.py:227
  228.2 49.3 %all-to-all-done = bf16[16,72,8,64]{1,3,2,0:T(8,128)(2,1)S(1)} async-done(((bf16[16,72,8,64]{1,3,2,0:T(8,128)(2,1)}), bf16[16,72,8,64]{1,3,2,0:T(8,128)(2,1)S(1)}, u32[]{:S(2)}, u32[]{:S(2)}) %all-to-all-start) | async-done | bytes 1179680 | tf_op jit(solution)/shard_map/all_to_all | solution.py:227
  280.7 20.1 %all-reduce.6.cloned.1.call-done = bf16[72,1024]{1,0:T(8,128)(2,1)} async-done(((bf16[72,1024]{1,0:T(8,128)(2,1)}), bf16[72,1024]{1,0:T(8,128)(2,1)}) %all-reduce.6.cloned.1.call-update) | async-done | bytes 147472 | tf_op jit(solution)/shard_map/psum | solution.py:77
  304.1 7.0 %convolution_convert_fusion = bf16[72,1024]{1,0:T(8,128)(2,1)} fusion(bf16[2048,1024]{1,0:T(8,128)(2,1)} %param.37, bf16[72,1024]{1,0:T(8,128)(2,1)S(1)} %multiply_convert_fusion.1, bf16[1024,2048]{1,0:T(8,128)(2,1)} %param.36), kind=kOutput, calls=%fused_computation.72 | convolution fusion | flops 613638144 | bytes 8683520 | tf_op jit(solution)/shard_map/dot_general | solution.py:260
  311.1 21.8 %all-reduce.8.cloned.1.call-done = bf16[72,1024]{1,0:T(8,128)(2,1)} async-done(((bf16[72,1024]{1,0:T(8,128)(2,1)}), bf16[72,1024]{1,0:T(8,128)(2,1)}) %all-reduce.8.cloned.1.call-update) | async-done | bytes 147472 | tf_op jit(solution)/shard_map/psum | solution.py:77
  336.8 13.2 %all_gather.11 = bf16[32,1024]{1,0:T(8,128)(2,1)S(1)} all-gather(bf16[8,1024]{1,0:T(8,128)(2,1)S(1)} %slice.108), channel_id=1, replica_groups=mesh['req'=4,'seq'=4,'tp'=2] {'seq'}, dimensions={0}, use_global_device_ids=true | all-gather | bytes 81920 | tf_op jit(solution)/shard_map/all_gather | solution.py:81
  (200 shorter events, 65.8 us)
Async XLA Ops:
  7.2 57.8 %copy-start = (bf16[512,1024]{1,0:T(8,128)(2,1)S(1)}, bf16[512,1024]{1,0:T(8,128)(2,1)}, u32[]{:S(2)}) copy-start(bf16[512,1024]{1,0:T(8,128)(2,1)} %param.33) | copy-start | bytes 3145732
  7.2 51.4 %all-gather.3.cloned.1.call-start = ((), (), s32[]{:S(2)}) async-start(), calls=%async_computation.3 | async-start | bytes 2621440 | tf_op jit(solution)/shard_map/all_gather | solution.py:152
  9.4 76.6 %all-reduce.4.cloned.1.call-start = ((), (), s32[]{:S(2)}) async-start(), calls=%async_computation.4 | async-start | bytes 294912 | tf_op jit(solution)/shard_map/psum | solution.py:77
  11.9 7.7 %copy-start.14 = (bf16[96,512]{1,0:T(8,128)(2,1)}, bf16[96,512]{1,0:T(8,128)(2,1)S(1)}, u32[]{:S(2)}) copy-start(bf16[96,512]{1,0:T(8,128)(2,1)S(1)} %convolution_convert_fusion.5) | copy-start | bytes 294916
  11.9 3.5 copy-start.18
  11.9 4.5 %copy-start.16 = (s32[2]{0:T(128)S(1)}, s32[2]{0:T(128)}, u32[]{:S(2)}) copy-start(s32[2]{0:T(128)} %param.25) | copy-start | bytes 28
  13.5 6.1 %copy-start.15 = (bf16[96,512]{1,0:T(8,128)(2,1)}, bf16[96,512]{1,0:T(8,128)(2,1)S(1)}, u32[]{:S(2)}) copy-start(bf16[96,512]{1,0:T(8,128)(2,1)S(1)} %convolution_convert_fusion.4) | copy-start | bytes 294916
  15.1 4.5 %copy-start.11 = (bf16[96,512]{1,0:T(8,128)(2,1)}, bf16[96,512]{1,0:T(8,128)(2,1)S(1)}, u32[]{:S(2)}) copy-start(bf16[96,512]{1,0:T(8,128)(2,1)S(1)} %convolution_convert_fusion.3) | copy-start | bytes 294916
  20.2 2.1 slice-start
  23.1 1.8 slice-start.2
  23.1 1.9 slice-start.3
  23.1 2.7 slice-start.1
  23.1 2.8 copy-start.17
  58.5 27.4 %copy-start.9 = (bf16[2,32,1024]{2,1,0:T(8,128)(2,1)S(1)}, bf16[2,32,1024]{2,1,0:T(8,128)(2,1)}, u32[]{:S(2)}) copy-start(bf16[2,32,1024]{2,1,0:T(8,128)(2,1)} %param.21) | copy-start | bytes 393220
  63.7 25.5 %copy-start.10 = (bf16[1024,512]{1,0:T(8,128)(2,1)S(1)}, bf16[1024,512]{1,0:T(8,128)(2,1)}, u32[]{:S(2)}) copy-start(bf16[1024,512]{1,0:T(8,128)(2,1)} %param.34) | copy-start | bytes 3145732
  65.9 62.8 %all-gather.5.cloned.1.call-start = ((), (), s32[]{:S(2)}) async-start(), calls=%async_computation.5 | async-start | bytes 1253376 | tf_op jit(solution)/shard_map/all_gather | solution.py:183
  89.2 5.0 %copy-start.7 = (bf16[72,1024]{1,0:T(8,128)(2,1)}, bf16[72,1024]{1,0:T(8,128)(2,1)S(1)}, u32[]{:S(2)}) copy-start(bf16[72,1024]{1,0:T(8,128)(2,1)S(1)} %multiply_convert_fusion.2) | copy-start | bytes 442372
  100.4 3.6 %copy-start.2 = (s32[4]{0:T(128)S(1)}, s32[4]{0:T(128)}, u32[]{:S(2)}) copy-start(s32[4]{0:T(128)} %param.28) | copy-start | bytes 52
  100.4 4.4 %copy-start.19 = (s32[32]{0:T(128)S(1)}, s32[32]{0:T(128)}, u32[]{:S(2)}) copy-start(s32[32]{0:T(128)} %param.27) | copy-start | bytes 388
  136.1 5.2 %copy-start.6 = (bf16[2,8,72,8,64]{2,1,0,4,3:T(8,128)(2,1)}, bf16[2,8,72,8,64]{2,1,0,4,3:T(8,128)(2,1)S(1)}, u32[]{:S(2)}) copy-start(bf16[2,8,72,8,64]{2,1,0,4,3:T(8,128)(2,1)S(1)} %reshape.466) | copy-start | bytes 3538948
  144.6 5.1 %copy-start.4 = (bf16[2,16,32,8,64]{4,3,2,1,0:T(8,128)(2,1)}, bf16[2,16,32,8,64]{4,3,2,1,0:T(8,128)(2,1)S(1)}, u32[]{:S(2)}) copy-start(bf16[2,16,32,8,64]{4,3,2,1,0:T(8,128)(2,1)S(1)} %get-tuple-element.274) | copy-start | bytes 3145732 | tf_op jit(solution)/shard_map/while
  149.7 1.6 copy-start.3
  172.4 2.0 copy-start.5
  174.4 5.1 %copy-start.4 = (bf16[2,16,32,8,64]{4,3,2,1,0:T(8,128)(2,1)}, bf16[2,16,32,8,64]{4,3,2,1,0:T(8,128)(2,1)S(1)}, u32[]{:S(2)}) copy-start(bf16[2,16,32,8,64]{4,3,2,1,0:T(8,128)(2,1)S(1)} %get-tuple-element.274) | copy-start | bytes 3145732 | tf_op jit(solution)/shard_map/while
  179.5 1.6 copy-start.3
  202.1 2.0 copy-start.5
  214.3 9.9 %all-to-all-start.2 = ((bf16[16,72,8]{1,2,0:T(8,128)(2,1)}), bf16[16,72,8]{1,2,0:T(8,128)(2,1)S(1)}, u32[]{:S(2)}, u32[]{:S(2)}) async-start(bf16[16,72,8]{1,2,0:T(8,128)(2,1)} %bitcast.210), calls=%async_computation.2 | async-start | bytes 65536 | tf_op jit(solution)/shard_map/all_to_all | solution.py:241
  224.2 53.4 %all-to-all-start = ((bf16[16,72,8,64]{1,3,2,0:T(8,128)(2,1)}), bf16[16,72,8,64]{1,3,2,0:T(8,128)(2,1)S(1)}, u32[]{:S(2)}, u32[]{:S(2)}) async-start(bf16[16,72,8,64]{1,3,2,0:T(8,128)(2,1)} %bitcast.36), calls=%async_computation | async-start | bytes 4194304 | tf_op jit(solution)/shard_map/all_to_all | solution.py:227
  228.1 72.7 %all-reduce.6.cloned.1.call-start = ((), (), s32[]{:S(2)}) async-start(), calls=%async_computation.6 | async-start | bytes 294912 | tf_op jit(solution)/shard_map/psum | solution.py:77
  277.6 23.3 %copy-start.8 = (bf16[72,1024]{1,0:T(8,128)(2,1)S(1)}, bf16[72,1024]{1,0:T(8,128)(2,1)}, u32[]{:S(2)}) copy-start(bf16[72,1024]{1,0:T(8,128)(2,1)} %copy-done.7) | copy-start | bytes 442372
  280.4 52.5 %all-reduce.8.cloned.1.call-start = ((), (), s32[]{:S(2)}) async-start(), calls=%async_computation.7 | async-start | bytes 294912 | tf_op jit(solution)/shard_map/psum | solution.py:77
  304.1 46.6 %copy-start.1 = (bf16[512,1024]{1,0:T(8,128)(2,1)S(1)}, bf16[512,1024]{1,0:T(8,128)(2,1)}, u32[]{:S(2)}) copy-start(bf16[512,1024]{1,0:T(8,128)(2,1)} %param.33) | copy-start | bytes 3145732
  (2 other events, 2.2 us)
Sparse Core Ops, SparseCore 0:
  9.6 48.9 all-gather.2
  66.0 19.9 all-reduce.3
  90.3 38.3 all-gather.4
  280.5 20.2 all-reduce.5
  311.2 21.6 all-reduce.7
where the time goes:
time: 359 us; the launch traced here: 357 us
  waiting for transfers between devices  168 us (47%)
  local copies, waits for them, and re-layouts  84.7 us (24%)
  matrix products  36.5 us (10%)
  blocking collectives  23.4 us (7%)
  other arithmetic  21.3 us (6%)
  between operations  15.1 us (4%)
  starting transfers between devices  8 us (2%)
    psum x3, waiting for transfers between devices, head_sums(): return lax.psum(partial_rows.astype(jnp.bfloat16), 'tp').astype(jnp.float32)  61.1 us
    all_to_all x1, waiting for transfers between devices, local(): lax.all_to_all(sent_weighted.astype(jnp.bfloat16), ('req', 'seq'), split_...  49.3 us
    all_gather x1, waiting for transfers between devices, local(): block_piece = lax.all_gather(long_kv, 'seq', axis=2, tiled=True)  31.3 us
    all_gather x1, waiting for transfers between devices, local(): gathered = lax.all_gather(cross_queries, ('req', 'seq'), axis=0, tiled=True)  23.9 us
    all_gather x1, blocking collectives, long_output(): return lax.all_gather(own_rows, 'seq', axis=0, tiled=True)  13.2 us
    gather x2, local copies, waits for them, and re-layouts, cross_block(): enc_keys[doc_short]  10.2 us
    all_to_all x1, blocking collectives, local(): lax.all_to_all(sent_maxima.astype(jnp.bfloat16), ('req', 'seq'), split_ax...  10.2 us
    dot_general x4, matrix products, cross_partial(): jnp.einsum('unhp,uphe->unhe', weights, value_rows.astype(jnp.float32), pr...  9.46 us
  transfers between devices with their start and end apart: 7, of which 7 were waited for; matrix products, arithmetic and copies ran while one was open for 10% of the time, Pallas kernels for 0%

commit v1 on v0

v1 whole, which is shorter than its diff:
```python
import functools

import jax
import jax.numpy as jnp
from jax import lax
from jax.experimental import pallas as pl
from jax.experimental.pallas import tpu as pltpu
from jax.sharding import PartitionSpec as P

HD = 64
LANES = 128
CORES = 2
PIECES = 3
MASKED = -1e30
EPS = 1e-05
F32 = jnp.float32
BF16 = jnp.bfloat16
VMEM = pl.BlockSpec(memory_space=pltpu.VMEM)
SMEM = pl.BlockSpec(memory_space=pltpu.SMEM)
ANY = pl.BlockSpec(memory_space=pl.ANY)


def iota(shape, axis):
    return lax.broadcasted_iota(jnp.int32, shape, axis)


def dot(a, b):
    return lax.dot_general(a, b, (((1,), (0,)), ((), ())), preferred_element_type=F32)


def dot_t(a, b):
    return lax.dot_general(a, b, (((1,), (1,)), ((), ())), preferred_element_type=F32)


def normalize(v):
    centered = v - jnp.mean(v, axis=-1, keepdims=True)
    return centered * lax.rsqrt(jnp.mean(centered * centered, axis=-1, keepdims=True) + EPS)


def head_mask(heads, rows, width):
    shape = (heads * rows, width)
    return (iota(shape, 0) // rows == iota(shape, 1) // HD).astype(F32)


def spread_heads(q, heads, mask):
    return jnp.concatenate([q] * heads, axis=0) * mask.astype(BF16)


def weigh(p, v):
    high = p.astype(BF16)
    return dot(high, v)


def fold_heads(o, heads):
    return jnp.sum(o.reshape(heads, o.shape[0] // heads, o.shape[1]), axis=0)


def pieces_of(x):
    high = x.astype(BF16)
    rest = x - high.astype(F32)
    mid = rest.astype(BF16)
    low = (rest - mid.astype(F32)).astype(BF16)
    return high, mid, low


def stat_block(lse, heads, rows):
    shape = (heads * rows, LANES)
    lane = iota(shape, 1)
    high, mid, low = (m.astype(F32) for m in pieces_of(lse))
    value = jnp.where(lane < heads, high, jnp.where(lane < 2 * heads, mid, low))
    keep = jnp.logical_and(lane % heads == iota(shape, 0) // rows, lane < PIECES * heads)
    return fold_heads(jnp.where(keep, value, 0.0), heads).astype(BF16)


def expand_stats(stats, heads):
    width = heads * HD
    lane = iota((LANES, width), 0)
    hot = jnp.logical_and(lane % heads == iota((LANES, width), 1) // HD, lane < PIECES * heads)
    return dot(stats, hot.astype(F32).astype(BF16))


def partial_payload(qs, k, v, allowed, mask, heads, rows):
    s = dot_t(qs, k) * HD ** (-0.5)
    if allowed is not None:
        s = jnp.where(allowed, s, MASKED)
    m = jnp.max(s, axis=-1, keepdims=True)
    p = jnp.exp(s - m)
    if allowed is not None:
        p = jnp.where(allowed, p, 0.0)
    l = jnp.maximum(jnp.sum(p, axis=-1, keepdims=True), 1e-30)
    o = fold_heads(weigh(p, v) * (mask / l), heads)
    return o.astype(BF16), stat_block(m + jnp.log(l), heads, rows)


def qkv_kernel(len_ref, xs_ref, xl_ref, w_ref, kv_ref, qkv_ref, pay_ref):
    short_rows = xs_ref.shape[0] * xs_ref.shape[1]
    rows, model = xl_ref.shape[1:]
    width = w_ref.shape[2]
    heads = width // HD
    x = jnp.concatenate([xs_ref[...].reshape(short_rows, model), xl_ref[0]], axis=0)
    for member in range(3):
        qkv_ref[member] = dot(x, w_ref[member]).astype(BF16)
    mask = head_mask(heads, rows, width)
    qs = spread_heads(qkv_ref[0, short_rows:, :], heads, mask)
    span = kv_ref.shape[2]
    positions = iota((1, span), 1) + lax.axis_index("seq") * span
    o, stats = partial_payload(
        qs, kv_ref[0, 0], kv_ref[0, 1], positions < len_ref[0], mask, heads, rows
    )
    pay_ref[:, :width] = o
    pay_ref[:, width:] = stats


def attend_kernel(hops, len_ref, ps_ref, pl_ref, qkv_ref, skv_ref, wo_ref, *rest):
    pay_refs, (out_ref, attn, pays) = rest[: hops + 1], rest[hops + 1 :]
    requests, _, span, width = skv_ref.shape
    heads = width // HD
    rows = ps_ref.shape[1]
    zed = lax.axis_index("seq")
    seqs = hops + 1
    for hop in range(seqs):
        pays[lax.rem(zed - hop + seqs, seqs)] = pay_refs[hop][...]
    mask = head_mask(heads, rows, width)
    node_j = iota((rows, rows), 0)
    node_i = iota((rows, rows), 1)
    eye = (node_i == node_j).astype(F32)

    def tree(parents):
        hot = jnp.logical_and(parents == node_j, node_i > 0).astype(F32)
        closure = eye + hot
        reach = 1
        while reach < rows:
            b = closure.astype(BF16)
            closure = jnp.minimum(dot(b, b), 1.0)
            reach *= 2
        flat = lax.dot_general(
            closure.astype(BF16),
            eye.astype(BF16),
            (((0,), (0,)), ((), ())),
            preferred_element_type=F32,
        )
        return jnp.concatenate([flat] * heads, axis=0) > 0.5

    for j in range(requests):
        row = j * rows
        qs = spread_heads(qkv_ref[0, row : row + rows, :], heads, mask)
        allowed = iota((1, span), 1) < len_ref[j]
        s = jnp.where(allowed, dot_t(qs, skv_ref[j, 0]) * HD ** (-0.5), MASKED)
        allowed_d = tree(ps_ref[j : j + 1, :])
        d = jnp.where(
            allowed_d, dot_t(qs, qkv_ref[1, row : row + rows, :]) * HD ** (-0.5), MASKED
        )
        m = jnp.maximum(jnp.max(s, axis=-1, keepdims=True), jnp.max(d, axis=-1, keepdims=True))
        p = jnp.where(allowed, jnp.exp(s - m), 0.0)
        pd = jnp.where(allowed_d, jnp.exp(d - m), 0.0)
        l = jnp.sum(p, axis=-1, keepdims=True) + jnp.sum(pd, axis=-1, keepdims=True)
        o = weigh(p, skv_ref[j, 1]) + weigh(pd, qkv_ref[2, row : row + rows, :])
        attn[row : row + rows, :] = fold_heads(o * (mask / l), heads).astype(BF16)

    row = requests * rows
    qs = spread_heads(qkv_ref[0, row:, :], heads, mask)
    o, stats = partial_payload(
        qs, qkv_ref[1, row:, :], qkv_ref[2, row:, :], tree(pl_ref[...]), mask, heads, rows
    )
    values = [o.astype(F32)] + [pays[z, :, :width].astype(F32) for z in range(seqs)]
    scores = [expand_stats(stats, heads)] + [
        expand_stats(pays[z, :, width:], heads) for z in range(seqs)
    ]
    attn[row:, :] = merge(values, scores).astype(BF16)
    out_ref[...] = dot(attn[...], wo_ref[...]).astype(BF16)


def merge(values, scores):
    top = functools.reduce(jnp.maximum, scores)
    total = None
    for value, score in zip(values, scores):
        w = jnp.exp(score - top)
        total = w if total is None else total + w
        acc = w * value if total is w else acc + w * value
    return acc / total


def query_kernel(xs_ref, xl_ref, a_ref, b_ref, w_ref, h_ref, q_ref, qs_ref):
    short_rows = xs_ref.shape[0] * xs_ref.shape[1]
    x = jnp.concatenate([xs_ref[...].reshape(short_rows, -1), xl_ref[0]], axis=0).astype(F32)
    h = normalize(x + (a_ref[...].astype(F32) + b_ref[...].astype(F32))).astype(BF16)
    h_ref[...] = h
    q = dot(h, w_ref[...]).astype(BF16)
    q_ref[...] = q[short_rows:]
    qs_ref[...] = q[:short_rows]


def cross_kernel(
    seqs, requests, group_ref, doc_ref, long_ref, own_ref, other_ref, q_ref, pay_ref, kv, sems
):
    pay_rows = pay_ref.shape[1]
    width = q_ref.shape[1]
    heads = width // HD
    span = own_ref.shape[2]
    short_total = seqs * requests
    rows = q_ref.shape[0] // (short_total + 1)
    group = group_ref[0]
    zed = lax.axis_index("seq")

    def doc_of(e):
        place = lax.rem(zed - e // requests + seqs, seqs)
        at = (group * seqs + place) * requests + lax.rem(e, requests)
        return doc_ref[at]

    def copies(e, doc):
        return (
            pltpu.make_async_copy(own_ref.at[:, doc], kv.at[e, :, pl.ds(0, span)], sems.at[e, 0]),
            pltpu.make_async_copy(
                other_ref.at[:, doc], kv.at[e, :, pl.ds(span, span)], sems.at[e, 1]
            ),
        )

    def start(e, carry):
        for copy in copies(e, doc_of(e)):
            copy.start()
        return carry

    for copy in copies(short_total, long_ref[group]):
        copy.start()
    lax.fori_loop(0, short_total, start, 0)
    mask = head_mask(heads, rows, width)

    def one(e, doc):
        for copy in copies(e, doc):
            copy.wait()
        qs = spread_heads(q_ref[pl.ds(pl.multiple_of(e * rows, rows), rows), :], heads, mask)
        return partial_payload(qs, kv[e, 0], kv[e, 1], None, mask, heads, rows)

    o, stats = one(short_total, long_ref[group])
    for k in range(seqs):
        pay_ref[k, requests * rows :, :width] = o
        pay_ref[k, requests * rows :, width:] = stats
    for e in range(short_total):
        o, stats = one(e, doc_of(e))
        k, row = e // requests, (e % requests) * rows
        pay_ref[k, row : row + rows, :width] = o
        pay_ref[k, row : row + rows, width:] = stats


def merge_kernel(places, seqs, w_ref, *rest):
    ins, (out_ref, pays, cross) = rest[: len(places)], rest[len(places) :]
    rows, width = cross.shape
    heads = width // HD
    pairs = lax.axis_size("req") // CORES
    yed = lax.axis_index("req") // CORES
    zed = lax.axis_index("seq")
    for ref, (dy, dz) in zip(ins, places):
        at = lax.rem(yed - dy + pairs, pairs) * seqs + lax.rem(zed + dz, seqs)
        pays[at] = ref[...]
    step = 32
    for row in range(0, rows, step):
        part = slice(row, row + step)
        values = [pays[s, part, :width].astype(F32) for s in range(len(places))]
        scores = [expand_stats(pays[s, part, width:], heads) for s in range(len(places))]
        cross[part, :] = merge(values, scores).astype(BF16)
    out_ref[...] = dot(cross[...], w_ref[...]).astype(BF16)


def gelu(x):
    return 0.5 * x * (1.0 + lax.erf(x * 0.5**0.5))


def ffn_kernel(h_ref, a_ref, b_ref, up_ref, down_ref, h2_ref, out_ref, acc):
    step = pl.program_id(0)

    @pl.when(step == 0)
    def _():
        total = h_ref[...].astype(F32) + (a_ref[...].astype(F32) + b_ref[...].astype(F32))
        h2_ref[...] = normalize(total).astype(BF16)

    act = gelu(dot(h2_ref[...], up_ref[...])).astype(BF16)
    part = dot(act, down_ref[...])

    @pl.when(step == 0)
    def _():
        acc[...] = part

    @pl.when(step > 0)
    def _():
        acc[...] += part

    @pl.when(step == pl.num_programs(0) - 1)
    def _():
        out_ref[...] = acc[...].astype(BF16)


def final_kernel(h_ref, a_ref, b_ref, ys_ref, yl_ref):
    total = h_ref[...].astype(F32) + (a_ref[...].astype(F32) + b_ref[...].astype(F32))
    y = normalize(total).astype(BF16)
    short_rows = ys_ref.shape[0] * ys_ref.shape[1]
    ys_ref[...] = y[:short_rows].reshape(ys_ref.shape)
    yl_ref[0] = y[short_rows:]


def call(kernel, name, out, ins, scratch=(), flops=10**8, moved=10**6, **kw):
    many = isinstance(out, (tuple, list))
    return pl.pallas_call(
        kernel,
        out_shape=out,
        in_specs=ins,
        out_specs=[VMEM] * len(out) if many else VMEM,
        scratch_shapes=list(scratch),
        name=name,
        cost_estimate=pl.CostEstimate(flops=flops, bytes_accessed=moved, transcendentals=0),
        compiler_params=pltpu.CompilerParams(vmem_limit_bytes=48 << 20),
        **kw,
    )


def shape(dims, dtype=BF16):
    return jax.ShapeDtypeStruct(dims, dtype)


def local(
    x_short,
    x_long,
    parents,
    long_parents,
    short_len,
    long_len,
    doc_ids,
    long_doc,
    short_kv,
    long_kv,
    enc_kv,
    w_qkv,
    w_out,
    w_cross_q,
    w_cross_out,
    w_up,
    w_down,
):
    requests, rows, model = x_short.shape
    width = w_qkv.shape[2]
    heads = width // HD
    short_rows = requests * rows
    all_rows = short_rows + rows
    seqs = lax.axis_size("seq")
    reqs = lax.axis_size("req")
    tps = lax.axis_size("tp")
    pairs = reqs // CORES
    pay = width + LANES
    span = enc_kv.shape[2]
    both = ("req", "seq")

    def seq_shift(x, k):
        return lax.ppermute(x, "seq", [(i, (i + k) % seqs) for i in range(seqs)])

    def yz_shift(x, dy, dz):
        perm = []
        for y in range(pairs):
            for c in range(CORES):
                for z in range(seqs):
                    to = ((y + dy) % pairs * CORES + c) * seqs + (z + dz) % seqs
                    perm.append(((y * CORES + c) * seqs + z, to))
        return lax.ppermute(x, both, perm)

    def tp_swap(x):
        return lax.ppermute(x, "tp", [(i, (i + 1) % tps) for i in range(tps)])

    other_kv = lax.ppermute(enc_kv, "req", [(i, i ^ 1) for i in range(reqs)])

    qkv, long_pay = call(
        qkv_kernel,
        "qkv",
        (shape((3, all_rows, width)), shape((rows, pay))),
        [SMEM] + [VMEM] * 4,
    )(long_len, x_short, x_long, w_qkv, long_kv)
    got = [seq_shift(long_pay, k) for k in range(1, seqs)]
    partial = call(
        functools.partial(attend_kernel, seqs - 1),
        "attend",
        shape((all_rows, model)),
        [SMEM] + [VMEM] * (5 + seqs),
        [pltpu.VMEM((all_rows, width), BF16), pltpu.VMEM((seqs, rows, pay), BF16)],
    )(short_len, parents, long_parents, qkv, short_kv, w_out, long_pay, *got)

    hidden_one, q_long, q_short = call(
        query_kernel,
        "query",
        (shape((all_rows, model)), shape((rows, width)), shape((short_rows, width))),
        [VMEM] * 5,
    )(x_short, x_long, partial, tp_swap(partial), w_cross_q)

    own_q = jnp.concatenate([q_short] + [seq_shift(q_short, k) for k in range(1, seqs)] + [q_long])
    entries = seqs * requests + 1
    req = lax.axis_index("req").astype(jnp.int32)

    def cross(dy, q):
        y = (req // CORES - dy + pairs) % pairs
        group = (y * CORES + req % CORES).reshape(1)
        return call(
            functools.partial(cross_kernel, seqs, requests),
            "cross",
            shape((seqs, all_rows, pay)),
            [SMEM] * 3 + [ANY] * 2 + [VMEM],
            [
                pltpu.VMEM((entries, 2, CORES * span, width), BF16),
                pltpu.SemaphoreType.DMA((entries, 2)),
            ],
        )(group, doc_ids, long_doc, enc_kv, other_kv, q)

    pieces, places = [], []
    for dy in range(pairs):
        out = cross(dy, own_q if dy == 0 else yz_shift(own_q, dy, 0))
        for k in range(seqs):
            block = out[k]
            if (dy, k) != (0, 0):
                block = yz_shift(block, -dy, -k)
            pieces.append(block)
            places.append(((-dy) % pairs, k))
    partial = call(
        functools.partial(merge_kernel, tuple(places), seqs),
        "merge",
        shape((all_rows, model)),
        [VMEM] * (1 + len(pieces)),
        [pltpu.VMEM((len(pieces), all_rows, pay), BF16), pltpu.VMEM((all_rows, width), BF16)],
    )(w_cross_out, *pieces)

    hidden = w_up.shape[1]
    block = 512
    whole = pl.BlockSpec((all_rows, model), lambda i: (0, 0))
    hidden_two, partial = pl.pallas_call(
        ffn_kernel,
        grid=(hidden // block,),
        out_shape=(shape((all_rows, model)), shape((all_rows, model))),
        in_specs=[
            whole,
            whole,
            whole,
            pl.BlockSpec((model, block), lambda i: (0, i)),
            pl.BlockSpec((block, model), lambda i: (i, 0)),
        ],
        out_specs=(whole, whole),
        scratch_shapes=[pltpu.VMEM((all_rows, model), F32)],
        name="ffn",
        compiler_params=pltpu.CompilerParams(
            dimension_semantics=("arbitrary",), vmem_limit_bytes=48 << 20
        ),
    )(hidden_one, partial, tp_swap(partial), w_up, w_down)

    return call(
        final_kernel,
        "final",
        (shape((requests, rows, model)), shape((1, rows, model))),
        [VMEM] * 3,
    )(hidden_two, partial, tp_swap(partial))


def solution(mesh):
    in_specs = (
        P(("req", "seq"), None, None),
        P("req", None, None),
        P(("req", "seq"), None),
        P("req", None),
        P(("req", "seq")),
        P("req"),
        P(),
        P(),
        P(("req", "seq"), None, None, "tp"),
        P("req", None, "seq", "tp"),
        P(None, None, ("req", "seq"), "tp"),
        P(None, None, "tp"),
        P("tp", None),
        P(None, "tp"),
        P("tp", None),
        P(None, "tp"),
        P("tp", None),
    )
    out_specs = (P(("req", "seq"), None, None), P("req", None, None))
    return jax.shard_map(local, mesh=mesh, in_specs=in_specs, out_specs=out_specs, check_vma=False)
```

time: 359 us -> 98 us (0.27)
  waiting for transfers between devices: 168 us -> 32.7 us
  local copies, waits for them, and re-layouts: 84.7 us -> 8.99 us
  matrix products: 36.5 us -> 0 us
  Pallas kernels: 0 us -> 26.9 us
  blocking collectives: 23.4 us -> 0 us
  other arithmetic: 21.3 us -> 0 us
  starting transfers between devices: 8 us -> 27.6 us
  between operations: 15.1 us -> 1.44 us
    psum x3 -> x0, waiting for transfers between devices: 61.1 us -> none  [head_sums(): return lax.psum(partial_rows.astype(jnp.bfloat16), 'tp').astype(jnp.float32)]
    all_gather x2 -> x0, waiting for transfers between devices: 55.1 us -> none  [the longest x1 31.3 us: local(): block_piece = lax.all_gather(long_kv, 'seq', axis=2, tiled=True)]
    all_to_all x2 -> x0, waiting for transfers between devices: 51.4 us -> none  [the longest x1 49.3 us: local(): lax.all_to_all(sent_weighted.astype(jnp.bfloat16), ('req', 'seq'), split_...]
    dot_general x33 -> x0, matrix products: 36.5 us -> none  [the longest x4 9.46 us: cross_partial(): jnp.einsum('unhp,uphe->unhe', weights, value_rows.astype(jnp.float32), pr...]
    ppermute x0 -> x18, waiting for transfers between devices: none -> 32.7 us  [the longest x3 12.8 us: tp_swap(): return lax.ppermute(x, 'tp', [(i, (i + 1) % tps) for i in range(tps)])]
    gather x9 -> x0, local copies, waits for them, and re-layouts: 31.3 us -> none  [the longest x2 10.2 us: cross_block(): enc_keys[doc_short]]
    ppermute x0 -> x18, starting transfers between devices: none -> 27.6 us  [the longest x8 12.8 us: yz_shift(): return lax.ppermute(x, both, perm)]
    pallas_call x0 -> x8, Pallas kernels: none -> 26.9 us  [the longest x2 14.1 us: cross(): call(functools.partial(cross_kernel, seqs, requests), 'cross', shape((seq...]
  transfers between devices with their start and end apart: 7 -> 18, of which waited for: 7 -> 11; matrix products, arithmetic and copies ran while one was open for 10% -> 0% of each run, Pallas kernels for 0% -> 13%
where the time goes in v1:
time: 98 us; the launch traced here: 97.6 us
  waiting for transfers between devices  32.7 us (33%)
  starting transfers between devices  27.6 us (28%)
  Pallas kernels  26.9 us (27%)
  local copies, waits for them, and re-layouts  8.99 us (9%)
  between operations  1.44 us (1%)
    pallas_call x2, Pallas kernels, cross(): call(functools.partial(cross_kernel, seqs, requests), 'cross', shape((seq...  14.1 us
    ppermute x3, waiting for transfers between devices, tp_swap(): return lax.ppermute(x, 'tp', [(i, (i + 1) % tps) for i in range(tps)])  12.8 us
    ppermute x8, starting transfers between devices, yz_shift(): return lax.ppermute(x, both, perm)  12.8 us
    ppermute x8, waiting for transfers between devices, yz_shift(): return lax.ppermute(x, both, perm)  10.6 us
    ppermute x6, starting transfers between devices, seq_shift(): return lax.ppermute(x, 'seq', [(i, (i + k) % seqs) for i in range(seqs)])  9.6 us
    ppermute x6, waiting for transfers between devices, seq_shift(): return lax.ppermute(x, 'seq', [(i, (i + k) % seqs) for i in range(seqs)])  9.23 us
    unnamed x38, local copies, waits for them, and re-layouts  8.9 us
    pallas_call x1, Pallas kernels, local(): pl.pallas_call(ffn_kernel, grid=(hidden // block,), out_shape=(shape((all...  4.92 us
  transfers between devices with their start and end apart: 18, of which 11 were waited for; matrix products, arithmetic and copies ran while one was open for 0% of the time, Pallas kernels for 13%

profile of v1, /device:TPU:0, one launch (start us, length us, event | category | flops | bytes accessed | tf_op | source)
XLA Modules:
  0.0 97.6 jit_solution(11133264216685123547)
XLA Ops:
  1.8 1.9 %copy-done.3 = bf16[3,1024,512]{2,1,0:T(8,128)(2,1)S(1)} copy-done((bf16[3,1024,512]{2,1,0:T(8,128)(2,1)S(1)}, bf16[3,1024,512]{2,1,0:T(8,128)(2,1)}, u32[]{:S(2)}) %copy-start.3) | copy-done | bytes 3145752
  3.7 0.9 copy-done.8
  4.6 1.0 %copy-done.10 = bf16[1,2,256,512]{3,2,1,0:T(8,128)(2,1)S(1)} copy-done((bf16[1,2,256,512]{3,2,1,0:T(8,128)(2,1)S(1)}, bf16[1,2,256,512]{3,2,1,0:T(8,128)(2,1)}, u32[]{:S(2)}) %copy-start.10) | copy-done | bytes 524312
  6.5 1.1 %qkv.1 = (bf16[3,96,512]{2,1,0:T(8,128)(2,1)S(1)}, bf16[32,640]{1,0:T(8,128)(2,1)S(1)}) custom-call(s32[1]{0:T(128)S(6)} %copy.23.len_ref, bf16[2,32,1024]{2,1,0:T(8,128)(2,1)S(1)} %copy-done.8, bf16[1,32,1024]{2,1,0:T(8,128)(2,1)S(1)} %copy-done.11, bf16[3,1024,512]{2,1,0:T(8,128)(2,1)S(1)} %copy-done.3, bf16[1,2,256,512]{3,2,1,0:T(8,128)(2,1)S(1)} %copy-done.10), custom_call_target="tpu_custom_call" | custom-call | flops 100000000 | bytes 1000000 | tf_op jit(solution)/shard_map/qkv/pallas_call | solution.py:368
  7.6 4.7 %collective-permute-start.2 = (bf16[32,640]{1,0:T(8,128)(2,1)S(1)}, bf16[32,640]{1,0:T(8,128)(2,1)S(1)}, u32[]{:S(2)}, u32[]{:S(2)}) collective-permute-start(bf16[32,640]{1,0:T(8,128)(2,1)S(1)} %get-tuple-element.10.rest_0_), channel_id=1, source_target_pairs={{0,6},{2,0},{4,2},{6,4},{1,7},{3,1},{5,3},{7,5},{8,14},{10,8},{12,... | collective-permute-start | bytes 122888 | tf_op jit(solution)/shard_map/ppermute | solution.py:352
  12.3 1.0 %collective-permute-start = (bf16[32,640]{1,0:T(8,128)(2,1)S(1)}, bf16[32,640]{1,0:T(8,128)(2,1)S(1)}, u32[]{:S(2)}, u32[]{:S(2)}) collective-permute-start(bf16[32,640]{1,0:T(8,128)(2,1)S(1)} %get-tuple-element.10.rest_0_), channel_id=1, source_target_pairs={{0,2},{2,4},{4,6},{6,0},{1,3},{3,5},{5,7},{7,1},{8,10},{10,12},{12... | collective-permute-start | bytes 122888 | tf_op jit(solution)/shard_map/ppermute | solution.py:352
  13.3 0.9 collective-permute-done.2.rest_3_
  14.1 3.5 %collective-permute-done.1.rest_2_ = bf16[32,640]{1,0:T(8,128)(2,1)S(1)} collective-permute-done((bf16[32,640]{1,0:T(8,128)(2,1)S(1)}, bf16[32,640]{1,0:T(8,128)(2,1)S(1)}, u32[]{:S(2)}, u32[]{:S(2)}) %collective-permute-start.1) | collective-permute-done | bytes 40992 | tf_op jit(solution)/shard_map/ppermute | solution.py:352
  20.0 4.4 %attend.1.a_ref = bf16[96,1024]{1,0:T(8,128)(2,1)S(1)} custom-call(s32[2]{0:T(128)S(1)} %copy-done.15, s32[2,32]{1,0:T(2,128)S(1)} %copy-done.14, s32[1,32]{1,0:T(1,128)S(1)} %copy-done.16, bf16[3,96,512]{2,1,0:T(8,128)(2,1)S(1)} %get-tuple-element.9.qkv_ref, bf16[2,2,512,512]{3,2,1,0:T(8,128)(2,1)S(1)} %copy-done.4, bf16[512,1024]{1,0:T(8,128)(2,1)S(1)} %copy-done.5, ...), custom_call_target="tpu_custom_call" | custom-call | flops 100000000 | bytes 1000000 | tf_op jit(solution)/shard_map/attend/pallas_call | solution.py:375
  24.4 1.5 %collective-permute-start.3 = (bf16[96,1024]{1,0:T(8,128)(2,1)S(1)}, bf16[96,1024]{1,0:T(8,128)(2,1)S(1)}, u32[]{:S(2)}, u32[]{:S(2)}) collective-permute-start(bf16[96,1024]{1,0:T(8,128)(2,1)S(1)} %attend.1.a_ref), channel_id=1, source_target_pairs={{0,1},{1,0},{2,3},{3,2},{4,5},{5,4},{6,7},{7,6},{8,9},{9,8},{10,11... | collective-permute-start | bytes 589832 | tf_op jit(solution)/shard_map/ppermute | solution.py:364
  26.0 4.5 %collective-permute-done.3.b_ref = bf16[96,1024]{1,0:T(8,128)(2,1)S(1)} collective-permute-done((bf16[96,1024]{1,0:T(8,128)(2,1)S(1)}, bf16[96,1024]{1,0:T(8,128)(2,1)S(1)}, u32[]{:S(2)}, u32[]{:S(2)}) %collective-permute-start.3) | collective-permute-done | bytes 196640 | tf_op jit(solution)/shard_map/ppermute | solution.py:364
  31.0 1.7 %collective-permute-start.7 = (bf16[64,512]{1,0:T(8,128)(2,1)S(1)}, bf16[64,512]{1,0:T(8,128)(2,1)S(1)}, u32[]{:S(2)}, u32[]{:S(2)}) collective-permute-start(bf16[64,512]{1,0:T(8,128)(2,1)S(1)} %get-tuple-element.12), channel_id=1, source_target_pairs={{0,6},{2,0},{4,2},{6,4},{1,7},{3,1},{5,3},{7,5},{8,14},{10,8},{12,... | collective-permute-start | bytes 196616 | tf_op jit(solution)/shard_map/ppermute | solution.py:352
  33.0 1.9 %collective-permute-start.5 = (bf16[64,512]{1,0:T(8,128)(2,1)S(1)}, bf16[64,512]{1,0:T(8,128)(2,1)S(1)}, u32[]{:S(2)}, u32[]{:S(2)}) collective-permute-start(bf16[64,512]{1,0:T(8,128)(2,1)S(1)} %get-tuple-element.12), channel_id=1, source_target_pairs={{0,2},{2,4},{4,6},{6,0},{1,3},{3,5},{5,7},{7,1},{8,10},{10,12},{12... | collective-permute-start | bytes 196616 | tf_op jit(solution)/shard_map/ppermute | solution.py:352
  34.9 4.1 %collective-permute-done.5 = bf16[64,512]{1,0:T(8,128)(2,1)S(1)} collective-permute-done((bf16[64,512]{1,0:T(8,128)(2,1)S(1)}, bf16[64,512]{1,0:T(8,128)(2,1)S(1)}, u32[]{:S(2)}, u32[]{:S(2)}) %collective-permute-start.5) | collective-permute-done | bytes 65568 | tf_op jit(solution)/shard_map/ppermute | solution.py:352
  39.4 1.6 %collective-permute-start.11 = (bf16[288,512]{1,0:T(8,128)(2,1)S(1)}, bf16[288,512]{1,0:T(8,128)(2,1)S(1)}, u32[]{:S(2)}, u32[]{:S(2)}) collective-permute-start(bf16[288,512]{1,0:T(8,128)(2,1)S(1)} %constant_dynamic-update-slice_fusion.q_ref), channel_id=1, source_target_pairs={{0,16},{2,18},{4,20},{6,22},{8,24},{10,26},{12,28},{14,30},{16,0},... | collective-permute-start | bytes 884744 | tf_op jit(solution)/shard_map/ppermute | solution.py:361
  41.0 5.3 %collective-permute-done.11.q_ref = bf16[288,512]{1,0:T(8,128)(2,1)S(1)} collective-permute-done((bf16[288,512]{1,0:T(8,128)(2,1)S(1)}, bf16[288,512]{1,0:T(8,128)(2,1)S(1)}, u32[]{:S(2)}, u32[]{:S(2)}) %collective-permute-start.11) | collective-permute-done | bytes 294944 | tf_op jit(solution)/shard_map/ppermute | solution.py:361
  46.4 2.2 %copy-done = bf16[2,32,64,512]{3,2,1,0:T(8,128)(2,1)S(1)} copy-done((bf16[2,32,64,512]{3,2,1,0:T(8,128)(2,1)S(1)}, bf16[2,32,64,512]{3,2,1,0:T(8,128)(2,1)}, u32[]{:S(2)}) %copy-start) | copy-done | bytes 4194328
  48.5 7.1 %cross.3 = bf16[4,96,640]{2,1,0:T(8,128)(2,1)S(1)} custom-call(s32[1]{0:T(128)} %bitcast.5.group_ref, s32[32]{0:T(128)S(1)} %copy-done.12, s32[4]{0:T(128)S(1)} %copy-done.13, bf16[2,32,64,512]{3,2,1,0:T(8,128)(2,1)S(1)} %copy-done, bf16[2,32,64,512]{3,2,1,0:T(8,128)(2,1)} %collective-permute-done.4.other_ref, bf16[288,512]{1,0:T(8,128)(2,1)S(1)} %collective-permute-done.11.q_ref), custom_call_target="tpu_custom_call" | custom-call | flops 100000000 | bytes 1000000 | tf_op jit(solution)/shard_map/cross/pallas_call | solution.py:397
  56.4 2.0 %collective-permute-start.14 = (bf16[96,640]{1,0:T(8,128)(2,1)S(1)}, bf16[96,640]{1,0:T(8,128)(2,1)S(1)}, u32[]{:S(2)}, u32[]{:S(2)}) collective-permute-start(bf16[96,640]{1,0:T(8,128)(2,1)S(1)} %get-tuple-element.17), channel_id=1, source_target_pairs={{0,20},{2,22},{4,16},{6,18},{8,28},{10,30},{12,24},{14,26},{16,4},... | collective-permute-start | bytes 368648 | tf_op jit(solution)/shard_map/ppermute | solution.py:361
  58.4 3.7 %collective-permute-start.13 = (bf16[96,640]{1,0:T(8,128)(2,1)S(1)}, bf16[96,640]{1,0:T(8,128)(2,1)S(1)}, u32[]{:S(2)}, u32[]{:S(2)}) collective-permute-start(bf16[96,640]{1,0:T(8,128)(2,1)S(1)} %get-tuple-element.18), channel_id=1, source_target_pairs={{0,22},{2,16},{4,18},{6,20},{8,30},{10,24},{12,26},{14,28},{16,6},... | collective-permute-start | bytes 368648 | tf_op jit(solution)/shard_map/ppermute | solution.py:361
  62.7 7.1 %cross.2 = bf16[4,96,640]{2,1,0:T(8,128)(2,1)S(1)} custom-call(s32[1]{0:T(128)} %bitcast.group_ref, s32[32]{0:T(128)S(1)} %copy-done.12, s32[4]{0:T(128)S(1)} %copy-done.13, bf16[2,32,64,512]{3,2,1,0:T(8,128)(2,1)S(1)} %copy-done.1, bf16[2,32,64,512]{3,2,1,0:T(8,128)(2,1)} %collective-permute-done.4.other_ref, ...), custom_call_target="tpu_custom_call" | custom-call | flops 100000000 | bytes 1000000 | tf_op jit(solution)/shard_map/cross/pallas_call | solution.py:397
  69.9 1.3 %collective-permute-start.9 = (bf16[96,640]{1,0:T(8,128)(2,1)S(1)}, bf16[96,640]{1,0:T(8,128)(2,1)S(1)}, u32[]{:S(2)}, u32[]{:S(2)}) collective-permute-start(bf16[96,640]{1,0:T(8,128)(2,1)S(1)} %get-tuple-element.21), channel_id=1, source_target_pairs={{0,4},{2,6},{4,0},{6,2},{8,12},{10,14},{12,8},{14,10},{16,20},{18,... | collective-permute-start | bytes 368648 | tf_op jit(solution)/shard_map/ppermute | solution.py:361
  71.2 2.8 %collective-permute-start.8 = (bf16[96,640]{1,0:T(8,128)(2,1)S(1)}, bf16[96,640]{1,0:T(8,128)(2,1)S(1)}, u32[]{:S(2)}, u32[]{:S(2)}) collective-permute-start(bf16[96,640]{1,0:T(8,128)(2,1)S(1)} %get-tuple-element.22), channel_id=1, source_target_pairs={{0,6},{2,0},{4,2},{6,4},{8,14},{10,8},{12,10},{14,12},{16,22},{18,... | collective-permute-start | bytes 368648 | tf_op jit(solution)/shard_map/ppermute | solution.py:361
  74.1 2.7 %collective-permute-done.10.rest_3_ = bf16[96,640]{1,0:T(8,128)(2,1)S(1)} collective-permute-done((bf16[96,640]{1,0:T(8,128)(2,1)S(1)}, bf16[96,640]{1,0:T(8,128)(2,1)S(1)}, u32[]{:S(2)}, u32[]{:S(2)}) %collective-permute-start.10) | collective-permute-done | bytes 122912 | tf_op jit(solution)/shard_map/ppermute | solution.py:361
  76.7 2.6 %collective-permute-done.9.rest_2_ = bf16[96,640]{1,0:T(8,128)(2,1)S(1)} collective-permute-done((bf16[96,640]{1,0:T(8,128)(2,1)S(1)}, bf16[96,640]{1,0:T(8,128)(2,1)S(1)}, u32[]{:S(2)}, u32[]{:S(2)}) %collective-permute-start.9) | collective-permute-done | bytes 122912 | tf_op jit(solution)/shard_map/ppermute | solution.py:361
  79.3 0.9 merge.1.a_ref
  80.3 1.6 %collective-permute-start.16 = (bf16[96,1024]{1,0:T(8,128)(2,1)S(1)}, bf16[96,1024]{1,0:T(8,128)(2,1)S(1)}, u32[]{:S(2)}, u32[]{:S(2)}) collective-permute-start(bf16[96,1024]{1,0:T(8,128)(2,1)S(1)} %merge.1.a_ref), channel_id=1, source_target_pairs={{0,1},{1,0},{2,3},{3,2},{4,5},{5,4},{6,7},{7,6},{8,9},{9,8},{10,11... | collective-permute-start | bytes 589832 | tf_op jit(solution)/shard_map/ppermute | solution.py:364
  81.8 4.2 %collective-permute-done.16.b_ref = bf16[96,1024]{1,0:T(8,128)(2,1)S(1)} collective-permute-done((bf16[96,1024]{1,0:T(8,128)(2,1)S(1)}, bf16[96,1024]{1,0:T(8,128)(2,1)S(1)}, u32[]{:S(2)}, u32[]{:S(2)}) %collective-permute-start.16) | collective-permute-done | bytes 196640 | tf_op jit(solution)/shard_map/ppermute | solution.py:364
  86.0 4.9 %ffn.1 = (bf16[96,1024]{1,0:T(8,128)(2,1)S(1)}, bf16[96,1024]{1,0:T(8,128)(2,1)S(1)}) custom-call(bf16[96,1024]{1,0:T(8,128)(2,1)S(1)} %get-tuple-element.11.h_ref, bf16[96,1024]{1,0:T(8,128)(2,1)S(1)} %merge.1.a_ref, bf16[96,1024]{1,0:T(8,128)(2,1)S(1)} %collective-permute-done.16.b_ref, bf16[1024,2048]{1,0:T(8,128)(2,1)S(1)} %copy-done.2, ...), custom_call_target="tpu_custom_call" | custom-call | tf_op jit(solution)/shard_map/ffn/pallas_call | solution.py:428
  90.9 1.6 %collective-permute-start.17 = (bf16[96,1024]{1,0:T(8,128)(2,1)S(1)}, bf16[96,1024]{1,0:T(8,128)(2,1)S(1)}, u32[]{:S(2)}, u32[]{:S(2)}) collective-permute-start(bf16[96,1024]{1,0:T(8,128)(2,1)S(1)} %get-tuple-element.15.a_ref), channel_id=1, source_target_pairs={{0,1},{1,0},{2,3},{3,2},{4,5},{5,4},{6,7},{7,6},{8,9},{9,8},{10,11... | collective-permute-start | bytes 589832 | tf_op jit(solution)/shard_map/ppermute | solution.py:364
  92.5 4.2 %collective-permute-done.17.b_ref = bf16[96,1024]{1,0:T(8,128)(2,1)S(1)} collective-permute-done((bf16[96,1024]{1,0:T(8,128)(2,1)S(1)}, bf16[96,1024]{1,0:T(8,128)(2,1)S(1)}, u32[]{:S(2)}, u32[]{:S(2)}) %collective-permute-start.17) | collective-permute-done | bytes 196640 | tf_op jit(solution)/shard_map/ppermute | solution.py:364
  96.7 0.9 final.1
  (53 shorter events, 6.4 us)
Async XLA Ops:
  0.6 45.7 %collective-permute-start.4 = (bf16[2,32,64,512]{3,2,1,0:T(8,128)(2,1)}, bf16[2,32,64,512]{3,2,1,0:T(8,128)(2,1)}, u32[]{:S(2)}, u32[]{:S(2)}) collective-permute-start(bf16[2,32,64,512]{3,2,1,0:T(8,128)(2,1)} %own_ref.3), channel_id=1, source_target_pairs={{0,8},{8,0},{16,24},{24,16},{1,9},{9,1},{17,25},{25,17},{2,10},{10... | collective-permute-start | bytes 12582920 | tf_op jit(solution)/shard_map/ppermute | solution.py:366
  1.8 1.9 %copy-start.3 = (bf16[3,1024,512]{2,1,0:T(8,128)(2,1)S(1)}, bf16[3,1024,512]{2,1,0:T(8,128)(2,1)}, u32[]{:S(2)}) copy-start(bf16[3,1024,512]{2,1,0:T(8,128)(2,1)} %w_ref.3) | copy-start | bytes 9437188
  3.7 0.9 copy-start.8
  4.6 1.0 %copy-start.10 = (bf16[1,2,256,512]{3,2,1,0:T(8,128)(2,1)S(1)}, bf16[1,2,256,512]{3,2,1,0:T(8,128)(2,1)}, u32[]{:S(2)}) copy-start(bf16[1,2,256,512]{3,2,1,0:T(8,128)(2,1)} %kv_ref.1) | copy-start | bytes 1572868
  5.6 0.8 copy-start.11
  6.5 11.6 %copy-start.4 = (bf16[2,2,512,512]{3,2,1,0:T(8,128)(2,1)S(1)}, bf16[2,2,512,512]{3,2,1,0:T(8,128)(2,1)}, u32[]{:S(2)}) copy-start(bf16[2,2,512,512]{3,2,1,0:T(8,128)(2,1)} %skv_ref.1) | copy-start | bytes 6291460
  6.5 11.6 %copy-start.5 = (bf16[512,1024]{1,0:T(8,128)(2,1)S(1)}, bf16[512,1024]{1,0:T(8,128)(2,1)}, u32[]{:S(2)}) copy-start(bf16[512,1024]{1,0:T(8,128)(2,1)} %wo_ref.1) | copy-start | bytes 3145732
  6.5 24.0 %copy-start.6 = (bf16[1024,512]{1,0:T(8,128)(2,1)S(1)}, bf16[1024,512]{1,0:T(8,128)(2,1)}, u32[]{:S(2)}) copy-start(bf16[1024,512]{1,0:T(8,128)(2,1)} %w_ref.4) | copy-start | bytes 3145732
  6.5 24.0 %copy-start.9 = (bf16[2,32,1024]{2,1,0:T(8,128)(2,1)S(1)}, bf16[2,32,1024]{2,1,0:T(8,128)(2,1)}, u32[]{:S(2)}) copy-start(bf16[2,32,1024]{2,1,0:T(8,128)(2,1)} %xs_ref.3) | copy-start | bytes 393220
  6.5 39.8 %copy-start.12 = (s32[32]{0:T(128)S(1)}, s32[32]{0:T(128)}, u32[]{:S(2)}) copy-start(s32[32]{0:T(128)} %doc_ref.3) | copy-start | bytes 388
  6.5 39.8 %copy-start.13 = (s32[4]{0:T(128)S(1)}, s32[4]{0:T(128)}, u32[]{:S(2)}) copy-start(s32[4]{0:T(128)} %long_ref.3) | copy-start | bytes 52
  7.6 6.5 %collective-permute-start.2 = (bf16[32,640]{1,0:T(8,128)(2,1)S(1)}, bf16[32,640]{1,0:T(8,128)(2,1)S(1)}, u32[]{:S(2)}, u32[]{:S(2)}) collective-permute-start(bf16[32,640]{1,0:T(8,128)(2,1)S(1)} %get-tuple-element.10.rest_0_), channel_id=1, source_target_pairs={{0,6},{2,0},{4,2},{6,4},{1,7},{3,1},{5,3},{7,5},{8,14},{10,8},{12,... | collective-permute-start | bytes 122888 | tf_op jit(solution)/shard_map/ppermute | solution.py:352
  12.2 5.3 %collective-permute-start.1 = (bf16[32,640]{1,0:T(8,128)(2,1)S(1)}, bf16[32,640]{1,0:T(8,128)(2,1)S(1)}, u32[]{:S(2)}, u32[]{:S(2)}) collective-permute-start(bf16[32,640]{1,0:T(8,128)(2,1)S(1)} %get-tuple-element.10.rest_0_), channel_id=1, source_target_pairs={{0,4},{2,6},{4,0},{6,2},{1,5},{3,7},{5,1},{7,3},{8,12},{10,14},{12... | collective-permute-start | bytes 122888 | tf_op jit(solution)/shard_map/ppermute | solution.py:352
  12.3 5.8 %collective-permute-start = (bf16[32,640]{1,0:T(8,128)(2,1)S(1)}, bf16[32,640]{1,0:T(8,128)(2,1)S(1)}, u32[]{:S(2)}, u32[]{:S(2)}) collective-permute-start(bf16[32,640]{1,0:T(8,128)(2,1)S(1)} %get-tuple-element.10.rest_0_), channel_id=1, source_target_pairs={{0,2},{2,4},{4,6},{6,0},{1,3},{3,5},{5,7},{7,1},{8,10},{10,12},{12... | collective-permute-start | bytes 122888 | tf_op jit(solution)/shard_map/ppermute | solution.py:352
  24.4 6.0 %collective-permute-start.3 = (bf16[96,1024]{1,0:T(8,128)(2,1)S(1)}, bf16[96,1024]{1,0:T(8,128)(2,1)S(1)}, u32[]{:S(2)}, u32[]{:S(2)}) collective-permute-start(bf16[96,1024]{1,0:T(8,128)(2,1)S(1)} %attend.1.a_ref), channel_id=1, source_target_pairs={{0,1},{1,0},{2,3},{3,2},{4,5},{5,4},{6,7},{7,6},{8,9},{9,8},{10,11... | collective-permute-start | bytes 589832 | tf_op jit(solution)/shard_map/ppermute | solution.py:364
  31.0 8.4 %collective-permute-start.7 = (bf16[64,512]{1,0:T(8,128)(2,1)S(1)}, bf16[64,512]{1,0:T(8,128)(2,1)S(1)}, u32[]{:S(2)}, u32[]{:S(2)}) collective-permute-start(bf16[64,512]{1,0:T(8,128)(2,1)S(1)} %get-tuple-element.12), channel_id=1, source_target_pairs={{0,6},{2,0},{4,2},{6,4},{1,7},{3,1},{5,3},{7,5},{8,14},{10,8},{12,... | collective-permute-start | bytes 196616 | tf_op jit(solution)/shard_map/ppermute | solution.py:352
  32.7 6.7 %collective-permute-start.6 = (bf16[64,512]{1,0:T(8,128)(2,1)S(1)}, bf16[64,512]{1,0:T(8,128)(2,1)S(1)}, u32[]{:S(2)}, u32[]{:S(2)}) collective-permute-start(bf16[64,512]{1,0:T(8,128)(2,1)S(1)} %get-tuple-element.12), channel_id=1, source_target_pairs={{0,4},{2,6},{4,0},{6,2},{1,5},{3,7},{5,1},{7,3},{8,12},{10,14},{12... | collective-permute-start | bytes 196616 | tf_op jit(solution)/shard_map/ppermute | solution.py:352
  33.0 6.1 %collective-permute-start.5 = (bf16[64,512]{1,0:T(8,128)(2,1)S(1)}, bf16[64,512]{1,0:T(8,128)(2,1)S(1)}, u32[]{:S(2)}, u32[]{:S(2)}) collective-permute-start(bf16[64,512]{1,0:T(8,128)(2,1)S(1)} %get-tuple-element.12), channel_id=1, source_target_pairs={{0,2},{2,4},{4,6},{6,0},{1,3},{3,5},{5,7},{7,1},{8,10},{10,12},{12... | collective-permute-start | bytes 196616 | tf_op jit(solution)/shard_map/ppermute | solution.py:352
  39.4 6.9 %collective-permute-start.11 = (bf16[288,512]{1,0:T(8,128)(2,1)S(1)}, bf16[288,512]{1,0:T(8,128)(2,1)S(1)}, u32[]{:S(2)}, u32[]{:S(2)}) collective-permute-start(bf16[288,512]{1,0:T(8,128)(2,1)S(1)} %constant_dynamic-update-slice_fusion.q_ref), channel_id=1, source_target_pairs={{0,16},{2,18},{4,20},{6,22},{8,24},{10,26},{12,28},{14,30},{16,0},... | collective-permute-start | bytes 884744 | tf_op jit(solution)/shard_map/ppermute | solution.py:361
  46.3 2.2 %copy-start = (bf16[2,32,64,512]{3,2,1,0:T(8,128)(2,1)S(1)}, bf16[2,32,64,512]{3,2,1,0:T(8,128)(2,1)}, u32[]{:S(2)}) copy-start(bf16[2,32,64,512]{3,2,1,0:T(8,128)(2,1)} %own_ref.3) | copy-start | bytes 12582916
  48.5 14.1 %copy-start.1 = (bf16[2,32,64,512]{3,2,1,0:T(8,128)(2,1)S(1)}, bf16[2,32,64,512]{3,2,1,0:T(8,128)(2,1)}, u32[]{:S(2)}) copy-start(bf16[2,32,64,512]{3,2,1,0:T(8,128)(2,1)} %own_ref.3) | copy-start | bytes 12582916
  55.7 14.2 %collective-permute-start.15 = (bf16[96,640]{1,0:T(8,128)(2,1)S(1)}, bf16[96,640]{1,0:T(8,128)(2,1)S(1)}, u32[]{:S(2)}, u32[]{:S(2)}) collective-permute-start(bf16[96,640]{1,0:T(8,128)(2,1)S(1)} %get-tuple-element.16), channel_id=1, source_target_pairs={{0,18},{2,20},{4,22},{6,16},{8,26},{10,28},{12,30},{14,24},{16,2},... | collective-permute-start | bytes 368648 | tf_op jit(solution)/shard_map/ppermute | solution.py:361
  56.4 14.8 %collective-permute-start.14 = (bf16[96,640]{1,0:T(8,128)(2,1)S(1)}, bf16[96,640]{1,0:T(8,128)(2,1)S(1)}, u32[]{:S(2)}, u32[]{:S(2)}) collective-permute-start(bf16[96,640]{1,0:T(8,128)(2,1)S(1)} %get-tuple-element.17), channel_id=1, source_target_pairs={{0,20},{2,22},{4,16},{6,18},{8,28},{10,30},{12,24},{14,26},{16,4},... | collective-permute-start | bytes 368648 | tf_op jit(solution)/shard_map/ppermute | solution.py:361
  58.4 15.6 %collective-permute-start.13 = (bf16[96,640]{1,0:T(8,128)(2,1)S(1)}, bf16[96,640]{1,0:T(8,128)(2,1)S(1)}, u32[]{:S(2)}, u32[]{:S(2)}) collective-permute-start(bf16[96,640]{1,0:T(8,128)(2,1)S(1)} %get-tuple-element.18), channel_id=1, source_target_pairs={{0,22},{2,16},{4,18},{6,20},{8,30},{10,24},{12,26},{14,28},{16,6},... | collective-permute-start | bytes 368648 | tf_op jit(solution)/shard_map/ppermute | solution.py:361
  62.2 11.9 %collective-permute-start.12 = (bf16[96,640]{1,0:T(8,128)(2,1)S(1)}, bf16[96,640]{1,0:T(8,128)(2,1)S(1)}, u32[]{:S(2)}, u32[]{:S(2)}) collective-permute-start(bf16[96,640]{1,0:T(8,128)(2,1)S(1)} %get-tuple-element.19), channel_id=1, source_target_pairs={{0,16},{2,18},{4,20},{6,22},{8,24},{10,26},{12,28},{14,30},{16,0},... | collective-permute-start | bytes 368648 | tf_op jit(solution)/shard_map/ppermute | solution.py:361
  62.7 16.6 %copy-start.7 = (bf16[512,1024]{1,0:T(8,128)(2,1)S(1)}, bf16[512,1024]{1,0:T(8,128)(2,1)}, u32[]{:S(2)}) copy-start(bf16[512,1024]{1,0:T(8,128)(2,1)} %w_ref.5) | copy-start | bytes 3145732
  62.7 23.3 %copy-start.2 = (bf16[1024,2048]{1,0:T(8,128)(2,1)S(1)}, bf16[1024,2048]{1,0:T(8,128)(2,1)}, u32[]{:S(2)}) copy-start(bf16[1024,2048]{1,0:T(8,128)(2,1)} %up_ref.1) | copy-start | bytes 12582916
  69.8 6.9 %collective-permute-start.10 = (bf16[96,640]{1,0:T(8,128)(2,1)S(1)}, bf16[96,640]{1,0:T(8,128)(2,1)S(1)}, u32[]{:S(2)}, u32[]{:S(2)}) collective-permute-start(bf16[96,640]{1,0:T(8,128)(2,1)S(1)} %get-tuple-element.20), channel_id=1, source_target_pairs={{0,2},{2,4},{4,6},{6,0},{8,10},{10,12},{12,14},{14,8},{16,18},{18,... | collective-permute-start | bytes 368648 | tf_op jit(solution)/shard_map/ppermute | solution.py:361
  69.9 9.4 %collective-permute-start.9 = (bf16[96,640]{1,0:T(8,128)(2,1)S(1)}, bf16[96,640]{1,0:T(8,128)(2,1)S(1)}, u32[]{:S(2)}, u32[]{:S(2)}) collective-permute-start(bf16[96,640]{1,0:T(8,128)(2,1)S(1)} %get-tuple-element.21), channel_id=1, source_target_pairs={{0,4},{2,6},{4,0},{6,2},{8,12},{10,14},{12,8},{14,10},{16,20},{18,... | collective-permute-start | bytes 368648 | tf_op jit(solution)/shard_map/ppermute | solution.py:361
  71.2 8.1 %collective-permute-start.8 = (bf16[96,640]{1,0:T(8,128)(2,1)S(1)}, bf16[96,640]{1,0:T(8,128)(2,1)S(1)}, u32[]{:S(2)}, u32[]{:S(2)}) collective-permute-start(bf16[96,640]{1,0:T(8,128)(2,1)S(1)} %get-tuple-element.22), channel_id=1, source_target_pairs={{0,6},{2,0},{4,2},{6,4},{8,14},{10,8},{12,10},{14,12},{16,22},{18,... | collective-permute-start | bytes 368648 | tf_op jit(solution)/shard_map/ppermute | solution.py:361
  80.3 5.7 %collective-permute-start.16 = (bf16[96,1024]{1,0:T(8,128)(2,1)S(1)}, bf16[96,1024]{1,0:T(8,128)(2,1)S(1)}, u32[]{:S(2)}, u32[]{:S(2)}) collective-permute-start(bf16[96,1024]{1,0:T(8,128)(2,1)S(1)} %merge.1.a_ref), channel_id=1, source_target_pairs={{0,1},{1,0},{2,3},{3,2},{4,5},{5,4},{6,7},{7,6},{8,9},{9,8},{10,11... | collective-permute-start | bytes 589832 | tf_op jit(solution)/shard_map/ppermute | solution.py:364
  90.9 5.7 %collective-permute-start.17 = (bf16[96,1024]{1,0:T(8,128)(2,1)S(1)}, bf16[96,1024]{1,0:T(8,128)(2,1)S(1)}, u32[]{:S(2)}, u32[]{:S(2)}) collective-permute-start(bf16[96,1024]{1,0:T(8,128)(2,1)S(1)} %get-tuple-element.15.a_ref), channel_id=1, source_target_pairs={{0,1},{1,0},{2,3},{3,2},{4,5},{5,4},{6,7},{7,6},{8,9},{9,8},{10,11... | collective-permute-start | bytes 589832 | tf_op jit(solution)/shard_map/ppermute | solution.py:364
  (3 other events, 2.0 us)

commit v2 on v1

v2 whole, which is shorter than its diff:
```python
import functools

import jax
import jax.numpy as jnp
from jax import lax
from jax.experimental import pallas as pl
from jax.experimental.pallas import tpu as pltpu
from jax.sharding import PartitionSpec as P

HD = 64
LANES = 128
CORES = 2
PIECES = 3
SLOTS = 4
MASKED = -1e30
EPS = 1e-05
F32 = jnp.float32
BF16 = jnp.bfloat16
VMEM = pl.BlockSpec(memory_space=pltpu.VMEM)
SMEM = pl.BlockSpec(memory_space=pltpu.SMEM)
HBM = pl.BlockSpec(memory_space=pltpu.HBM)


def iota(shape, axis):
    return lax.broadcasted_iota(jnp.int32, shape, axis)


def dot(a, b):
    return lax.dot_general(a, b, (((1,), (0,)), ((), ())), preferred_element_type=F32)


def dot_t(a, b):
    return lax.dot_general(a, b, (((1,), (1,)), ((), ())), preferred_element_type=F32)


def normalize(v):
    centered = v - jnp.mean(v, axis=-1, keepdims=True)
    return centered * lax.rsqrt(jnp.mean(centered * centered, axis=-1, keepdims=True) + EPS)


def halves(rows, dtype):
    low = (iota((rows, LANES), 1) < HD).astype(F32)
    return low.astype(dtype), (1.0 - low).astype(dtype)


def scores_of(q, k):
    rows, width = q.shape
    low, high = halves(rows, BF16)
    parts = []
    for at in range(0, width, LANES):
        tile = q[:, at : at + LANES]
        pair = jnp.concatenate([tile * low, tile * high], axis=0)
        parts.append(dot_t(pair, k[:, at : at + LANES]))
    return jnp.concatenate(parts, axis=0) * HD ** (-0.5)


def values_of(p, v):
    width = v.shape[1]
    rows = p.shape[0] * HD // width
    low = iota((rows, LANES), 1) < HD
    p = p.astype(BF16)
    parts = []
    for at in range(0, width, LANES):
        row = at // HD * rows
        o = dot(p[row : row + 2 * rows], v[:, at : at + LANES])
        parts.append(jnp.where(low, o[:rows], o[rows:]))
    return jnp.concatenate(parts, axis=1)


def pack_stats(lse, heads, group):
    rows = lse.shape[0] // heads
    lane = iota((rows, LANES), 1)
    spread = jnp.zeros((rows, LANES), F32)
    for h in range(heads):
        spread = jnp.where(lane % heads == h, lse[h * rows : (h + 1) * rows], spread)
    high = spread.astype(BF16).astype(F32)
    rest = spread - high
    mid = rest.astype(BF16).astype(F32)
    low = (rest - mid).astype(BF16).astype(F32)
    place = lane // heads
    base = group * SLOTS
    packed = jnp.where(place == base, high, 0.0)
    packed = jnp.where(place == base + 1, mid, packed)
    return jnp.where(place == base + 2, low, packed)


def expand_stats(stats, heads, group=0):
    width = heads * HD
    lane = iota((LANES, width), 0)
    place = lane // heads - group * SLOTS
    hot = jnp.logical_and(lane % heads == iota((LANES, width), 1) // HD, place >= 0)
    hot = jnp.logical_and(hot, place < PIECES)
    return dot(stats, hot.astype(F32).astype(BF16))


def softmax_part(s, allowed):
    if allowed is not None:
        s = jnp.where(allowed, s, MASKED)
    m = jnp.max(s, axis=-1, keepdims=True)
    p = jnp.exp(s - m)
    if allowed is not None:
        p = jnp.where(allowed, p, 0.0)
    l = jnp.maximum(jnp.sum(p, axis=-1, keepdims=True), 1e-30)
    return p * (1.0 / l), m + jnp.log(l)


def merge(values, scores):
    top = functools.reduce(jnp.maximum, scores)
    total = acc = None
    for value, score in zip(values, scores):
        w = jnp.exp(score - top)
        total = w if total is None else total + w
        acc = w * value if acc is None else acc + w * value
    return acc / total


def ancestors(parents):
    rows = parents.shape[1]
    node_j = iota((rows, rows), 0)
    node_i = iota((rows, rows), 1)
    eye = (node_i == node_j).astype(F32)
    hot = jnp.logical_and(parents == node_j, node_i > 0).astype(F32)
    closure = eye + hot
    reach = 1
    while reach < rows:
        b = closure.astype(BF16)
        closure = jnp.minimum(dot(b, b), 1.0)
        reach *= 2
    return lax.dot_general(
        closure.astype(BF16),
        eye.astype(BF16),
        (((0,), (0,)), ((), ())),
        preferred_element_type=F32,
    )


def qkv_kernel(*refs):
    ins, outs, rest = refs[:8], refs[8:13], refs[13:]
    qkv_ref, x_ref, pay_ref, tree_ref, allow_ref = outs
    held, sems, ll = rest[:7], rest[7], ins[7]
    xs, xl, w, kv, ps, lp, sl = held
    copies = [
        pltpu.make_async_copy(a, b, sems.at[i])
        for i, (a, b) in enumerate(zip(ins, held))
        if i != 2
    ]
    w_copies = [
        pltpu.make_async_copy(ins[2].at[m], w.at[m], sems.at[7 + m]) for m in range(3)
    ]
    for copy in copies[4:] + copies[:2] + w_copies + copies[2:4]:
        copy.start()
    requests, short, model = xs.shape
    short_rows = requests * short
    rows = xl.shape[1]
    width = w.shape[2]
    heads = width // HD
    for copy in copies[3:]:
        copy.wait()
    for j in range(requests):
        tree_ref[j] = ancestors(ps[j : j + 1, :])
        allow_ref[j : j + 1, :] = (iota((1, allow_ref.shape[1]), 1) < sl[j]).astype(F32)
    tree_ref[requests] = ancestors(lp[...])
    for copy in copies[:2]:
        copy.wait()
    x = jnp.concatenate([xs[...].reshape(short_rows, model), xl[0]], axis=0)
    x_ref[...] = x
    for m in range(3):
        w_copies[m].wait()
        qkv_ref[m] = dot(x, w[m]).astype(BF16)
    copies[2].wait()
    span = kv.shape[2]
    allowed = iota((1, span), 1) + lax.axis_index("seq") * span < ll[0]
    s = scores_of(qkv_ref[0, short_rows:, :], kv[0, 0])
    p, lse = softmax_part(s, allowed)
    pay_ref[:, :width] = values_of(p, kv[0, 1]).astype(BF16)
    pay_ref[:, width:] = pack_stats(lse, heads, 0).astype(BF16)


def attend_kernel(qkv_ref, skv_ref, tree_ref, allow_ref, attn_ref, draft_ref, stat_ref):
    requests, _, span, width = skv_ref.shape
    heads = width // HD
    rows = tree_ref.shape[1]
    for j in range(requests):
        part = slice(j * rows, (j + 1) * rows)
        q = qkv_ref[0, part, :]
        allowed = allow_ref[j : j + 1, :] > 0.5
        allowed_d = jnp.concatenate([tree_ref[j]] * heads, axis=0) > 0.5
        s = jnp.where(allowed, scores_of(q, skv_ref[j, 0]), MASKED)
        d = jnp.where(allowed_d, scores_of(q, qkv_ref[1, part, :]), MASKED)
        m = jnp.maximum(jnp.max(s, axis=-1, keepdims=True), jnp.max(d, axis=-1, keepdims=True))
        p = jnp.where(allowed, jnp.exp(s - m), 0.0)
        pd = jnp.where(allowed_d, jnp.exp(d - m), 0.0)
        l = jnp.sum(p, axis=-1, keepdims=True) + jnp.sum(pd, axis=-1, keepdims=True)
        inverse = 1.0 / l
        o = values_of(p * inverse, skv_ref[j, 1]) + values_of(pd * inverse, qkv_ref[2, part, :])
        attn_ref[part, :] = o.astype(BF16)
    row = requests * rows
    allowed = jnp.concatenate([tree_ref[requests]] * heads, axis=0) > 0.5
    p, lse = softmax_part(scores_of(qkv_ref[0, row:, :], qkv_ref[1, row:, :]), allowed)
    draft_ref[...] = values_of(p, qkv_ref[2, row:, :])
    stat_ref[...] = pack_stats(lse, heads, 0).astype(BF16)


def output_kernel(hops, attn_ref, draft_ref, stat_ref, wo_ref, *rest):
    pay_refs, (out_ref, attn, pays) = rest[: hops + 1], rest[hops + 1 :]
    short_rows, width = attn_ref.shape
    heads = width // HD
    zed = lax.axis_index("seq")
    seqs = hops + 1
    for hop in range(seqs):
        pays[lax.rem(zed - hop + seqs, seqs)] = pay_refs[hop][...]
    values = [draft_ref[...]] + [pays[z, :, :width].astype(F32) for z in range(seqs)]
    scores = [expand_stats(stat_ref[...], heads)] + [
        expand_stats(pays[z, :, width:], heads) for z in range(seqs)
    ]
    attn[:short_rows, :] = attn_ref[...]
    attn[short_rows:, :] = merge(values, scores).astype(BF16)
    out_ref[...] = dot(attn[...], wo_ref[...]).astype(BF16)


def query_kernel(x_ref, a_ref, b_ref, w_ref, h_ref, q_ref, qs_ref):
    short_rows = qs_ref.shape[0]
    x = x_ref[...].astype(F32)
    h = normalize(x + (a_ref[...].astype(F32) + b_ref[...].astype(F32))).astype(BF16)
    h_ref[...] = h
    q = dot(h, w_ref[...]).astype(BF16)
    q_ref[...] = q[short_rows:]
    qs_ref[...] = q[:short_rows]


def fetch_kernel(seqs, requests, dys, doc_ref, long_ref, own_ref, other_ref, *rest):
    outs, sems = rest[: len(dys)], rest[len(dys)]
    span = own_ref.shape[2]
    short_total = seqs * requests
    zed = lax.axis_index("seq")
    req = lax.axis_index("req")
    pairs = lax.axis_size("req") // CORES
    for at, dy in enumerate(dys):
        group = lax.rem(req // CORES - dy + pairs, pairs) * CORES + lax.rem(req, CORES)
        kv = outs[at]
        copies = []
        for e in range(short_total + 1):
            if e == short_total:
                doc = long_ref[group]
            else:
                place = lax.rem(zed - e // requests + seqs, seqs)
                doc = doc_ref[(group * seqs + place) * requests + e % requests]
            for half, ref in enumerate((own_ref, other_ref)):
                copies.append(
                    pltpu.make_async_copy(
                        ref.at[:, doc],
                        kv.at[e, :, pl.ds(half * span, span)],
                        sems.at[at, e, half],
                    )
                )
                copies[-1].start()
        if at == 0:
            first = copies
        else:
            first = first + copies
    for copy in first:
        copy.wait()


def cross_kernel(seqs, requests, kv_ref, q_ref, *pay_refs):
    all_rows = q_ref.shape[0]
    width = q_ref.shape[1]
    heads = width // HD
    short_total = seqs * requests
    rows = all_rows // (short_total + 1)
    pay_rows = (requests + 1) * rows

    def one(e, group):
        s = scores_of(q_ref[e * rows : (e + 1) * rows, :], kv_ref[e, 0])
        p, lse = softmax_part(s, None)
        return values_of(p, kv_ref[e, 1]).astype(BF16), pack_stats(lse, heads, group)

    long_o, long_stats = one(short_total, requests)
    for k in range(seqs):
        stats = long_stats
        for j in range(requests):
            o, more = one(k * requests + j, j)
            stats = stats + more
            pay_refs[k][j * rows : (j + 1) * rows, :] = o
        pay_refs[k][requests * rows : pay_rows, :] = long_o
        for at in range(0, rows, 8):
            lanes = slice(at // 8 * LANES, (at // 8 + 1) * LANES)
            pay_refs[k][pay_rows:, lanes] = stats[at : at + 8].astype(BF16)


def merge_kernel(places, seqs, w_ref, *rest):
    ins, (out_ref, pays, cross) = rest[: len(places)], rest[len(places) :]
    all_rows, width = cross.shape
    heads = width // HD
    pairs = lax.axis_size("req") // CORES
    yed = lax.axis_index("req") // CORES
    zed = lax.axis_index("seq")
    for ref, (dy, dz) in zip(ins, places):
        at = lax.rem(yed - dy + pairs, pairs) * seqs + lax.rem(zed + dz, seqs)
        pays[at] = ref[...]
    stats = []
    for s in range(len(places)):
        block = pays[s, all_rows:, :].astype(F32)
        tiles = [block[:, at : at + LANES] for at in range(0, width, LANES)]
        stats.append(jnp.concatenate(tiles, axis=0).astype(BF16))
    step = 8 * width // LANES
    for group in range(all_rows // step):
        part = slice(group * step, (group + 1) * step)
        values = [pays[s, part, :].astype(F32) for s in range(len(places))]
        scores = [expand_stats(stats[s], heads, group) for s in range(len(places))]
        cross[part, :] = merge(values, scores).astype(BF16)
    out_ref[...] = dot(cross[...], w_ref[...]).astype(BF16)


def gelu(x):
    return 0.5 * x * (1.0 + lax.erf(x * 0.5**0.5))


def ffn_kernel(h_ref, a_ref, b_ref, up_ref, down_ref, h2_ref, out_ref):
    total = h_ref[...].astype(F32) + (a_ref[...].astype(F32) + b_ref[...].astype(F32))
    h2 = normalize(total).astype(BF16)
    h2_ref[...] = h2
    acc = None
    for at in range(0, up_ref.shape[1], 512):
        act = gelu(dot(h2, up_ref[:, at : at + 512])).astype(BF16)
        part = dot(act, down_ref[at : at + 512, :])
        acc = part if acc is None else acc + part
    out_ref[...] = acc.astype(BF16)


def final_kernel(h_ref, a_ref, b_ref, ys_ref, yl_ref):
    total = h_ref[...].astype(F32) + (a_ref[...].astype(F32) + b_ref[...].astype(F32))
    y = normalize(total).astype(BF16)
    short_rows = ys_ref.shape[0] * ys_ref.shape[1]
    ys_ref[...] = y[:short_rows].reshape(ys_ref.shape)
    yl_ref[0] = y[short_rows:]


def call(kernel, name, out, ins, scratch=(), flops=10**8, moved=10**6, grant=16 << 20):
    many = isinstance(out, (tuple, list))
    return pl.pallas_call(
        kernel,
        out_shape=out,
        in_specs=ins,
        out_specs=[VMEM] * len(out) if many else VMEM,
        scratch_shapes=list(scratch),
        name=name,
        cost_estimate=pl.CostEstimate(flops=flops, bytes_accessed=moved, transcendentals=0),
        compiler_params=pltpu.CompilerParams(vmem_limit_bytes=grant),
    )


def in_hbm(x):
    return pltpu.with_memory_space_constraint(x, pltpu.HBM)


def shape(dims, dtype=BF16):
    return jax.ShapeDtypeStruct(dims, dtype)


def local(
    x_short,
    x_long,
    parents,
    long_parents,
    short_len,
    long_len,
    doc_ids,
    long_doc,
    short_kv,
    long_kv,
    enc_kv,
    w_qkv,
    w_out,
    w_cross_q,
    w_cross_out,
    w_up,
    w_down,
):
    requests, rows, model = x_short.shape
    width = w_qkv.shape[2]
    heads = width // HD
    short_rows = requests * rows
    all_rows = short_rows + rows
    seqs = lax.axis_size("seq")
    reqs = lax.axis_size("req")
    tps = lax.axis_size("tp")
    pairs = reqs // CORES
    pay = width + LANES
    span = enc_kv.shape[2]
    both = ("req", "seq")

    def seq_shift(x, k):
        return lax.ppermute(x, "seq", [(i, (i + k) % seqs) for i in range(seqs)])

    def yz_shift(x, dy, dz):
        perm = []
        for y in range(pairs):
            for c in range(CORES):
                for z in range(seqs):
                    to = ((y + dy) % pairs * CORES + c) * seqs + (z + dz) % seqs
                    perm.append(((y * CORES + c) * seqs + z, to))
        return lax.ppermute(x, both, perm)

    def tp_swap(x):
        return lax.ppermute(x, "tp", [(i, (i + 1) % tps) for i in range(tps)])

    other_kv = lax.ppermute(enc_kv, "req", [(i, i ^ 1) for i in range(reqs)])

    qkv, inputs, long_pay, tree, allow = call(
        qkv_kernel,
        "qkv",
        (
            shape((3, all_rows, width)),
            shape((all_rows, model)),
            shape((rows, pay)),
            shape((requests + 1, rows, rows), F32),
            shape((requests, short_kv.shape[2]), F32),
        ),
        [HBM] * 7 + [SMEM],
        [
            pltpu.VMEM(x_short.shape, BF16),
            pltpu.VMEM(x_long.shape, BF16),
            pltpu.VMEM(w_qkv.shape, BF16),
            pltpu.VMEM(long_kv.shape, BF16),
            pltpu.VMEM(parents.shape, jnp.int32),
            pltpu.VMEM(long_parents.shape, jnp.int32),
            pltpu.SMEM(short_len.shape, jnp.int32),
            pltpu.SemaphoreType.DMA((10,)),
        ],
    )(
        *map(in_hbm, (x_short, x_long, w_qkv, long_kv, parents, long_parents, short_len)), long_len
    )
    got = [seq_shift(long_pay, k) for k in range(1, seqs)]
    attn, draft, stats = call(
        attend_kernel,
        "attend",
        (shape((short_rows, width)), shape((rows, width), F32), shape((rows, LANES))),
        [VMEM] * 4,
    )(qkv, short_kv, tree, allow)
    partial = call(
        functools.partial(output_kernel, seqs - 1),
        "output",
        shape((all_rows, model)),
        [VMEM] * (4 + seqs),
        [pltpu.VMEM((all_rows, width), BF16), pltpu.VMEM((seqs, rows, pay), BF16)],
    )(attn, draft, stats, w_out, long_pay, *got)

    hidden_one, q_long, q_short = call(
        query_kernel,
        "query",
        (shape((all_rows, model)), shape((rows, width)), shape((short_rows, width))),
        [VMEM] * 4,
    )(inputs, partial, tp_swap(partial), w_cross_q)

    shifted = [q_short] + [seq_shift(q_short, k) for k in range(1, seqs)]
    entries = seqs * requests + 1
    dys = tuple(range(pairs))
    docs, _ = lax.optimization_barrier((doc_ids, q_short))
    kvs = call(
        functools.partial(fetch_kernel, seqs, requests, dys),
        "fetch",
        tuple(shape((entries, 2, CORES * span, width)) for _ in dys),
        [SMEM] * 2 + [HBM] * 2,
        [pltpu.SemaphoreType.DMA((pairs, entries, 2))],
        flops=4 * 10**9,
    )(docs, long_doc, in_hbm(enc_kv), other_kv)
    shifted, kvs = lax.optimization_barrier((shifted, kvs))
    own_q = jnp.concatenate(shifted + [q_long])
    pay_rows = all_rows + rows * LANES // width

    pieces, places = [], []
    for dy in dys:
        q = own_q
        if dy:
            q, *done = lax.optimization_barrier((yz_shift(own_q, dy, 0), *out))
        out = call(
            functools.partial(cross_kernel, seqs, requests),
            "cross",
            [shape((pay_rows, width))] * seqs,
            [VMEM] * 2,
            flops=4 * 10**9,
        )(kvs[dy], q)
        for k in range(seqs):
            block = out[k]
            if (dy, k) != (0, 0):
                block = yz_shift(block, -dy, -k)
            pieces.append(block)
            places.append(((-dy) % pairs, k))
    partial = call(
        functools.partial(merge_kernel, tuple(places), seqs),
        "merge",
        shape((all_rows, model)),
        [VMEM] * (1 + len(pieces)),
        [pltpu.VMEM((len(pieces), pay_rows, width), BF16), pltpu.VMEM((all_rows, width), BF16)],
    )(w_cross_out, *pieces)

    hidden_two, partial = call(
        ffn_kernel, "ffn", (shape((all_rows, model)),) * 2, [VMEM] * 5
    )(hidden_one, partial, tp_swap(partial), w_up, w_down)

    return call(
        final_kernel,
        "final",
        (shape((requests, rows, model)), shape((1, rows, model))),
        [VMEM] * 3,
    )(hidden_two, partial, tp_swap(partial))


def solution(mesh):
    in_specs = (
        P(("req", "seq"), None, None),
        P("req", None, None),
        P(("req", "seq"), None),
        P("req", None),
        P(("req", "seq")),
        P("req"),
        P(),
        P(),
        P(("req", "seq"), None, None, "tp"),
        P("req", None, "seq", "tp"),
        P(None, None, ("req", "seq"), "tp"),
        P(None, None, "tp"),
        P("tp", None),
        P(None, "tp"),
        P("tp", None),
        P(None, "tp"),
        P("tp", None),
    )
    out_specs = (P(("req", "seq"), None, None), P("req", None, None))
    return jax.shard_map(local, mesh=mesh, in_specs=in_specs, out_specs=out_specs, check_vma=False)
```

time: 98 us -> 72.9 us (0.74)
  waiting for transfers between devices: 32.7 us -> 19.7 us
  local copies, waits for them, and re-layouts: 8.99 us -> 0.07 us
  Pallas kernels: 26.9 us -> 22.5 us
  starting transfers between devices: 27.6 us -> 28.8 us
    unnamed x38 -> x20, local copies, waits for them, and re-layouts: 8.9 us -> 0.06 us
    ppermute x6, waiting for transfers between devices: 9.23 us -> 1.89 us  [seq_shift(): return lax.ppermute(x, 'seq', [(i, (i + k) % seqs) for i in range(seqs)])]
    ppermute x8, waiting for transfers between devices: 10.6 us -> 4.75 us  [yz_shift(): return lax.ppermute(x, both, perm)]
    pallas_call x5 -> x7, Pallas kernels: 24.5 us -> 20.1 us  [the longest x2 7.13 us: local(): call(functools.partial(cross_kernel, seqs, requests), 'cross', [shape((pa...]
    ppermute x6, starting transfers between devices: 9.6 us -> 10.7 us  [seq_shift(): return lax.ppermute(x, 'seq', [(i, (i + k) % seqs) for i in range(seqs)])]
  transfers between devices with their start and end apart: 18 -> 18, of which waited for: 11 -> 9; matrix products, arithmetic and copies ran while one was open for 0% -> 0% of each run, Pallas kernels for 13% -> 26%
where the time goes in v2:
time: 72.9 us; the launch traced here: 72.7 us
  starting transfers between devices  28.8 us (40%)
  Pallas kernels  22.5 us (31%)
  waiting for transfers between devices  19.7 us (27%)
  between operations  1.73 us (2%)
    ppermute x3, waiting for transfers between devices, tp_swap(): return lax.ppermute(x, 'tp', [(i, (i + 1) % tps) for i in range(tps)])  13.1 us
    ppermute x8, starting transfers between devices, yz_shift(): return lax.ppermute(x, both, perm)  12.9 us
    ppermute x6, starting transfers between devices, seq_shift(): return lax.ppermute(x, 'seq', [(i, (i + k) % seqs) for i in range(seqs)])  10.7 us
    pallas_call x2, Pallas kernels, local(): call(functools.partial(cross_kernel, seqs, requests), 'cross', [shape((pa...  7.13 us
    pallas_call x1, Pallas kernels, local(): call(qkv_kernel, 'qkv', (shape((3, all_rows, width)), shape((all_rows, mo...  5.31 us
    ppermute x8, waiting for transfers between devices, yz_shift(): return lax.ppermute(x, both, perm)  4.75 us
    ppermute x3, starting transfers between devices, tp_swap(): return lax.ppermute(x, 'tp', [(i, (i + 1) % tps) for i in range(tps)])  4.66 us
    pallas_call x1, Pallas kernels, local(): call(functools.partial(fetch_kernel, seqs, requests, dys), 'fetch', tuple...  3.42 us
  transfers between devices with their start and end apart: 18, of which 9 were waited for; matrix products, arithmetic and copies ran while one was open for 0% of the time, Pallas kernels for 26%

profile of v2, /device:TPU:0, one launch (start us, length us, event | category | flops | bytes accessed | tf_op | source)
XLA Modules:
  0.0 72.7 jit_solution(6793296580087208870)
XLA Ops:
  0.7 0.5 collective-permute-start.7
  2.1 5.3 %qkv.1 = (bf16[3,96,512]{2,1,0:T(8,128)(2,1)S(1)}, bf16[96,1024]{1,0:T(8,128)(2,1)S(1)}, bf16[32,640]{1,0:T(8,128)(2,1)S(1)}, f32[3,32,32]{2,1,0:T(8,128)S(1)}, f32[2,512]{1,0:T(2,128)S(1)}) custom-call(bf16[2,32,1024]{2,1,0:T(8,128)(2,1)} %refs_0_.1, bf16[1,32,1024]{2,1,0:T(8,128)(2,1)} %refs_1_.1, bf16[3,1024,512]{2,1,0:T(8,128)(2,1)} %refs_2_.1, ...), custom_call_target="tpu_custom_call" | custom-call | flops 100000000 | bytes 1000000 | tf_op jit(solution)/shard_map/qkv/pallas_call | solution.py:410
  7.4 2.9 %collective-permute-start = (bf16[32,640]{1,0:T(8,128)(2,1)S(1)}, bf16[32,640]{1,0:T(8,128)(2,1)S(1)}, u32[]{:S(2)}, u32[]{:S(2)}) collective-permute-start(bf16[32,640]{1,0:T(8,128)(2,1)S(1)} %get-tuple-element.40.rest_0_), channel_id=1, source_target_pairs={{0,2},{2,4},{4,6},{6,0},{1,3},{3,5},{5,7},{7,1},{8,10},{10,12},{12... | collective-permute-start | bytes 122888 | tf_op jit(solution)/shard_map/ppermute | solution.py:394
  10.3 2.6 %collective-permute-start.1 = (bf16[32,640]{1,0:T(8,128)(2,1)S(1)}, bf16[32,640]{1,0:T(8,128)(2,1)S(1)}, u32[]{:S(2)}, u32[]{:S(2)}) collective-permute-start(bf16[32,640]{1,0:T(8,128)(2,1)S(1)} %get-tuple-element.40.rest_0_), channel_id=1, source_target_pairs={{0,4},{2,6},{4,0},{6,2},{1,5},{3,7},{5,1},{7,3},{8,12},{10,14},{12... | collective-permute-start | bytes 122888 | tf_op jit(solution)/shard_map/ppermute | solution.py:394
  12.9 1.4 %collective-permute-start.2 = (bf16[32,640]{1,0:T(8,128)(2,1)S(1)}, bf16[32,640]{1,0:T(8,128)(2,1)S(1)}, u32[]{:S(2)}, u32[]{:S(2)}) collective-permute-start(bf16[32,640]{1,0:T(8,128)(2,1)S(1)} %get-tuple-element.40.rest_0_), channel_id=1, source_target_pairs={{0,6},{2,0},{4,2},{6,4},{1,7},{3,1},{5,3},{7,5},{8,14},{10,8},{12,... | collective-permute-start | bytes 122888 | tf_op jit(solution)/shard_map/ppermute | solution.py:394
  14.3 1.8 %attend.1 = (bf16[64,512]{1,0:T(8,128)(2,1)S(1)}, f32[32,512]{1,0:T(8,128)S(1)}, bf16[32,128]{1,0:T(8,128)(2,1)S(1)}) custom-call(bf16[3,96,512]{2,1,0:T(8,128)(2,1)S(1)} %get-tuple-element.34.qkv_ref, bf16[2,2,512,512]{3,2,1,0:T(8,128)(2,1)S(1)} %copy-done.2, f32[3,32,32]{2,1,0:T(8,128)S(1)} %get-tuple-element.35.tree_ref, ...), custom_call_target="tpu_custom_call" | custom-call | flops 100000000 | bytes 1000000 | tf_op jit(solution)/shard_map/attend/pallas_call | solution.py:435
  16.9 0.5 output.1.a_ref
  17.4 1.6 %collective-permute-start.3 = (bf16[96,1024]{1,0:T(8,128)(2,1)S(1)}, bf16[96,1024]{1,0:T(8,128)(2,1)S(1)}, u32[]{:S(2)}, u32[]{:S(2)}) collective-permute-start(bf16[96,1024]{1,0:T(8,128)(2,1)S(1)} %output.1.a_ref), channel_id=1, source_target_pairs={{0,1},{1,0},{2,3},{3,2},{4,5},{5,4},{6,7},{7,6},{8,9},{9,8},{10,11... | collective-permute-start | bytes 589832 | tf_op jit(solution)/shard_map/ppermute | solution.py:406
  19.0 4.5 %collective-permute-done.3.b_ref = bf16[96,1024]{1,0:T(8,128)(2,1)S(1)} collective-permute-done((bf16[96,1024]{1,0:T(8,128)(2,1)S(1)}, bf16[96,1024]{1,0:T(8,128)(2,1)S(1)}, u32[]{:S(2)}, u32[]{:S(2)}) %collective-permute-start.3) | collective-permute-done | bytes 196640 | tf_op jit(solution)/shard_map/ppermute | solution.py:406
  23.5 0.5 query.1
  24.0 1.3 %collective-permute-start.4 = (bf16[64,512]{1,0:T(8,128)(2,1)S(1)}, bf16[64,512]{1,0:T(8,128)(2,1)S(1)}, u32[]{:S(2)}, u32[]{:S(2)}) collective-permute-start(bf16[64,512]{1,0:T(8,128)(2,1)S(1)} %get-tuple-element.47), channel_id=1, source_target_pairs={{0,2},{2,4},{4,6},{6,0},{1,3},{3,5},{5,7},{7,1},{8,10},{10,12},{12... | collective-permute-start | bytes 196616 | tf_op jit(solution)/shard_map/ppermute | solution.py:394
  25.3 2.2 %collective-permute-start.5 = (bf16[64,512]{1,0:T(8,128)(2,1)S(1)}, bf16[64,512]{1,0:T(8,128)(2,1)S(1)}, u32[]{:S(2)}, u32[]{:S(2)}) collective-permute-start(bf16[64,512]{1,0:T(8,128)(2,1)S(1)} %get-tuple-element.47), channel_id=1, source_target_pairs={{0,4},{2,6},{4,0},{6,2},{1,5},{3,7},{5,1},{7,3},{8,12},{10,14},{12... | collective-permute-start | bytes 196616 | tf_op jit(solution)/shard_map/ppermute | solution.py:394
  27.9 3.4 %fetch.1 = (bf16[9,2,128,512]{3,2,1,0:T(8,128)(2,1)S(1)}, bf16[9,2,128,512]{3,2,1,0:T(8,128)(2,1)S(1)}) custom-call(s32[32]{0:T(128)S(1)} %copy-done.6, s32[4]{0:T(128)S(1)} %copy-done.7, bf16[2,32,64,512]{3,2,1,0:T(8,128)(2,1)} %own_ref.1, bf16[2,32,64,512]{3,2,1,0:T(8,128)(2,1)S(1)} %collective-permute-done.7.other_ref), custom_call_target="tpu_custom_call" | custom-call | flops 4000000000 | bytes 1000000 | tf_op jit(solution)/shard_map/fetch/pallas_call | solution.py:460
  31.7 0.6 collective-permute-done.6
  32.4 1.6 %collective-permute-start.11 = (bf16[288,512]{1,0:T(8,128)(2,1)S(1)}, bf16[288,512]{1,0:T(8,128)(2,1)S(1)}, u32[]{:S(2)}, u32[]{:S(2)}) collective-permute-start(bf16[288,512]{1,0:T(8,128)(2,1)S(1)} %constant_dynamic-update-slice_fusion.q_ref), channel_id=1, source_target_pairs={{0,16},{2,18},{4,20},{6,22},{8,24},{10,26},{12,28},{14,30},{16,0},... | collective-permute-start | bytes 884744 | tf_op jit(solution)/shard_map/ppermute | solution.py:403
  34.1 3.6 %cross.2 = (bf16[104,512]{1,0:T(8,128)(2,1)S(1)}, bf16[104,512]{1,0:T(8,128)(2,1)S(1)}, bf16[104,512]{1,0:T(8,128)(2,1)S(1)}, bf16[104,512]{1,0:T(8,128)(2,1)S(1)}) custom-call(bf16[9,2,128,512]{3,2,1,0:T(8,128)(2,1)S(1)} %get-tuple-element.46.kv_ref, bf16[288,512]{1,0:T(8,128)(2,1)S(1)} %constant_dynamic-update-slice_fusion.q_ref), custom_call_target="tpu_custom_call" | custom-call | flops 4000000000 | bytes 1000000 | tf_op jit(solution)/shard_map/cross/pallas_call | solution.py:477
  37.6 0.6 collective-permute-start.10
  38.3 3.2 %collective-permute-start.8 = (bf16[104,512]{1,0:T(8,128)(2,1)S(1)}, bf16[104,512]{1,0:T(8,128)(2,1)S(1)}, u32[]{:S(2)}, u32[]{:S(2)}) collective-permute-start(bf16[104,512]{1,0:T(8,128)(2,1)S(1)} %get-tuple-element.53), channel_id=1, source_target_pairs={{0,6},{2,0},{4,2},{6,4},{8,14},{10,8},{12,10},{14,12},{16,22},{18,... | collective-permute-start | bytes 319496 | tf_op jit(solution)/shard_map/ppermute | solution.py:403
  41.5 3.6 %cross.3 = (bf16[104,512]{1,0:T(8,128)(2,1)S(1)}, bf16[104,512]{1,0:T(8,128)(2,1)S(1)}, bf16[104,512]{1,0:T(8,128)(2,1)S(1)}, bf16[104,512]{1,0:T(8,128)(2,1)S(1)}) custom-call(bf16[9,2,128,512]{3,2,1,0:T(8,128)(2,1)S(1)} %get-tuple-element.56.kv_ref, bf16[288,512]{1,0:T(8,128)(2,1)S(1)} %collective-permute-done.11.q_ref), custom_call_target="tpu_custom_call" | custom-call | flops 4000000000 | bytes 1000000 | tf_op jit(solution)/shard_map/cross/pallas_call | solution.py:477
  45.1 0.5 collective-permute-start.12
  45.7 2.1 %collective-permute-start.13 = (bf16[104,512]{1,0:T(8,128)(2,1)S(1)}, bf16[104,512]{1,0:T(8,128)(2,1)S(1)}, u32[]{:S(2)}, u32[]{:S(2)}) collective-permute-start(bf16[104,512]{1,0:T(8,128)(2,1)S(1)} %get-tuple-element.59), channel_id=1, source_target_pairs={{0,22},{2,16},{4,18},{6,20},{8,30},{10,24},{12,26},{14,28},{16,6},... | collective-permute-start | bytes 319496 | tf_op jit(solution)/shard_map/ppermute | solution.py:403
  47.8 1.8 %collective-permute-start.14 = (bf16[104,512]{1,0:T(8,128)(2,1)S(1)}, bf16[104,512]{1,0:T(8,128)(2,1)S(1)}, u32[]{:S(2)}, u32[]{:S(2)}) collective-permute-start(bf16[104,512]{1,0:T(8,128)(2,1)S(1)} %get-tuple-element.60), channel_id=1, source_target_pairs={{0,20},{2,22},{4,16},{6,18},{8,28},{10,30},{12,24},{14,26},{16,4},... | collective-permute-start | bytes 319496 | tf_op jit(solution)/shard_map/ppermute | solution.py:403
  49.6 2.9 %collective-permute-start.15 = (bf16[104,512]{1,0:T(8,128)(2,1)S(1)}, bf16[104,512]{1,0:T(8,128)(2,1)S(1)}, u32[]{:S(2)}, u32[]{:S(2)}) collective-permute-start(bf16[104,512]{1,0:T(8,128)(2,1)S(1)} %get-tuple-element.61), channel_id=1, source_target_pairs={{0,18},{2,20},{4,22},{6,16},{8,26},{10,28},{12,30},{14,24},{16,2},... | collective-permute-start | bytes 319496 | tf_op jit(solution)/shard_map/ppermute | solution.py:403
  52.5 1.2 %collective-permute-done.13.rest_5_ = bf16[104,512]{1,0:T(8,128)(2,1)S(1)} collective-permute-done((bf16[104,512]{1,0:T(8,128)(2,1)S(1)}, bf16[104,512]{1,0:T(8,128)(2,1)S(1)}, u32[]{:S(2)}, u32[]{:S(2)}) %collective-permute-start.13) | collective-permute-done | bytes 106528 | tf_op jit(solution)/shard_map/ppermute | solution.py:403
  53.7 3.5 %collective-permute-done.14.rest_6_ = bf16[104,512]{1,0:T(8,128)(2,1)S(1)} collective-permute-done((bf16[104,512]{1,0:T(8,128)(2,1)S(1)}, bf16[104,512]{1,0:T(8,128)(2,1)S(1)}, u32[]{:S(2)}, u32[]{:S(2)}) %collective-permute-start.14) | collective-permute-done | bytes 106528 | tf_op jit(solution)/shard_map/ppermute | solution.py:403
  57.2 0.9 %merge.1.a_ref = bf16[96,1024]{1,0:T(8,128)(2,1)S(1)} custom-call(bf16[512,1024]{1,0:T(8,128)(2,1)S(1)} %copy-done.5, bf16[104,512]{1,0:T(8,128)(2,1)S(1)} %get-tuple-element.52.rest_0_, bf16[104,512]{1,0:T(8,128)(2,1)S(1)} %collective-permute-done.8.rest_1_, bf16[104,512]{1,0:T(8,128)(2,1)S(1)} %collective-permute-done.9.rest_2_, ...), custom_call_target="tpu_custom_call" | custom-call | flops 100000000 | bytes 1000000 | tf_op jit(solution)/shard_map/merge/pallas_call | solution.py:490
  58.2 1.6 %collective-permute-start.16 = (bf16[96,1024]{1,0:T(8,128)(2,1)S(1)}, bf16[96,1024]{1,0:T(8,128)(2,1)S(1)}, u32[]{:S(2)}, u32[]{:S(2)}) collective-permute-start(bf16[96,1024]{1,0:T(8,128)(2,1)S(1)} %merge.1.a_ref), channel_id=1, source_target_pairs={{0,1},{1,0},{2,3},{3,2},{4,5},{5,4},{6,7},{7,6},{8,9},{9,8},{10,11... | collective-permute-start | bytes 589832 | tf_op jit(solution)/shard_map/ppermute | solution.py:406
  59.7 4.4 %collective-permute-done.16.b_ref = bf16[96,1024]{1,0:T(8,128)(2,1)S(1)} collective-permute-done((bf16[96,1024]{1,0:T(8,128)(2,1)S(1)}, bf16[96,1024]{1,0:T(8,128)(2,1)S(1)}, u32[]{:S(2)}, u32[]{:S(2)}) %collective-permute-start.16) | collective-permute-done | bytes 196640 | tf_op jit(solution)/shard_map/ppermute | solution.py:406
  64.1 2.0 %ffn.1 = (bf16[96,1024]{1,0:T(8,128)(2,1)S(1)}, bf16[96,1024]{1,0:T(8,128)(2,1)S(1)}) custom-call(bf16[96,1024]{1,0:T(8,128)(2,1)S(1)} %get-tuple-element.41.h_ref, bf16[96,1024]{1,0:T(8,128)(2,1)S(1)} %merge.1.a_ref, bf16[96,1024]{1,0:T(8,128)(2,1)S(1)} %collective-permute-done.16.b_ref, bf16[1024,2048]{1,0:T(8,128)(2,1)S(1)} %copy-done, ...), custom_call_target="tpu_custom_call" | custom-call | flops 100000000 | bytes 1000000 | tf_op jit(solution)/shard_map/ffn/pallas_call | solution.py:498
  66.1 1.5 %collective-permute-start.17 = (bf16[96,1024]{1,0:T(8,128)(2,1)S(1)}, bf16[96,1024]{1,0:T(8,128)(2,1)S(1)}, u32[]{:S(2)}, u32[]{:S(2)}) collective-permute-start(bf16[96,1024]{1,0:T(8,128)(2,1)S(1)} %get-tuple-element.63.a_ref), channel_id=1, source_target_pairs={{0,1},{1,0},{2,3},{3,2},{4,5},{5,4},{6,7},{7,6},{8,9},{9,8},{10,11... | collective-permute-start | bytes 589832 | tf_op jit(solution)/shard_map/ppermute | solution.py:406
  67.6 4.2 %collective-permute-done.17.b_ref = bf16[96,1024]{1,0:T(8,128)(2,1)S(1)} collective-permute-done((bf16[96,1024]{1,0:T(8,128)(2,1)S(1)}, bf16[96,1024]{1,0:T(8,128)(2,1)S(1)}, u32[]{:S(2)}, u32[]{:S(2)}) %collective-permute-start.17) | collective-permute-done | bytes 196640 | tf_op jit(solution)/shard_map/ppermute | solution.py:406
  71.8 0.9 %final.1 = (bf16[2,32,1024]{2,1,0:T(8,128)(2,1)}, bf16[1,32,1024]{2,1,0:T(8,128)(2,1)}) custom-call(bf16[96,1024]{1,0:T(8,128)(2,1)S(1)} %get-tuple-element.62.h_ref, bf16[96,1024]{1,0:T(8,128)(2,1)S(1)} %get-tuple-element.63.a_ref, bf16[96,1024]{1,0:T(8,128)(2,1)S(1)} %collective-permute-done.17.b_ref), custom_call_target="tpu_custom_call" | custom-call | flops 100000000 | bytes 1000000 | tf_op jit(solution)/shard_map/final/pallas_call | solution.py:502
  (35 shorter events, 1.8 us)
Async XLA Ops:
  0.6 13.6 %copy-start.2 = (bf16[2,2,512,512]{3,2,1,0:T(8,128)(2,1)S(1)}, bf16[2,2,512,512]{3,2,1,0:T(8,128)(2,1)}, u32[]{:S(2)}) copy-start(bf16[2,2,512,512]{3,2,1,0:T(8,128)(2,1)} %skv_ref.1) | copy-start | bytes 6291460
  0.6 16.3 %copy-start.3 = (bf16[512,1024]{1,0:T(8,128)(2,1)S(1)}, bf16[512,1024]{1,0:T(8,128)(2,1)}, u32[]{:S(2)}) copy-start(bf16[512,1024]{1,0:T(8,128)(2,1)} %wo_ref.1) | copy-start | bytes 3145732
  0.7 22.9 %copy-start.4 = (bf16[1024,512]{1,0:T(8,128)(2,1)S(1)}, bf16[1024,512]{1,0:T(8,128)(2,1)}, u32[]{:S(2)}) copy-start(bf16[1024,512]{1,0:T(8,128)(2,1)} %w_ref.2) | copy-start | bytes 3145732
  0.7 27.3 %collective-permute-start.7 = (bf16[2,32,64,512]{3,2,1,0:T(8,128)(2,1)}, bf16[2,32,64,512]{3,2,1,0:T(8,128)(2,1)S(1)}, u32[]{:S(2)}, u32[]{:S(2)}) collective-permute-start(bf16[2,32,64,512]{3,2,1,0:T(8,128)(2,1)} %own_ref.1), channel_id=1, source_target_pairs={{0,8},{8,0},{16,24},{24,16},{1,9},{9,1},{17,25},{25,17},{2,10},{10... | collective-permute-start | bytes 12582920 | tf_op jit(solution)/shard_map/ppermute | solution.py:408
  2.1 25.8 %copy-start.6 = (s32[32]{0:T(128)S(1)}, s32[32]{0:T(128)}, u32[]{:S(2)}) copy-start(s32[32]{0:T(128)} %doc_ref) | copy-start | bytes 388
  2.1 25.8 %copy-start.7 = (s32[4]{0:T(128)S(1)}, s32[4]{0:T(128)}, u32[]{:S(2)}) copy-start(s32[4]{0:T(128)} %long_ref.1) | copy-start | bytes 52
  7.4 8.6 %collective-permute-start = (bf16[32,640]{1,0:T(8,128)(2,1)S(1)}, bf16[32,640]{1,0:T(8,128)(2,1)S(1)}, u32[]{:S(2)}, u32[]{:S(2)}) collective-permute-start(bf16[32,640]{1,0:T(8,128)(2,1)S(1)} %get-tuple-element.40.rest_0_), channel_id=1, source_target_pairs={{0,2},{2,4},{4,6},{6,0},{1,3},{3,5},{5,7},{7,1},{8,10},{10,12},{12... | collective-permute-start | bytes 122888 | tf_op jit(solution)/shard_map/ppermute | solution.py:394
  10.3 6.2 %collective-permute-start.1 = (bf16[32,640]{1,0:T(8,128)(2,1)S(1)}, bf16[32,640]{1,0:T(8,128)(2,1)S(1)}, u32[]{:S(2)}, u32[]{:S(2)}) collective-permute-start(bf16[32,640]{1,0:T(8,128)(2,1)S(1)} %get-tuple-element.40.rest_0_), channel_id=1, source_target_pairs={{0,4},{2,6},{4,0},{6,2},{1,5},{3,7},{5,1},{7,3},{8,12},{10,14},{12... | collective-permute-start | bytes 122888 | tf_op jit(solution)/shard_map/ppermute | solution.py:394
  12.9 4.0 %collective-permute-start.2 = (bf16[32,640]{1,0:T(8,128)(2,1)S(1)}, bf16[32,640]{1,0:T(8,128)(2,1)S(1)}, u32[]{:S(2)}, u32[]{:S(2)}) collective-permute-start(bf16[32,640]{1,0:T(8,128)(2,1)S(1)} %get-tuple-element.40.rest_0_), channel_id=1, source_target_pairs={{0,6},{2,0},{4,2},{6,4},{1,7},{3,1},{5,3},{7,5},{8,14},{10,8},{12,... | collective-permute-start | bytes 122888 | tf_op jit(solution)/shard_map/ppermute | solution.py:394
  17.4 6.1 %collective-permute-start.3 = (bf16[96,1024]{1,0:T(8,128)(2,1)S(1)}, bf16[96,1024]{1,0:T(8,128)(2,1)S(1)}, u32[]{:S(2)}, u32[]{:S(2)}) collective-permute-start(bf16[96,1024]{1,0:T(8,128)(2,1)S(1)} %output.1.a_ref), channel_id=1, source_target_pairs={{0,1},{1,0},{2,3},{3,2},{4,5},{5,4},{6,7},{7,6},{8,9},{9,8},{10,11... | collective-permute-start | bytes 589832 | tf_op jit(solution)/shard_map/ppermute | solution.py:406
  24.0 7.3 %collective-permute-start.4 = (bf16[64,512]{1,0:T(8,128)(2,1)S(1)}, bf16[64,512]{1,0:T(8,128)(2,1)S(1)}, u32[]{:S(2)}, u32[]{:S(2)}) collective-permute-start(bf16[64,512]{1,0:T(8,128)(2,1)S(1)} %get-tuple-element.47), channel_id=1, source_target_pairs={{0,2},{2,4},{4,6},{6,0},{1,3},{3,5},{5,7},{7,1},{8,10},{10,12},{12... | collective-permute-start | bytes 196616 | tf_op jit(solution)/shard_map/ppermute | solution.py:394
  25.3 6.4 %collective-permute-start.5 = (bf16[64,512]{1,0:T(8,128)(2,1)S(1)}, bf16[64,512]{1,0:T(8,128)(2,1)S(1)}, u32[]{:S(2)}, u32[]{:S(2)}) collective-permute-start(bf16[64,512]{1,0:T(8,128)(2,1)S(1)} %get-tuple-element.47), channel_id=1, source_target_pairs={{0,4},{2,6},{4,0},{6,2},{1,5},{3,7},{5,1},{7,3},{8,12},{10,14},{12... | collective-permute-start | bytes 196616 | tf_op jit(solution)/shard_map/ppermute | solution.py:394
  27.5 4.9 %collective-permute-start.6 = (bf16[64,512]{1,0:T(8,128)(2,1)S(1)}, bf16[64,512]{1,0:T(8,128)(2,1)S(1)}, u32[]{:S(2)}, u32[]{:S(2)}) collective-permute-start(bf16[64,512]{1,0:T(8,128)(2,1)S(1)} %get-tuple-element.47), channel_id=1, source_target_pairs={{0,6},{2,0},{4,2},{6,4},{1,7},{3,1},{5,3},{7,5},{8,14},{10,8},{12,... | collective-permute-start | bytes 196616 | tf_op jit(solution)/shard_map/ppermute | solution.py:394
  32.4 9.1 %collective-permute-start.11 = (bf16[288,512]{1,0:T(8,128)(2,1)S(1)}, bf16[288,512]{1,0:T(8,128)(2,1)S(1)}, u32[]{:S(2)}, u32[]{:S(2)}) collective-permute-start(bf16[288,512]{1,0:T(8,128)(2,1)S(1)} %constant_dynamic-update-slice_fusion.q_ref), channel_id=1, source_target_pairs={{0,16},{2,18},{4,20},{6,22},{8,24},{10,26},{12,28},{14,30},{16,0},... | collective-permute-start | bytes 884744 | tf_op jit(solution)/shard_map/ppermute | solution.py:403
  37.6 10.1 %collective-permute-start.10 = (bf16[104,512]{1,0:T(8,128)(2,1)S(1)}, bf16[104,512]{1,0:T(8,128)(2,1)S(1)}, u32[]{:S(2)}, u32[]{:S(2)}) collective-permute-start(bf16[104,512]{1,0:T(8,128)(2,1)S(1)} %get-tuple-element.55), channel_id=1, source_target_pairs={{0,2},{2,4},{4,6},{6,0},{8,10},{10,12},{12,14},{14,8},{16,18},{18,... | collective-permute-start | bytes 319496 | tf_op jit(solution)/shard_map/ppermute | solution.py:403
  38.3 11.3 %collective-permute-start.8 = (bf16[104,512]{1,0:T(8,128)(2,1)S(1)}, bf16[104,512]{1,0:T(8,128)(2,1)S(1)}, u32[]{:S(2)}, u32[]{:S(2)}) collective-permute-start(bf16[104,512]{1,0:T(8,128)(2,1)S(1)} %get-tuple-element.53), channel_id=1, source_target_pairs={{0,6},{2,0},{4,2},{6,4},{8,14},{10,8},{12,10},{14,12},{16,22},{18,... | collective-permute-start | bytes 319496 | tf_op jit(solution)/shard_map/ppermute | solution.py:403
  41.5 11.0 %collective-permute-start.9 = (bf16[104,512]{1,0:T(8,128)(2,1)S(1)}, bf16[104,512]{1,0:T(8,128)(2,1)S(1)}, u32[]{:S(2)}, u32[]{:S(2)}) collective-permute-start(bf16[104,512]{1,0:T(8,128)(2,1)S(1)} %get-tuple-element.54), channel_id=1, source_target_pairs={{0,4},{2,6},{4,0},{6,2},{8,12},{10,14},{12,8},{14,10},{16,20},{18,... | collective-permute-start | bytes 319496 | tf_op jit(solution)/shard_map/ppermute | solution.py:403
  41.5 15.7 %copy-start.5 = (bf16[512,1024]{1,0:T(8,128)(2,1)S(1)}, bf16[512,1024]{1,0:T(8,128)(2,1)}, u32[]{:S(2)}) copy-start(bf16[512,1024]{1,0:T(8,128)(2,1)} %w_ref.3) | copy-start | bytes 3145732
  41.5 22.6 %copy-start = (bf16[1024,2048]{1,0:T(8,128)(2,1)S(1)}, bf16[1024,2048]{1,0:T(8,128)(2,1)}, u32[]{:S(2)}) copy-start(bf16[1024,2048]{1,0:T(8,128)(2,1)} %up_ref.1) | copy-start | bytes 12582916
  41.5 22.6 %copy-start.1 = (bf16[2048,1024]{1,0:T(8,128)(2,1)S(1)}, bf16[2048,1024]{1,0:T(8,128)(2,1)}, u32[]{:S(2)}) copy-start(bf16[2048,1024]{1,0:T(8,128)(2,1)} %down_ref.1) | copy-start | bytes 12582916
  45.1 7.4 %collective-permute-start.12 = (bf16[104,512]{1,0:T(8,128)(2,1)S(1)}, bf16[104,512]{1,0:T(8,128)(2,1)S(1)}, u32[]{:S(2)}, u32[]{:S(2)}) collective-permute-start(bf16[104,512]{1,0:T(8,128)(2,1)S(1)} %get-tuple-element.58), channel_id=1, source_target_pairs={{0,16},{2,18},{4,20},{6,22},{8,24},{10,26},{12,28},{14,30},{16,0},... | collective-permute-start | bytes 319496 | tf_op jit(solution)/shard_map/ppermute | solution.py:403
  45.7 8.0 %collective-permute-start.13 = (bf16[104,512]{1,0:T(8,128)(2,1)S(1)}, bf16[104,512]{1,0:T(8,128)(2,1)S(1)}, u32[]{:S(2)}, u32[]{:S(2)}) collective-permute-start(bf16[104,512]{1,0:T(8,128)(2,1)S(1)} %get-tuple-element.59), channel_id=1, source_target_pairs={{0,22},{2,16},{4,18},{6,20},{8,30},{10,24},{12,26},{14,28},{16,6},... | collective-permute-start | bytes 319496 | tf_op jit(solution)/shard_map/ppermute | solution.py:403
  47.8 9.5 %collective-permute-start.14 = (bf16[104,512]{1,0:T(8,128)(2,1)S(1)}, bf16[104,512]{1,0:T(8,128)(2,1)S(1)}, u32[]{:S(2)}, u32[]{:S(2)}) collective-permute-start(bf16[104,512]{1,0:T(8,128)(2,1)S(1)} %get-tuple-element.60), channel_id=1, source_target_pairs={{0,20},{2,22},{4,16},{6,18},{8,28},{10,30},{12,24},{14,26},{16,4},... | collective-permute-start | bytes 319496 | tf_op jit(solution)/shard_map/ppermute | solution.py:403
  49.6 7.7 %collective-permute-start.15 = (bf16[104,512]{1,0:T(8,128)(2,1)S(1)}, bf16[104,512]{1,0:T(8,128)(2,1)S(1)}, u32[]{:S(2)}, u32[]{:S(2)}) collective-permute-start(bf16[104,512]{1,0:T(8,128)(2,1)S(1)} %get-tuple-element.61), channel_id=1, source_target_pairs={{0,18},{2,20},{4,22},{6,16},{8,26},{10,28},{12,30},{14,24},{16,2},... | collective-permute-start | bytes 319496 | tf_op jit(solution)/shard_map/ppermute | solution.py:403
  58.2 5.9 %collective-permute-start.16 = (bf16[96,1024]{1,0:T(8,128)(2,1)S(1)}, bf16[96,1024]{1,0:T(8,128)(2,1)S(1)}, u32[]{:S(2)}, u32[]{:S(2)}) collective-permute-start(bf16[96,1024]{1,0:T(8,128)(2,1)S(1)} %merge.1.a_ref), channel_id=1, source_target_pairs={{0,1},{1,0},{2,3},{3,2},{4,5},{5,4},{6,7},{7,6},{8,9},{9,8},{10,11... | collective-permute-start | bytes 589832 | tf_op jit(solution)/shard_map/ppermute | solution.py:406
  66.1 5.7 %collective-permute-start.17 = (bf16[96,1024]{1,0:T(8,128)(2,1)S(1)}, bf16[96,1024]{1,0:T(8,128)(2,1)S(1)}, u32[]{:S(2)}, u32[]{:S(2)}) collective-permute-start(bf16[96,1024]{1,0:T(8,128)(2,1)S(1)} %get-tuple-element.63.a_ref), channel_id=1, source_target_pairs={{0,1},{1,0},{2,3},{3,2},{4,5},{5,4},{6,7},{7,6},{8,9},{9,8},{10,11... | collective-permute-start | bytes 589832 | tf_op jit(solution)/shard_map/ppermute | solution.py:406

commit v3 on v2

v3 whole, which is shorter than its diff:
```python
import functools

import jax
import jax.numpy as jnp
from jax import lax
from jax.experimental import pallas as pl
from jax.experimental.pallas import tpu as pltpu
from jax.sharding import PartitionSpec as P

HD = 64
LANES = 128
CORES = 2
PIECES = 3
SLOTS = 4
MASKED = -1e30
EPS = 1e-05
F32 = jnp.float32
BF16 = jnp.bfloat16
VMEM = pl.BlockSpec(memory_space=pltpu.VMEM)
SMEM = pl.BlockSpec(memory_space=pltpu.SMEM)
HBM = pl.BlockSpec(memory_space=pltpu.HBM)


def iota(shape, axis):
    return lax.broadcasted_iota(jnp.int32, shape, axis)


def dot(a, b):
    return lax.dot_general(a, b, (((1,), (0,)), ((), ())), preferred_element_type=F32)


def dot_t(a, b):
    return lax.dot_general(a, b, (((1,), (1,)), ((), ())), preferred_element_type=F32)


def normalize(v):
    centered = v - jnp.mean(v, axis=-1, keepdims=True)
    return centered * lax.rsqrt(jnp.mean(centered * centered, axis=-1, keepdims=True) + EPS)


def halves(rows, dtype):
    low = (iota((rows, LANES), 1) < HD).astype(F32)
    return low.astype(dtype), (1.0 - low).astype(dtype)


def scores_of(q, k):
    rows, width = q.shape
    low, high = (half * HD ** (-0.5) for half in halves(rows, BF16))
    parts = []
    for at in range(0, width, LANES):
        tile = q[:, at : at + LANES]
        pair = jnp.concatenate([tile * low, tile * high], axis=0)
        parts.append(dot_t(pair, k[:, at : at + LANES]))
    return jnp.concatenate(parts, axis=0)


def sums_of(p):
    return dot(p, jnp.ones((p.shape[1], LANES), BF16))


def values_of(terms, total):
    width = terms[0][1].shape[1]
    rows = total.shape[0] * HD // width
    low = iota((rows, LANES), 1) < HD
    parts = []
    for at in range(0, width, LANES):
        row = at // HD * rows
        mid, end = row + rows, row + 2 * rows
        o = sum(dot(p[row:end], v[:, at : at + LANES]) for p, v in terms)
        o = jnp.where(low, o[:rows], o[rows:])
        parts.append(o / jnp.where(low, total[row:mid], total[mid:end]))
    return jnp.concatenate(parts, axis=1)


def spread(columns, heads):
    rows = columns.shape[0] // heads
    lane = iota((rows, LANES), 1) % heads
    out = jnp.zeros((rows, LANES), F32)
    for h in range(heads):
        out = jnp.where(lane == h, columns[h * rows : (h + 1) * rows], out)
    return out


def pack_stats(lse, heads, group=None):
    place = iota(lse.shape, 1) // heads
    if group is None:
        group, place = 0, place % SLOTS
    high = lse.astype(BF16).astype(F32)
    rest = lse - high
    mid = rest.astype(BF16).astype(F32)
    low = (rest - mid).astype(BF16).astype(F32)
    base = group * SLOTS
    packed = jnp.where(place == base, high, 0.0)
    packed = jnp.where(place == base + 1, mid, packed)
    return jnp.where(place == base + 2, low, packed)


def piece_hot(heads, group, shape, per_head):
    lane = iota(shape, 0)
    place = lane // heads - group * SLOTS
    hot = jnp.logical_and(lane % heads == per_head, place >= 0)
    return jnp.logical_and(hot, place < PIECES).astype(F32).astype(BF16)


def expand_stats(stats, heads, group=0):
    shape = (LANES, heads * HD)
    return dot(stats, piece_hot(heads, group, shape, iota(shape, 1) // HD))


def respread(stats, heads):
    shape = (LANES, LANES)
    return dot(stats, piece_hot(heads, 0, shape, iota(shape, 1) % heads))


def softmax_part(s, v, heads, allowed=None):
    if allowed is not None:
        s = jnp.where(allowed, s, MASKED)
    m = jnp.max(s, axis=-1, keepdims=True)
    p = jnp.exp(s - m)
    if allowed is not None:
        p = jnp.where(allowed, p, 0.0)
    p = p.astype(BF16)
    l = jnp.maximum(sums_of(p), 1e-30)
    return values_of([(p, v)], l), spread(m, heads) + jnp.log(spread(l, heads))


def merge(values, scores):
    top = functools.reduce(jnp.maximum, scores)
    total = acc = None
    for value, score in zip(values, scores):
        w = jnp.exp(score - top)
        total = w if total is None else total + w
        acc = w * value if acc is None else acc + w * value
    return acc / total


def ancestors(parents, rows):
    nodes = parents.shape[1]
    node_j = iota((nodes, nodes), 0)
    node_i = iota((nodes, nodes), 1)
    target = parents + node_i // rows * rows
    hot = jnp.logical_and(target == node_j, node_i % rows > 0).astype(F32)
    closure = (node_i == node_j).astype(F32) + hot
    reach = 1
    while reach < rows:
        b = closure.astype(BF16)
        closure = jnp.minimum(dot(b, b), 1.0)
        reach *= 2
    shape = (nodes, rows)
    place = (iota(shape, 0) % rows == iota(shape, 1)).astype(F32)
    return lax.dot_general(
        closure.astype(BF16),
        place.astype(BF16),
        (((0,), (0,)), ((), ())),
        preferred_element_type=F32,
    )


def first_kernel(
    xs_hbm, xl_hbm, w_hbm, kv_hbm, ps_hbm, lp_hbm, q_ref, x_ref, kv_ref, tree_ref, w, ps, lp, sems
):
    requests, rows, model = xs_hbm.shape
    short_rows = requests * rows
    moves = [(ps_hbm, ps), (lp_hbm, lp)]
    moves += [(xs_hbm.at[j], x_ref.at[pl.ds(j * rows, rows)]) for j in range(requests)]
    moves += [(xl_hbm.at[0], x_ref.at[pl.ds(short_rows, rows)]), (w_hbm.at[0], w)]
    moves += [(kv_hbm.at[0], kv_ref)]
    copies = [pltpu.make_async_copy(a, b, sems.at[i]) for i, (a, b) in enumerate(moves)]
    for copy in copies:
        copy.start()
    for copy in copies[:2]:
        copy.wait()
    parents = [ps[j : j + 1, :] for j in range(requests)] + [lp[...]]
    tree_ref[...] = ancestors(jnp.concatenate(parents, axis=1), rows)
    for copy in copies[2:-1]:
        copy.wait()
    q_ref[...] = dot(x_ref[...], w[...]).astype(BF16)
    copies[-1].wait()


def long_kernel(q_ref, kv_ref, len_ref, pay_ref):
    rows = pay_ref.shape[0]
    width = q_ref.shape[1]
    heads = width // HD
    span = kv_ref.shape[1]
    allowed = iota((1, span), 1) + lax.axis_index("seq") * span < len_ref[:, :1]
    s = scores_of(q_ref[q_ref.shape[0] - rows :, :], kv_ref[0])
    o, lse = softmax_part(s, kv_ref[1], heads, allowed)
    pay_ref[:, :width] = o.astype(BF16)
    pay_ref[:, width:] = pack_stats(lse, heads, 0).astype(BF16)


def short_attend(q, k, v, cache_k, cache_v, allowed, tree, heads):
    allowed_d = jnp.concatenate([tree] * heads, axis=0) > 0.5
    s = jnp.where(allowed, scores_of(q, cache_k), MASKED)
    d = jnp.where(allowed_d, scores_of(q, k), MASKED)
    m = jnp.maximum(jnp.max(s, axis=-1, keepdims=True), jnp.max(d, axis=-1, keepdims=True))
    p = jnp.exp(s - m).astype(BF16)
    pd = jnp.exp(d - m).astype(BF16)
    return values_of([(p, cache_v), (pd, v)], sums_of(p) + sums_of(pd)).astype(BF16)


def attend_kernel(
    q_ref, x_ref, w_ref, skv_ref, tree_ref, sl_hbm, attn_ref, draft_ref, stat_ref, sl, sem
):
    requests = skv_ref.shape[0]
    rows = tree_ref.shape[1]
    copy = pltpu.make_async_copy(sl_hbm, sl, sem.at[0])
    copy.start()
    heads = q_ref.shape[1] // HD
    span = skv_ref.shape[2]
    x = x_ref[...]
    k = dot(x, w_ref[1]).astype(BF16)
    v = dot(x, w_ref[2]).astype(BF16)
    row = requests * rows
    allowed = jnp.concatenate([tree_ref[row:, :]] * heads, axis=0) > 0.5
    s = scores_of(q_ref[row:, :], k[row:])
    o, lse = softmax_part(s, v[row:], heads, allowed)
    draft_ref[...] = o
    stat_ref[...] = pack_stats(lse, heads, 0).astype(BF16)
    copy.wait()
    for j in range(requests):
        part = slice(j * rows, (j + 1) * rows)
        attn_ref[part, :] = short_attend(
            q_ref[part, :], k[part], v[part], skv_ref[j, 0], skv_ref[j, 1],
            iota((1, span), 1) < sl[j], tree_ref[part, :], heads,
        )


def output_kernel(hops, attn_ref, draft_ref, stat_ref, wo_ref, *rest):
    pay_refs, (out_ref, attn, pays) = rest[: hops + 1], rest[hops + 1 :]
    short_rows, width = attn_ref.shape
    heads = width // HD
    zed = lax.axis_index("seq")
    for hop, ref in enumerate(pay_refs):
        pays[zed ^ hop] = ref[...]
    values = [draft_ref[...]] + [pays[z, :, :width].astype(F32) for z in range(hops + 1)]
    scores = [expand_stats(stat_ref[...], heads)] + [
        expand_stats(pays[z, :, width:], heads) for z in range(hops + 1)
    ]
    attn[:short_rows, :] = attn_ref[...]
    attn[short_rows:, :] = merge(values, scores).astype(BF16)
    out_ref[...] = dot(attn[...], wo_ref[...]).astype(BF16)


def query_kernel(x_ref, a_ref, b_ref, w_ref, h_ref, q_ref, qs_ref):
    short_rows = qs_ref.shape[0]
    x = x_ref[...].astype(F32)
    h = normalize(x + (a_ref[...].astype(F32) + b_ref[...].astype(F32))).astype(BF16)
    h_ref[...] = h
    q = dot(h, w_ref[...]).astype(BF16)
    q_ref[...] = q
    qs_ref[...] = q[:short_rows]


def fetch_kernel(seqs, requests, dys, doc_ref, long_ref, own_ref, other_ref, *rest):
    outs, sems = rest[: len(dys)], rest[len(dys)]
    span = own_ref.shape[2]
    short_total = seqs * requests
    zed = lax.axis_index("seq")
    req = lax.axis_index("req")
    pairs = lax.axis_size("req") // CORES
    for at, dy in enumerate(dys):
        group = lax.rem(req // CORES - dy + pairs, pairs) * CORES + lax.rem(req, CORES)
        kv = outs[at]
        copies = []
        for e in range(short_total + 1):
            if e == short_total:
                doc = long_ref[group]
            else:
                place = zed ^ (e // requests)
                doc = doc_ref[(group * seqs + place) * requests + e % requests]
            for half, ref in enumerate((own_ref, other_ref)):
                copies.append(
                    pltpu.make_async_copy(
                        ref.at[:, doc],
                        kv.at[e, :, pl.ds(half * span, span)],
                        sems.at[at, e, half],
                    )
                )
                copies[-1].start()
        if at == 0:
            first = copies
        else:
            first = first + copies
    for copy in first:
        copy.wait()


def document_part(kv_ref, e, q, heads, group):
    o, lse = softmax_part(scores_of(q, kv_ref[e, 0]), kv_ref[e, 1], heads)
    return o.astype(BF16), pack_stats(lse, heads, group)


def fill(pay_ref, parts, long_o, long_stats):
    rows = long_o.shape[0]
    for j, (o, more) in enumerate(parts):
        pay_ref[j * rows : (j + 1) * rows, :] = o
        long_stats = long_stats + more
    end = (len(parts) + 1) * rows
    pay_ref[end - rows : end, :] = long_o
    write_stats(pay_ref, end, long_stats)


def write_stats(pay_ref, row, stats):
    for at in range(0, stats.shape[0], 8):
        lanes = slice(at // 8 * LANES, (at // 8 + 1) * LANES)
        pay_ref[row : row + 8, lanes] = stats[at : at + 8].astype(BF16)


def read_stats(block):
    block = block.astype(F32)
    tiles = [block[:, at : at + LANES] for at in range(0, block.shape[1], LANES)]
    return jnp.concatenate(tiles, axis=0).astype(BF16)


def near_kernel(requests, kv_ref, q_ref, pay_ref, o_ref, stat_ref):
    rows, width = o_ref.shape
    heads = width // HD
    last = q_ref.shape[0] - rows
    o, stats = document_part(kv_ref, kv_ref.shape[0] - 1, q_ref[last:, :], heads, requests)
    o_ref[...] = o
    stat_ref[...] = stats
    parts = [
        document_part(kv_ref, j, q_ref[j * rows : (j + 1) * rows, :], heads, j)
        for j in range(requests)
    ]
    fill(pay_ref, parts, o, stats)


def row_kernel(requests, stacked, single, kv_ref, o_ref, stat_ref, q_ref, *outs):
    rows, width = o_ref.shape
    heads = width // HD
    targets = [outs[0].at[i] for i in range(len(stacked))]
    targets += outs[1 if stacked else 0 :]
    for k, target in zip(stacked + single, targets):
        parts = []
        for j in range(requests):
            row = ((k - 1) * requests + j) * rows
            q = q_ref[row : row + rows, :]
            parts.append(document_part(kv_ref, k * requests + j, q, heads, j))
        fill(target, parts, o_ref[...], stat_ref[...])


def join(two, out, groups, heads):
    rows, width = out.shape
    step = rows * width // (groups * width + LANES)
    end = groups * step
    lane, other = (iota((LANES, LANES), axis) for axis in range(2))
    slots = heads * SLOTS
    hot = jnp.logical_and(lane % heads == other % heads, lane // slots == other // slots)
    hot = jnp.logical_and(hot, lane // heads % SLOTS < PIECES).astype(F32).astype(BF16)
    stats = [read_stats(two[i, end:, :]) for i in range(2)]
    for group in range(groups):
        part = slice(group * step, (group + 1) * step)
        scores = [expand_stats(x, heads, group) for x in stats]
        out[part, :] = merge([two[i, part, :].astype(F32) for i in range(2)], scores).astype(BF16)
    left, right = (dot(x, hot) for x in stats)
    top = jnp.maximum(left, right)
    lse = top + jnp.log(jnp.exp(left - top) + jnp.exp(right - top))
    write_stats(out, end, pack_stats(lse, heads))


def join_kernel(groups, skip, odd_ref, *rest):
    count = len(rest) // 2
    two = rest[-1]
    heads = two.shape[2] // HD
    odd_z = lax.axis_index("seq") & 1
    for e in range(count):
        two[odd_z] = rest[e][...]
        two[1 - odd_z] = odd_ref[skip + e]
        join(two, rest[count + e], groups, heads)


def merge_kernel(dys, seqs, groups, w_ref, *rest):
    half = seqs // 2
    ins, (out_ref, pays, two, cross) = rest[:-4], rest[-4:]
    all_rows, width = cross.shape
    heads = width // HD
    pairs = lax.axis_size("req") // CORES
    yed = lax.axis_index("req") // CORES
    zed = lax.axis_index("seq")
    odd_z = zed & 1
    per = half + 1
    for at, dy in enumerate(dys):
        zero, one, *far = ins[at * per : (at + 1) * per]
        base = lax.rem(yed + dy, pairs) * half
        two[odd_z] = zero[...]
        two[1 - odd_z] = one[...] if dy else one[0]
        join(two, pays.at[base + zed // 2], groups, heads)
        for e, ref in enumerate(far, 1):
            pays[base + (zed ^ (2 * e)) // 2] = ref[...]
    total = len(dys) * half
    stats = [read_stats(pays[s, all_rows:, :]) for s in range(total)]
    step = all_rows // groups
    for group in range(groups):
        part = slice(group * step, (group + 1) * step)
        values = [pays[s, part, :].astype(F32) for s in range(total)]
        scores = [expand_stats(stats[s], heads, group) for s in range(total)]
        cross[part, :] = merge(values, scores).astype(BF16)
    out_ref[...] = dot(cross[...], w_ref[...]).astype(BF16)


def gelu(x):
    return 0.5 * x * (1.0 + lax.erf(x * 0.5**0.5))


def ffn_kernel(h_ref, a_ref, b_ref, up_ref, down_ref, h2_ref, out_ref):
    total = h_ref[...].astype(F32) + (a_ref[...].astype(F32) + b_ref[...].astype(F32))
    h2 = normalize(total).astype(BF16)
    h2_ref[...] = h2
    acc = None
    for at in range(0, up_ref.shape[1], 512):
        act = gelu(dot(h2, up_ref[:, at : at + 512])).astype(BF16)
        part = dot(act, down_ref[at : at + 512, :])
        acc = part if acc is None else acc + part
    out_ref[...] = acc.astype(BF16)


def final_kernel(h_ref, a_ref, b_ref, ys_ref, yl_ref):
    total = h_ref[...].astype(F32) + (a_ref[...].astype(F32) + b_ref[...].astype(F32))
    y = normalize(total).astype(BF16)
    short_rows = ys_ref.shape[0] * ys_ref.shape[1]
    ys_ref[...] = y[:short_rows].reshape(ys_ref.shape)
    yl_ref[0] = y[short_rows:]


def call(kernel, name, out, ins, scratch=(), flops=10**8, moved=10**6, grant=16 << 20):
    many = isinstance(out, (tuple, list))
    return pl.pallas_call(
        kernel,
        out_shape=out,
        in_specs=ins,
        out_specs=[VMEM] * len(out) if many else VMEM,
        scratch_shapes=list(scratch),
        name=name,
        cost_estimate=pl.CostEstimate(flops=flops, bytes_accessed=moved, transcendentals=0),
        compiler_params=pltpu.CompilerParams(vmem_limit_bytes=grant),
    )


def in_hbm(x):
    return pltpu.with_memory_space_constraint(x, pltpu.HBM)


def shape(dims, dtype=BF16):
    return jax.ShapeDtypeStruct(dims, dtype)


def local(
    x_short,
    x_long,
    parents,
    long_parents,
    short_len,
    long_len,
    doc_ids,
    long_doc,
    short_kv,
    long_kv,
    enc_kv,
    w_qkv,
    w_out,
    w_cross_q,
    w_cross_out,
    w_up,
    w_down,
):
    requests, rows, model = x_short.shape
    width = w_qkv.shape[2]
    heads = width // HD
    short_rows = requests * rows
    all_rows = short_rows + rows
    seqs = lax.axis_size("seq")
    reqs = lax.axis_size("req")
    tps = lax.axis_size("tp")
    pairs = reqs // CORES
    pay = width + LANES
    span = enc_kv.shape[2]
    both = ("req", "seq")

    def seq_pair(x, k):
        return lax.ppermute(x, "seq", [(i, i ^ k) for i in range(seqs)])

    def yz_move(x, dy, dz):
        perm = []
        for y in range(pairs):
            for c in range(CORES):
                for z in range(seqs):
                    to = ((y + dy) % pairs * CORES + c) * seqs + (z ^ dz)
                    perm.append(((y * CORES + c) * seqs + z, to))
        return lax.ppermute(x, both, perm)

    def tp_swap(x):
        return lax.ppermute(x, "tp", [(i, (i + 1) % tps) for i in range(tps)])

    xs, xl, w_hbm, kv_hbm = map(in_hbm, (x_short, x_long, w_qkv, long_kv))
    queries, inputs, cache, tree = call(
        first_kernel,
        "first",
        (
            shape((all_rows, width)),
            shape((all_rows, model)),
            shape(long_kv.shape[1:]),
            shape((all_rows, rows), F32),
        ),
        [HBM] * 6,
        [
            pltpu.VMEM((model, width), BF16),
            pltpu.VMEM(parents.shape, jnp.int32),
            pltpu.VMEM(long_parents.shape, jnp.int32),
            pltpu.SemaphoreType.DMA((requests + 5,)),
        ],
    )(xs, xl, w_hbm, kv_hbm, in_hbm(parents), in_hbm(long_parents))
    late = (w_qkv, short_kv, w_out, w_cross_q, enc_kv)
    late, queries = lax.optimization_barrier((late, queries))
    w_qkv, short_kv, w_out, w_cross_q, enc_kv = late
    long_pay = call(
        long_kernel, "long", shape((rows, pay)), [VMEM] * 3, flops=8 * 10**9
    )(queries, cache, jnp.broadcast_to(long_len.reshape(1, 1), (1, LANES)))
    got = [seq_pair(long_pay, k) for k in range(1, seqs)]
    other_kv = lax.ppermute(enc_kv, "req", [(i, i ^ 1) for i in range(reqs)])

    attn, draft, stats = call(
        attend_kernel,
        "attend",
        (shape((short_rows, width)), shape((rows, width), F32), shape((rows, LANES))),
        [VMEM] * 5 + [HBM],
        [pltpu.SMEM(short_len.shape, jnp.int32), pltpu.SemaphoreType.DMA((1,))],
        flops=4 * 10**9,
    )(queries, inputs, w_qkv, short_kv, tree, in_hbm(short_len))
    got, attn = lax.optimization_barrier((got, attn))
    partial = call(
        functools.partial(output_kernel, seqs - 1),
        "output",
        shape((all_rows, model)),
        [VMEM] * (4 + seqs),
        [pltpu.VMEM((all_rows, width), BF16), pltpu.VMEM((seqs, rows, pay), BF16)],
    )(attn, draft, stats, w_out, long_pay, *got)

    entries = seqs * requests + 1
    dys = tuple(range(pairs))
    docs, _ = lax.optimization_barrier((doc_ids, partial))
    kvs = call(
        functools.partial(fetch_kernel, seqs, requests, dys),
        "fetch",
        tuple(shape((entries, 2, CORES * span, width)) for _ in dys),
        [SMEM] * 2 + [HBM] * 2,
        [pltpu.SemaphoreType.DMA((pairs, entries, 2))],
        flops=4 * 10**9,
    )(docs, long_doc, in_hbm(enc_kv), other_kv)
    swapped, kvs = lax.optimization_barrier((tp_swap(partial), kvs))
    hidden_one, q_all, q_short = call(
        query_kernel,
        "query",
        (shape((all_rows, model)), shape((all_rows, width)), shape((short_rows, width))),
        [VMEM] * 4,
    )(inputs, partial, swapped, w_cross_q)

    pay_rows = all_rows + rows * LANES // width
    block = shape((pay_rows, width))
    groups = requests + 1
    half = seqs // 2
    odds, evens = list(range(1, seqs, 2)), list(range(2, seqs, 2))

    def near(kv, q):
        return call(
            functools.partial(near_kernel, requests),
            "near",
            (block, shape((rows, width)), shape((rows, LANES), F32)),
            [VMEM] * 2,
            flops=10**9,
        )(kv, q)

    def row(stacked, single, kv, long_o, long_stats, q):
        stack = [shape((len(stacked), pay_rows, width))] if stacked else []
        return call(
            functools.partial(row_kernel, requests, stacked, single),
            "row",
            stack + [block] * len(single),
            [VMEM] * 4,
            flops=10**9,
        )(kv, long_o, long_stats, q)

    def joined(skip, odd, even):
        return call(
            functools.partial(join_kernel, groups, skip),
            "join",
            [block] * len(even),
            [VMEM] * (1 + len(even)),
            [pltpu.VMEM((2, pay_rows, width), BF16)],
        )(odd, *even)

    shifted = [seq_pair(q_short, k) for k in range(1, seqs)]
    far_all = [yz_move(q_all, dy, 0) for dy in dys[1:]]
    zero, *long_part = near(kvs[0], q_all)
    shifted, zero = lax.optimization_barrier((shifted, zero))
    own_q = jnp.concatenate(shifted)
    far_q = [yz_move(own_q, dy, 0) for dy in dys[1:]]
    (odd,) = row(odds, [], kvs[0], *long_part, own_q)
    got = seq_pair(odd, 1)
    even = row([], evens, kvs[0], *long_part, own_q)
    ins = [zero, got]
    waiting = [(0, 1, got, even)]
    for dy in dys[1:]:
        q, even = lax.optimization_barrier((far_all[dy - 1], even))
        zero, *long_part = near(kvs[dy], q)
        ins.append(yz_move(zero, -dy, 0))
        q, _ = lax.optimization_barrier((far_q[dy - 1], zero))
        odd, one = row(odds[1:], odds[:1], kvs[dy], *long_part, q)
        got = seq_pair(odd, 1)
        ins.append(yz_move(one, -dy, 1))
        even = row([], evens, kvs[dy], *long_part, q)
        waiting.append((dy, 0, got, even))
    final = []
    for at, (dy, skip, got, even) in enumerate(waiting):
        final += ins[2 * at : 2 * at + 2]
        for e, x in zip(evens, joined(skip, got, even)):
            final.append(yz_move(x, -dy, e))
    partial = call(
        functools.partial(merge_kernel, dys, seqs, groups),
        "merge",
        shape((all_rows, model)),
        [VMEM] * (1 + len(final)),
        [
            pltpu.VMEM((pairs * half, pay_rows, width), BF16),
            pltpu.VMEM((2, pay_rows, width), BF16),
            pltpu.VMEM((all_rows, width), BF16),
        ],
    )(w_cross_out, *final)

    hidden_two, partial = call(
        ffn_kernel, "ffn", (shape((all_rows, model)),) * 2, [VMEM] * 5
    )(hidden_one, partial, tp_swap(partial), w_up, w_down)

    return call(
        final_kernel,
        "final",
        (shape((requests, rows, model)), shape((1, rows, model))),
        [VMEM] * 3,
    )(hidden_two, partial, tp_swap(partial))


def solution(mesh):
    in_specs = (
        P(("req", "seq"), None, None),
        P("req", None, None),
        P(("req", "seq"), None),
        P("req", None),
        P(("req", "seq")),
        P("req"),
        P(),
        P(),
        P(("req", "seq"), None, None, "tp"),
        P("req", None, "seq", "tp"),
        P(None, None, ("req", "seq"), "tp"),
        P(None, None, "tp"),
        P("tp", None),
        P(None, "tp"),
        P("tp", None),
        P(None, "tp"),
        P("tp", None),
    )
    out_specs = (P(("req", "seq"), None, None), P("req", None, None))
    return jax.shard_map(local, mesh=mesh, in_specs=in_specs, out_specs=out_specs, check_vma=False)
```

time: 72.9 us -> 69.6 us (0.955)
  starting transfers between devices: 28.8 us -> 25.6 us
  Pallas kernels: 22.5 us -> 19.9 us
  waiting for transfers between devices: 19.7 us -> 22.3 us
    ppermute x14, waiting for transfers between devices: 6.65 us -> 11.2 us  [the longest x6 6.8 us: yz_move(): return lax.ppermute(x, both, perm)]
    ppermute x14, starting transfers between devices: 23.6 us -> 20.4 us  [the longest x8 11 us: seq_pair(): return lax.ppermute(x, 'seq', [(i, i ^ k) for i in range(seqs)])]
    pallas_call x5 -> x12, Pallas kernels: 13.9 us -> 10.8 us  [the longest x4 4.16 us: row(): call(functools.partial(row_kernel, requests, stacked, single), 'row', sta...]
    ppermute x3, waiting for transfers between devices: 13.1 us -> 11.1 us  [tp_swap(): return lax.ppermute(x, 'tp', [(i, (i + 1) % tps) for i in range(tps)])]
  transfers between devices with their start and end apart: 18 -> 18, of which waited for: 9 -> 9; matrix products, arithmetic and copies ran while one was open for 0% -> 0% of each run, Pallas kernels for 26% -> 19%
where the time goes in v3:
time: 69.6 us; the launch traced here: 69.4 us
  starting transfers between devices  25.6 us (37%)
  waiting for transfers between devices  22.3 us (32%)
  Pallas kernels  19.9 us (29%)
  between operations  1.53 us (2%)
    ppermute x3, waiting for transfers between devices, tp_swap(): return lax.ppermute(x, 'tp', [(i, (i + 1) % tps) for i in range(tps)])  11.1 us
    ppermute x8, starting transfers between devices, seq_pair(): return lax.ppermute(x, 'seq', [(i, i ^ k) for i in range(seqs)])  11 us
    ppermute x6, starting transfers between devices, yz_move(): return lax.ppermute(x, both, perm)  9.48 us
    ppermute x6, waiting for transfers between devices, yz_move(): return lax.ppermute(x, both, perm)  6.8 us
    ppermute x3, starting transfers between devices, tp_swap(): return lax.ppermute(x, 'tp', [(i, (i + 1) % tps) for i in range(tps)])  4.67 us
    ppermute x8, waiting for transfers between devices, seq_pair(): return lax.ppermute(x, 'seq', [(i, i ^ k) for i in range(seqs)])  4.42 us
    pallas_call x4, Pallas kernels, row(): call(functools.partial(row_kernel, requests, stacked, single), 'row', sta...  4.16 us
    pallas_call x1, Pallas kernels, local(): call(functools.partial(fetch_kernel, seqs, requests, dys), 'fetch', tuple...  3.41 us
  transfers between devices with their start and end apart: 18, of which 9 were waited for; matrix products, arithmetic and copies ran while one was open for 0% of the time, Pallas kernels for 19%

profile of v3, /device:TPU:0, one launch (start us, length us, event | category | flops | bytes accessed | tf_op | source)
XLA Modules:
  0.0 69.4 jit_solution(15278823882082455461)
XLA Ops:
  0.6 2.0 %first.1 = (bf16[96,512]{1,0:T(8,128)(2,1)S(1)}, bf16[96,1024]{1,0:T(8,128)(2,1)S(1)}, bf16[2,256,512]{2,1,0:T(8,128)(2,1)S(1)}, f32[96,32]{1,0:T(8,128)S(1)}) custom-call(bf16[2,32,1024]{2,1,0:T(8,128)(2,1)} %xs_hbm.1, bf16[1,32,1024]{2,1,0:T(8,128)(2,1)} %xl_hbm.1, bf16[3,1024,512]{2,1,0:T(8,128)(2,1)} %w_ref.1, bf16[1,2,256,512]{3,2,1,0:T(8,128)(2,1)} %kv_hbm.1, ...), custom_call_target="tpu_custom_call" | custom-call | flops 100000000 | bytes 1000000 | tf_op jit(solution)/shard_map/first/pallas_call | solution.py:498
  4.3 2.7 %collective-permute-start = (bf16[32,640]{1,0:T(8,128)(2,1)S(1)}, bf16[32,640]{1,0:T(8,128)(2,1)S(1)}, u32[]{:S(2)}, u32[]{:S(2)}) collective-permute-start(bf16[32,640]{1,0:T(8,128)(2,1)S(1)} %long.1.rest_0_), channel_id=1, source_target_pairs={{0,2},{2,0},{4,6},{6,4},{1,3},{3,1},{5,7},{7,5},{8,10},{10,8},{12,... | collective-permute-start | bytes 122888 | tf_op jit(solution)/shard_map/ppermute | solution.py:483
  6.9 2.6 %collective-permute-start.1 = (bf16[32,640]{1,0:T(8,128)(2,1)S(1)}, bf16[32,640]{1,0:T(8,128)(2,1)S(1)}, u32[]{:S(2)}, u32[]{:S(2)}) collective-permute-start(bf16[32,640]{1,0:T(8,128)(2,1)S(1)} %long.1.rest_0_), channel_id=1, source_target_pairs={{0,4},{2,6},{4,0},{6,2},{1,5},{3,7},{5,1},{7,3},{8,12},{10,14},{12... | collective-permute-start | bytes 122888 | tf_op jit(solution)/shard_map/ppermute | solution.py:483
  9.5 2.3 %attend.1 = (bf16[64,512]{1,0:T(8,128)(2,1)S(1)}, f32[32,512]{1,0:T(8,128)S(1)}, bf16[32,128]{1,0:T(8,128)(2,1)S(1)}) custom-call(bf16[96,512]{1,0:T(8,128)(2,1)S(1)} %get-tuple-element.46.q_ref, bf16[96,1024]{1,0:T(8,128)(2,1)S(1)} %get-tuple-element.44.x_ref, bf16[3,1024,512]{2,1,0:T(8,128)(2,1)S(1)} %copy-done.2, bf16[2,2,512,512]{3,2,1,0:T(8,128)(2,1)S(1)} %copy-done.6, ...), custom_call_target="tpu_custom_call" | custom-call | flops 4000000000 | bytes 1000000 | tf_op jit(solution)/shard_map/attend/pallas_call | solution.py:524
  11.9 0.8 %collective-permute-done.1.rest_2_ = bf16[32,640]{1,0:T(8,128)(2,1)S(1)} collective-permute-done((bf16[32,640]{1,0:T(8,128)(2,1)S(1)}, bf16[32,640]{1,0:T(8,128)(2,1)S(1)}, u32[]{:S(2)}, u32[]{:S(2)}) %collective-permute-start.1) | collective-permute-done | bytes 40992 | tf_op jit(solution)/shard_map/ppermute | solution.py:483
  12.7 2.6 %collective-permute-done.2.rest_3_ = bf16[32,640]{1,0:T(8,128)(2,1)S(1)} collective-permute-done((bf16[32,640]{1,0:T(8,128)(2,1)S(1)}, bf16[32,640]{1,0:T(8,128)(2,1)S(1)}, u32[]{:S(2)}, u32[]{:S(2)}) %collective-permute-start.2) | collective-permute-done | bytes 40992 | tf_op jit(solution)/shard_map/ppermute | solution.py:483
  15.8 1.6 %collective-permute-start.3 = (bf16[96,1024]{1,0:T(8,128)(2,1)S(1)}, bf16[96,1024]{1,0:T(8,128)(2,1)S(1)}, u32[]{:S(2)}, u32[]{:S(2)}) collective-permute-start(bf16[96,1024]{1,0:T(8,128)(2,1)S(1)} %output.1.a_ref), channel_id=1, source_target_pairs={{0,1},{1,0},{2,3},{3,2},{4,5},{5,4},{6,7},{7,6},{8,9},{9,8},{10,11... | collective-permute-start | bytes 589832 | tf_op jit(solution)/shard_map/ppermute | solution.py:495
  17.4 3.4 %fetch.1 = (bf16[9,2,128,512]{3,2,1,0:T(8,128)(2,1)S(1)}, bf16[9,2,128,512]{3,2,1,0:T(8,128)(2,1)S(1)}) custom-call(s32[32]{0:T(128)S(1)} %copy-done.7, s32[4]{0:T(128)S(1)} %copy-done.8, bf16[2,32,64,512]{3,2,1,0:T(8,128)(2,1)} %own_ref, bf16[2,32,64,512]{3,2,1,0:T(8,128)(2,1)S(1)} %collective-permute-done.4.other_ref), custom_call_target="tpu_custom_call" | custom-call | flops 4000000000 | bytes 1000000 | tf_op jit(solution)/shard_map/fetch/pallas_call | solution.py:544
  20.8 0.7 %collective-permute-done.3.b_ref = bf16[96,1024]{1,0:T(8,128)(2,1)S(1)} collective-permute-done((bf16[96,1024]{1,0:T(8,128)(2,1)S(1)}, bf16[96,1024]{1,0:T(8,128)(2,1)S(1)}, u32[]{:S(2)}, u32[]{:S(2)}) %collective-permute-start.3) | collective-permute-done | bytes 196640 | tf_op jit(solution)/shard_map/ppermute | solution.py:495
  22.1 1.9 %collective-permute-start.6 = (bf16[64,512]{1,0:T(8,128)(2,1)S(1)}, bf16[64,512]{1,0:T(8,128)(2,1)S(1)}, u32[]{:S(2)}, u32[]{:S(2)}) collective-permute-start(bf16[64,512]{1,0:T(8,128)(2,1)S(1)} %get-tuple-element.66), channel_id=1, source_target_pairs={{0,4},{2,6},{4,0},{6,2},{1,5},{3,7},{5,1},{7,3},{8,12},{10,14},{12... | collective-permute-start | bytes 196616 | tf_op jit(solution)/shard_map/ppermute | solution.py:483
  24.0 2.5 %collective-permute-start.7 = (bf16[64,512]{1,0:T(8,128)(2,1)S(1)}, bf16[64,512]{1,0:T(8,128)(2,1)S(1)}, u32[]{:S(2)}, u32[]{:S(2)}) collective-permute-start(bf16[64,512]{1,0:T(8,128)(2,1)S(1)} %get-tuple-element.66), channel_id=1, source_target_pairs={{0,6},{2,4},{4,2},{6,0},{1,7},{3,5},{5,3},{7,1},{8,14},{10,12},{12... | collective-permute-start | bytes 196616 | tf_op jit(solution)/shard_map/ppermute | solution.py:483
  26.5 1.5 %collective-permute-start.10 = (bf16[96,512]{1,0:T(8,128)(2,1)S(1)}, bf16[96,512]{1,0:T(8,128)(2,1)S(1)}, u32[]{:S(2)}, u32[]{:S(2)}) collective-permute-start(bf16[96,512]{1,0:T(8,128)(2,1)S(1)} %get-tuple-element.68.q_ref), channel_id=1, source_target_pairs={{0,16},{2,18},{4,20},{6,22},{8,24},{10,26},{12,28},{14,30},{16,0},... | collective-permute-start | bytes 294920 | tf_op jit(solution)/shard_map/ppermute | solution.py:492
  28.0 1.0 %near.2 = (bf16[104,512]{1,0:T(8,128)(2,1)S(1)}, bf16[32,512]{1,0:T(8,128)(2,1)S(1)}, f32[32,128]{1,0:T(8,128)S(1)}) custom-call(bf16[9,2,128,512]{3,2,1,0:T(8,128)(2,1)S(1)} %get-tuple-element.67.kv_ref, bf16[96,512]{1,0:T(8,128)(2,1)S(1)} %get-tuple-element.68.q_ref), custom_call_target="tpu_custom_call" | custom-call | flops 1000000000 | bytes 1000000 | tf_op jit(solution)/shard_map/near/pallas_call | solution.py:567
  29.1 1.0 %collective-permute-done.7 = bf16[64,512]{1,0:T(8,128)(2,1)S(1)} collective-permute-done((bf16[64,512]{1,0:T(8,128)(2,1)S(1)}, bf16[64,512]{1,0:T(8,128)(2,1)S(1)}, u32[]{:S(2)}, u32[]{:S(2)}) %collective-permute-start.7) | collective-permute-done | bytes 65568 | tf_op jit(solution)/shard_map/ppermute | solution.py:483
  30.1 1.6 %collective-permute-start.12 = (bf16[192,512]{1,0:T(8,128)(2,1)S(1)}, bf16[192,512]{1,0:T(8,128)(2,1)S(1)}, u32[]{:S(2)}, u32[]{:S(2)}) collective-permute-start(bf16[192,512]{1,0:T(8,128)(2,1)S(1)} %constant_dynamic-update-slice_fusion.q_ref), channel_id=1, source_target_pairs={{0,16},{2,18},{4,20},{6,22},{8,24},{10,26},{12,28},{14,30},{16,0},... | collective-permute-start | bytes 589832 | tf_op jit(solution)/shard_map/ppermute | solution.py:492
  31.7 1.3 %row.4 = bf16[2,104,512]{2,1,0:T(8,128)(2,1)S(1)} custom-call(bf16[9,2,128,512]{3,2,1,0:T(8,128)(2,1)S(1)} %get-tuple-element.67.kv_ref, bf16[32,512]{1,0:T(8,128)(2,1)S(1)} %get-tuple-element.71.o_ref, f32[32,128]{1,0:T(8,128)S(1)} %get-tuple-element.72.stat_ref, bf16[192,512]{1,0:T(8,128)(2,1)S(1)} %constant_dynamic-update-slice_fusion.q_ref), custom_call_target="tpu_custom_call" | custom-call | flops 1000000000 | bytes 1000000 | tf_op jit(solution)/shard_map/row/pallas_call | solution.py:577
  33.9 1.0 %near.3 = (bf16[104,512]{1,0:T(8,128)(2,1)S(1)}, bf16[32,512]{1,0:T(8,128)(2,1)S(1)}, f32[32,128]{1,0:T(8,128)S(1)}) custom-call(bf16[9,2,128,512]{3,2,1,0:T(8,128)(2,1)S(1)} %get-tuple-element.76.kv_ref, bf16[96,512]{1,0:T(8,128)(2,1)S(1)} %collective-permute-done.10.q_ref), custom_call_target="tpu_custom_call" | custom-call | flops 1000000000 | bytes 1000000 | tf_op jit(solution)/shard_map/near/pallas_call | solution.py:567
  35.0 0.9 %collective-permute-done.12.q_ref = bf16[192,512]{1,0:T(8,128)(2,1)S(1)} collective-permute-done((bf16[192,512]{1,0:T(8,128)(2,1)S(1)}, bf16[192,512]{1,0:T(8,128)(2,1)S(1)}, u32[]{:S(2)}, u32[]{:S(2)}) %collective-permute-start.12) | collective-permute-done | bytes 196640 | tf_op jit(solution)/shard_map/ppermute | solution.py:492
  35.9 1.3 %row.6 = (bf16[1,104,512]{2,1,0:T(8,128)(2,1)S(1)}, bf16[104,512]{1,0:T(8,128)(2,1)S(1)}) custom-call(bf16[9,2,128,512]{3,2,1,0:T(8,128)(2,1)S(1)} %get-tuple-element.76.kv_ref, bf16[32,512]{1,0:T(8,128)(2,1)S(1)} %get-tuple-element.79.o_ref, f32[32,128]{1,0:T(8,128)S(1)} %get-tuple-element.80.stat_ref, bf16[192,512]{1,0:T(8,128)(2,1)S(1)} %collective-permute-done.12.q_ref), custom_call_target="tpu_custom_call" | custom-call | flops 1000000000 | bytes 1000000 | tf_op jit(solution)/shard_map/row/pallas_call | solution.py:577
  37.2 1.2 %collective-permute-start.14 = (bf16[1,104,512]{2,1,0:T(8,128)(2,1)S(1)}, bf16[1,104,512]{2,1,0:T(8,128)(2,1)S(1)}, u32[]{:S(2)}, u32[]{:S(2)}) collective-permute-start(bf16[1,104,512]{2,1,0:T(8,128)(2,1)S(1)} %get-tuple-element.83), channel_id=1, source_target_pairs={{0,2},{2,0},{4,6},{6,4},{1,3},{3,1},{5,7},{7,5},{8,10},{10,8},{12,... | collective-permute-start | bytes 319496 | tf_op jit(solution)/shard_map/ppermute | solution.py:483
  38.9 1.8 %collective-permute-start.13 = (bf16[104,512]{1,0:T(8,128)(2,1)S(1)}, bf16[104,512]{1,0:T(8,128)(2,1)S(1)}, u32[]{:S(2)}, u32[]{:S(2)}) collective-permute-start(bf16[104,512]{1,0:T(8,128)(2,1)S(1)} %get-tuple-element.82), channel_id=1, source_target_pairs={{0,18},{2,16},{4,22},{6,20},{8,26},{10,24},{12,30},{14,28},{16,2},... | collective-permute-start | bytes 319496 | tf_op jit(solution)/shard_map/ppermute | solution.py:492
  41.8 2.2 %collective-permute-start.9 = (bf16[104,512]{1,0:T(8,128)(2,1)S(1)}, bf16[104,512]{1,0:T(8,128)(2,1)S(1)}, u32[]{:S(2)}, u32[]{:S(2)}) collective-permute-start(bf16[104,512]{1,0:T(8,128)(2,1)S(1)} %join.2), channel_id=1, source_target_pairs={{0,4},{2,6},{4,0},{6,2},{8,12},{10,14},{12,8},{14,10},{16,20},{18,... | collective-permute-start | bytes 319496 | tf_op jit(solution)/shard_map/ppermute | solution.py:492
  44.3 1.8 %collective-permute-start.15 = (bf16[104,512]{1,0:T(8,128)(2,1)S(1)}, bf16[104,512]{1,0:T(8,128)(2,1)S(1)}, u32[]{:S(2)}, u32[]{:S(2)}) collective-permute-start(bf16[104,512]{1,0:T(8,128)(2,1)S(1)} %join.3), channel_id=1, source_target_pairs={{0,20},{2,22},{4,16},{6,18},{8,28},{10,30},{12,24},{14,26},{16,4},... | collective-permute-start | bytes 319496 | tf_op jit(solution)/shard_map/ppermute | solution.py:492
  46.1 2.5 %collective-permute-done.9.rest_2_ = bf16[104,512]{1,0:T(8,128)(2,1)S(1)} collective-permute-done((bf16[104,512]{1,0:T(8,128)(2,1)S(1)}, bf16[104,512]{1,0:T(8,128)(2,1)S(1)}, u32[]{:S(2)}, u32[]{:S(2)}) %collective-permute-start.9) | collective-permute-done | bytes 106528 | tf_op jit(solution)/shard_map/ppermute | solution.py:492
  48.6 3.4 %collective-permute-done.15.rest_5_ = bf16[104,512]{1,0:T(8,128)(2,1)S(1)} collective-permute-done((bf16[104,512]{1,0:T(8,128)(2,1)S(1)}, bf16[104,512]{1,0:T(8,128)(2,1)S(1)}, u32[]{:S(2)}, u32[]{:S(2)}) %collective-permute-start.15) | collective-permute-done | bytes 106528 | tf_op jit(solution)/shard_map/ppermute | solution.py:492
  52.0 1.0 %merge.1.a_ref = bf16[96,1024]{1,0:T(8,128)(2,1)S(1)} custom-call(bf16[512,1024]{1,0:T(8,128)(2,1)S(1)} %copy-done.5, bf16[104,512]{1,0:T(8,128)(2,1)S(1)} %get-tuple-element.70.rest_0_, bf16[2,104,512]{2,1,0:T(8,128)(2,1)S(1)} %collective-permute-done.8.odd_ref.rest_1_, bf16[104,512]{1,0:T(8,128)(2,1)S(1)} %collective-permute-done.9.rest_2_, ...), custom_call_target="tpu_custom_call" | custom-call | flops 100000000 | bytes 1000000 | tf_op jit(solution)/shard_map/merge/pallas_call | solution.py:620
  53.1 1.6 %collective-permute-start.16 = (bf16[96,1024]{1,0:T(8,128)(2,1)S(1)}, bf16[96,1024]{1,0:T(8,128)(2,1)S(1)}, u32[]{:S(2)}, u32[]{:S(2)}) collective-permute-start(bf16[96,1024]{1,0:T(8,128)(2,1)S(1)} %merge.1.a_ref), channel_id=1, source_target_pairs={{0,1},{1,0},{2,3},{3,2},{4,5},{5,4},{6,7},{7,6},{8,9},{9,8},{10,11... | collective-permute-start | bytes 589832 | tf_op jit(solution)/shard_map/ppermute | solution.py:495
  54.6 6.2 %collective-permute-done.16.b_ref = bf16[96,1024]{1,0:T(8,128)(2,1)S(1)} collective-permute-done((bf16[96,1024]{1,0:T(8,128)(2,1)S(1)}, bf16[96,1024]{1,0:T(8,128)(2,1)S(1)}, u32[]{:S(2)}, u32[]{:S(2)}) %collective-permute-start.16) | collective-permute-done | bytes 196640 | tf_op jit(solution)/shard_map/ppermute | solution.py:495
  60.8 2.0 %ffn.1 = (bf16[96,1024]{1,0:T(8,128)(2,1)S(1)}, bf16[96,1024]{1,0:T(8,128)(2,1)S(1)}) custom-call(bf16[96,1024]{1,0:T(8,128)(2,1)S(1)} %get-tuple-element.65.h_ref, bf16[96,1024]{1,0:T(8,128)(2,1)S(1)} %merge.1.a_ref, bf16[96,1024]{1,0:T(8,128)(2,1)S(1)} %collective-permute-done.16.b_ref, bf16[1024,2048]{1,0:T(8,128)(2,1)S(1)} %copy-done, ...), custom_call_target="tpu_custom_call" | custom-call | flops 100000000 | bytes 1000000 | tf_op jit(solution)/shard_map/ffn/pallas_call | solution.py:632
  62.8 1.6 %collective-permute-start.17 = (bf16[96,1024]{1,0:T(8,128)(2,1)S(1)}, bf16[96,1024]{1,0:T(8,128)(2,1)S(1)}, u32[]{:S(2)}, u32[]{:S(2)}) collective-permute-start(bf16[96,1024]{1,0:T(8,128)(2,1)S(1)} %get-tuple-element.85.a_ref), channel_id=1, source_target_pairs={{0,1},{1,0},{2,3},{3,2},{4,5},{5,4},{6,7},{7,6},{8,9},{9,8},{10,11... | collective-permute-start | bytes 589832 | tf_op jit(solution)/shard_map/ppermute | solution.py:495
  64.4 4.2 %collective-permute-done.17.b_ref = bf16[96,1024]{1,0:T(8,128)(2,1)S(1)} collective-permute-done((bf16[96,1024]{1,0:T(8,128)(2,1)S(1)}, bf16[96,1024]{1,0:T(8,128)(2,1)S(1)}, u32[]{:S(2)}, u32[]{:S(2)}) %collective-permute-start.17) | collective-permute-done | bytes 196640 | tf_op jit(solution)/shard_map/ppermute | solution.py:495
  68.5 0.9 %final.1 = (bf16[2,32,1024]{2,1,0:T(8,128)(2,1)}, bf16[1,32,1024]{2,1,0:T(8,128)(2,1)}) custom-call(bf16[96,1024]{1,0:T(8,128)(2,1)S(1)} %get-tuple-element.84.h_ref, bf16[96,1024]{1,0:T(8,128)(2,1)S(1)} %get-tuple-element.85.a_ref, bf16[96,1024]{1,0:T(8,128)(2,1)S(1)} %collective-permute-done.17.b_ref), custom_call_target="tpu_custom_call" | custom-call | flops 100000000 | bytes 1000000 | tf_op jit(solution)/shard_map/final/pallas_call | solution.py:636
  (43 shorter events, 4.7 us)
Async XLA Ops:
  2.6 14.8 %collective-permute-start.4 = (bf16[2,32,64,512]{3,2,1,0:T(8,128)(2,1)}, bf16[2,32,64,512]{3,2,1,0:T(8,128)(2,1)S(1)}, u32[]{:S(2)}, u32[]{:S(2)}) collective-permute-start(bf16[2,32,64,512]{3,2,1,0:T(8,128)(2,1)} %own_ref), channel_id=1, source_target_pairs={{0,8},{8,0},{16,24},{24,16},{1,9},{9,1},{17,25},{25,17},{2,10},{10... | collective-permute-start | bytes 12582920 | tf_op jit(solution)/shard_map/ppermute | solution.py:522
  3.8 5.7 %copy-start.2 = (bf16[3,1024,512]{2,1,0:T(8,128)(2,1)S(1)}, bf16[3,1024,512]{2,1,0:T(8,128)(2,1)}, u32[]{:S(2)}) copy-start(bf16[3,1024,512]{2,1,0:T(8,128)(2,1)} %w_ref.1) | copy-start | bytes 9437188
  3.8 5.7 %copy-start.6 = (bf16[2,2,512,512]{3,2,1,0:T(8,128)(2,1)S(1)}, bf16[2,2,512,512]{3,2,1,0:T(8,128)(2,1)}, u32[]{:S(2)}) copy-start(bf16[2,2,512,512]{3,2,1,0:T(8,128)(2,1)} %skv_ref) | copy-start | bytes 6291460
  4.3 7.6 %collective-permute-start = (bf16[32,640]{1,0:T(8,128)(2,1)S(1)}, bf16[32,640]{1,0:T(8,128)(2,1)S(1)}, u32[]{:S(2)}, u32[]{:S(2)}) collective-permute-start(bf16[32,640]{1,0:T(8,128)(2,1)S(1)} %long.1.rest_0_), channel_id=1, source_target_pairs={{0,2},{2,0},{4,6},{6,4},{1,3},{3,1},{5,7},{7,5},{8,10},{10,8},{12,... | collective-permute-start | bytes 122888 | tf_op jit(solution)/shard_map/ppermute | solution.py:483
  6.9 5.8 %collective-permute-start.1 = (bf16[32,640]{1,0:T(8,128)(2,1)S(1)}, bf16[32,640]{1,0:T(8,128)(2,1)S(1)}, u32[]{:S(2)}, u32[]{:S(2)}) collective-permute-start(bf16[32,640]{1,0:T(8,128)(2,1)S(1)} %long.1.rest_0_), channel_id=1, source_target_pairs={{0,4},{2,6},{4,0},{6,2},{1,5},{3,7},{5,1},{7,3},{8,12},{10,14},{12... | collective-permute-start | bytes 122888 | tf_op jit(solution)/shard_map/ppermute | solution.py:483
  9.5 5.8 %collective-permute-start.2 = (bf16[32,640]{1,0:T(8,128)(2,1)S(1)}, bf16[32,640]{1,0:T(8,128)(2,1)S(1)}, u32[]{:S(2)}, u32[]{:S(2)}) collective-permute-start(bf16[32,640]{1,0:T(8,128)(2,1)S(1)} %long.1.rest_0_), channel_id=1, source_target_pairs={{0,6},{2,4},{4,2},{6,0},{1,7},{3,5},{5,3},{7,1},{8,14},{10,12},{12... | collective-permute-start | bytes 122888 | tf_op jit(solution)/shard_map/ppermute | solution.py:483
  9.5 5.8 %copy-start.3 = (bf16[512,1024]{1,0:T(8,128)(2,1)S(1)}, bf16[512,1024]{1,0:T(8,128)(2,1)}, u32[]{:S(2)}) copy-start(bf16[512,1024]{1,0:T(8,128)(2,1)} %wo_ref) | copy-start | bytes 3145732
  9.5 7.8 %copy-start.7 = (s32[32]{0:T(128)S(1)}, s32[32]{0:T(128)}, u32[]{:S(2)}) copy-start(s32[32]{0:T(128)} %doc_ref) | copy-start | bytes 388
  9.5 7.8 %copy-start.8 = (s32[4]{0:T(128)S(1)}, s32[4]{0:T(128)}, u32[]{:S(2)}) copy-start(s32[4]{0:T(128)} %long_ref.1) | copy-start | bytes 52
  15.8 5.8 %copy-start.4 = (bf16[1024,512]{1,0:T(8,128)(2,1)S(1)}, bf16[1024,512]{1,0:T(8,128)(2,1)}, u32[]{:S(2)}) copy-start(bf16[1024,512]{1,0:T(8,128)(2,1)} %w_ref.2) | copy-start | bytes 3145732
  15.8 5.7 %collective-permute-start.3 = (bf16[96,1024]{1,0:T(8,128)(2,1)S(1)}, bf16[96,1024]{1,0:T(8,128)(2,1)S(1)}, u32[]{:S(2)}, u32[]{:S(2)}) collective-permute-start(bf16[96,1024]{1,0:T(8,128)(2,1)S(1)} %output.1.a_ref), channel_id=1, source_target_pairs={{0,1},{1,0},{2,3},{3,2},{4,5},{5,4},{6,7},{7,6},{8,9},{9,8},{10,11... | collective-permute-start | bytes 589832 | tf_op jit(solution)/shard_map/ppermute | solution.py:495
  22.0 7.0 %collective-permute-start.5 = (bf16[64,512]{1,0:T(8,128)(2,1)S(1)}, bf16[64,512]{1,0:T(8,128)(2,1)S(1)}, u32[]{:S(2)}, u32[]{:S(2)}) collective-permute-start(bf16[64,512]{1,0:T(8,128)(2,1)S(1)} %get-tuple-element.66), channel_id=1, source_target_pairs={{0,2},{2,0},{4,6},{6,4},{1,3},{3,1},{5,7},{7,5},{8,10},{10,8},{12,... | collective-permute-start | bytes 196616 | tf_op jit(solution)/shard_map/ppermute | solution.py:483
  22.1 7.0 %collective-permute-start.6 = (bf16[64,512]{1,0:T(8,128)(2,1)S(1)}, bf16[64,512]{1,0:T(8,128)(2,1)S(1)}, u32[]{:S(2)}, u32[]{:S(2)}) collective-permute-start(bf16[64,512]{1,0:T(8,128)(2,1)S(1)} %get-tuple-element.66), channel_id=1, source_target_pairs={{0,4},{2,6},{4,0},{6,2},{1,5},{3,7},{5,1},{7,3},{8,12},{10,14},{12... | collective-permute-start | bytes 196616 | tf_op jit(solution)/shard_map/ppermute | solution.py:483
  24.0 6.1 %collective-permute-start.7 = (bf16[64,512]{1,0:T(8,128)(2,1)S(1)}, bf16[64,512]{1,0:T(8,128)(2,1)S(1)}, u32[]{:S(2)}, u32[]{:S(2)}) collective-permute-start(bf16[64,512]{1,0:T(8,128)(2,1)S(1)} %get-tuple-element.66), channel_id=1, source_target_pairs={{0,6},{2,4},{4,2},{6,0},{1,7},{3,5},{5,3},{7,1},{8,14},{10,12},{12... | collective-permute-start | bytes 196616 | tf_op jit(solution)/shard_map/ppermute | solution.py:483
  26.5 7.4 %collective-permute-start.10 = (bf16[96,512]{1,0:T(8,128)(2,1)S(1)}, bf16[96,512]{1,0:T(8,128)(2,1)S(1)}, u32[]{:S(2)}, u32[]{:S(2)}) collective-permute-start(bf16[96,512]{1,0:T(8,128)(2,1)S(1)} %get-tuple-element.68.q_ref), channel_id=1, source_target_pairs={{0,16},{2,18},{4,20},{6,22},{8,24},{10,26},{12,28},{14,30},{16,0},... | collective-permute-start | bytes 294920 | tf_op jit(solution)/shard_map/ppermute | solution.py:492
  30.1 5.7 %collective-permute-start.12 = (bf16[192,512]{1,0:T(8,128)(2,1)S(1)}, bf16[192,512]{1,0:T(8,128)(2,1)S(1)}, u32[]{:S(2)}, u32[]{:S(2)}) collective-permute-start(bf16[192,512]{1,0:T(8,128)(2,1)S(1)} %constant_dynamic-update-slice_fusion.q_ref), channel_id=1, source_target_pairs={{0,16},{2,18},{4,20},{6,22},{8,24},{10,26},{12,28},{14,30},{16,0},... | collective-permute-start | bytes 589832 | tf_op jit(solution)/shard_map/ppermute | solution.py:492
  33.1 8.4 %collective-permute-start.8 = (bf16[2,104,512]{2,1,0:T(8,128)(2,1)S(1)}, bf16[2,104,512]{2,1,0:T(8,128)(2,1)S(1)}, u32[]{:S(2)}, u32[]{:S(2)}) collective-permute-start(bf16[2,104,512]{2,1,0:T(8,128)(2,1)S(1)} %row.4), channel_id=1, source_target_pairs={{0,2},{2,0},{4,6},{6,4},{1,3},{3,1},{5,7},{7,5},{8,10},{10,8},{12,... | collective-permute-start | bytes 638984 | tf_op jit(solution)/shard_map/ppermute | solution.py:483
  34.9 17.1 %copy-start.5 = (bf16[512,1024]{1,0:T(8,128)(2,1)S(1)}, bf16[512,1024]{1,0:T(8,128)(2,1)}, u32[]{:S(2)}) copy-start(bf16[512,1024]{1,0:T(8,128)(2,1)} %w_ref.3) | copy-start | bytes 3145732
  35.9 25.0 %copy-start = (bf16[1024,2048]{1,0:T(8,128)(2,1)S(1)}, bf16[1024,2048]{1,0:T(8,128)(2,1)}, u32[]{:S(2)}) copy-start(bf16[1024,2048]{1,0:T(8,128)(2,1)} %up_ref.1) | copy-start | bytes 12582916
  35.9 25.0 %copy-start.1 = (bf16[2048,1024]{1,0:T(8,128)(2,1)S(1)}, bf16[2048,1024]{1,0:T(8,128)(2,1)}, u32[]{:S(2)}) copy-start(bf16[2048,1024]{1,0:T(8,128)(2,1)} %down_ref.1) | copy-start | bytes 12582916
  37.2 6.8 %collective-permute-start.14 = (bf16[1,104,512]{2,1,0:T(8,128)(2,1)S(1)}, bf16[1,104,512]{2,1,0:T(8,128)(2,1)S(1)}, u32[]{:S(2)}, u32[]{:S(2)}) collective-permute-start(bf16[1,104,512]{2,1,0:T(8,128)(2,1)S(1)} %get-tuple-element.83), channel_id=1, source_target_pairs={{0,2},{2,0},{4,6},{6,4},{1,3},{3,1},{5,7},{7,5},{8,10},{10,8},{12,... | collective-permute-start | bytes 319496 | tf_op jit(solution)/shard_map/ppermute | solution.py:483
  38.4 7.7 %collective-permute-start.11 = (bf16[104,512]{1,0:T(8,128)(2,1)S(1)}, bf16[104,512]{1,0:T(8,128)(2,1)S(1)}, u32[]{:S(2)}, u32[]{:S(2)}) collective-permute-start(bf16[104,512]{1,0:T(8,128)(2,1)S(1)} %get-tuple-element.78), channel_id=1, source_target_pairs={{0,16},{2,18},{4,20},{6,22},{8,24},{10,26},{12,28},{14,30},{16,0},... | collective-permute-start | bytes 319496 | tf_op jit(solution)/shard_map/ppermute | solution.py:492
  38.9 7.2 %collective-permute-start.13 = (bf16[104,512]{1,0:T(8,128)(2,1)S(1)}, bf16[104,512]{1,0:T(8,128)(2,1)S(1)}, u32[]{:S(2)}, u32[]{:S(2)}) collective-permute-start(bf16[104,512]{1,0:T(8,128)(2,1)S(1)} %get-tuple-element.82), channel_id=1, source_target_pairs={{0,18},{2,16},{4,22},{6,20},{8,26},{10,24},{12,30},{14,28},{16,2},... | collective-permute-start | bytes 319496 | tf_op jit(solution)/shard_map/ppermute | solution.py:492
  41.8 6.8 %collective-permute-start.9 = (bf16[104,512]{1,0:T(8,128)(2,1)S(1)}, bf16[104,512]{1,0:T(8,128)(2,1)S(1)}, u32[]{:S(2)}, u32[]{:S(2)}) collective-permute-start(bf16[104,512]{1,0:T(8,128)(2,1)S(1)} %join.2), channel_id=1, source_target_pairs={{0,4},{2,6},{4,0},{6,2},{8,12},{10,14},{12,8},{14,10},{16,20},{18,... | collective-permute-start | bytes 319496 | tf_op jit(solution)/shard_map/ppermute | solution.py:492
  44.3 7.7 %collective-permute-start.15 = (bf16[104,512]{1,0:T(8,128)(2,1)S(1)}, bf16[104,512]{1,0:T(8,128)(2,1)S(1)}, u32[]{:S(2)}, u32[]{:S(2)}) collective-permute-start(bf16[104,512]{1,0:T(8,128)(2,1)S(1)} %join.3), channel_id=1, source_target_pairs={{0,20},{2,22},{4,16},{6,18},{8,28},{10,30},{12,24},{14,26},{16,4},... | collective-permute-start | bytes 319496 | tf_op jit(solution)/shard_map/ppermute | solution.py:492
  53.1 7.7 %collective-permute-start.16 = (bf16[96,1024]{1,0:T(8,128)(2,1)S(1)}, bf16[96,1024]{1,0:T(8,128)(2,1)S(1)}, u32[]{:S(2)}, u32[]{:S(2)}) collective-permute-start(bf16[96,1024]{1,0:T(8,128)(2,1)S(1)} %merge.1.a_ref), channel_id=1, source_target_pairs={{0,1},{1,0},{2,3},{3,2},{4,5},{5,4},{6,7},{7,6},{8,9},{9,8},{10,11... | collective-permute-start | bytes 589832 | tf_op jit(solution)/shard_map/ppermute | solution.py:495
  62.8 5.7 %collective-permute-start.17 = (bf16[96,1024]{1,0:T(8,128)(2,1)S(1)}, bf16[96,1024]{1,0:T(8,128)(2,1)S(1)}, u32[]{:S(2)}, u32[]{:S(2)}) collective-permute-start(bf16[96,1024]{1,0:T(8,128)(2,1)S(1)} %get-tuple-element.85.a_ref), channel_id=1, source_target_pairs={{0,1},{1,0},{2,3},{3,2},{4,5},{5,4},{6,7},{7,6},{8,9},{9,8},{10,11... | collective-permute-start | bytes 589832 | tf_op jit(solution)/shard_map/ppermute | solution.py:495

commit v4 on v3

--- a/solution.py
+++ b/solution.py
@@ -12,6 +12,9 @@
 CORES = 2
 PIECES = 3
 SLOTS = 4
+CHUNK = 1024
+OWN = 10**6
+FAR = 10**10
 MASKED = -1e30
 EPS = 1e-05
 F32 = jnp.float32
@@ -329,11 +332,12 @@
 
 
 def row_kernel(requests, stacked, single, kv_ref, o_ref, stat_ref, q_ref, *outs):
+    ks = stacked + single
     rows, width = o_ref.shape
     heads = width // HD
     targets = [outs[0].at[i] for i in range(len(stacked))]
     targets += outs[1 if stacked else 0 :]
-    for k, target in zip(stacked + single, targets):
+    for k, target in zip(ks, targets):
         parts = []
         for j in range(requests):
             row = ((k - 1) * requests + j) * rows
@@ -381,13 +385,17 @@
     yed = lax.axis_index("req") // CORES
     zed = lax.axis_index("seq")
     odd_z = zed & 1
-    per = half + 1
-    for at, dy in enumerate(dys):
-        zero, one, *far = ins[at * per : (at + 1) * per]
+    for dy in dys:
         base = lax.rem(yed + dy, pairs) * half
-        two[odd_z] = zero[...]
-        two[1 - odd_z] = one[...] if dy else one[0]
-        join(two, pays.at[base + zed // 2], groups, heads)
+        if dy:
+            zero, one, *far = ins[: half + 1]
+            two[odd_z] = zero[...]
+            two[1 - odd_z] = one[...]
+            join(two, pays.at[base + zed // 2], groups, heads)
+        else:
+            zero, *far = ins[:half]
+            pays[base + zed // 2] = zero[...]
+        ins = ins[half + 1 if dy else half :]
         for e, ref in enumerate(far, 1):
             pays[base + (zed ^ (2 * e)) // 2] = ref[...]
     total = len(dys) * half
@@ -410,9 +418,9 @@
     h2 = normalize(total).astype(BF16)
     h2_ref[...] = h2
     acc = None
-    for at in range(0, up_ref.shape[1], 512):
-        act = gelu(dot(h2, up_ref[:, at : at + 512])).astype(BF16)
-        part = dot(act, down_ref[at : at + 512, :])
+    for at in range(0, up_ref.shape[1], CHUNK):
+        act = gelu(dot(h2, up_ref[:, at : at + CHUNK])).astype(BF16)
+        part = dot(act, down_ref[at : at + CHUNK, :])
         acc = part if acc is None else acc + part
     out_ref[...] = acc.astype(BF16)
 
@@ -563,60 +571,58 @@
     half = seqs // 2
     odds, evens = list(range(1, seqs, 2)), list(range(2, seqs, 2))
 
-    def near(kv, q):
+    def near(kv, q, flops):
         return call(
             functools.partial(near_kernel, requests),
             "near",
             (block, shape((rows, width)), shape((rows, LANES), F32)),
             [VMEM] * 2,
-            flops=10**9,
+            flops=flops,
         )(kv, q)
 
-    def row(stacked, single, kv, long_o, long_stats, q):
+    def row(stacked, single, kv, long_o, long_stats, q, flops):
         stack = [shape((len(stacked), pay_rows, width))] if stacked else []
         return call(
             functools.partial(row_kernel, requests, stacked, single),
             "row",
             stack + [block] * len(single),
             [VMEM] * 4,
-            flops=10**9,
+            flops=flops,
         )(kv, long_o, long_stats, q)
 
-    def joined(skip, odd, even):
+    def joined(skip, odd, even, flops):
         return call(
             functools.partial(join_kernel, groups, skip),
             "join",
             [block] * len(even),
             [VMEM] * (1 + len(even)),
             [pltpu.VMEM((2, pay_rows, width), BF16)],
+            flops=flops,
         )(odd, *even)
 
+    far_all = [yz_move(q_all, dy, 0) for dy in dys[1:]]
     shifted = [seq_pair(q_short, k) for k in range(1, seqs)]
-    far_all = [yz_move(q_all, dy, 0) for dy in dys[1:]]
-    zero, *long_part = near(kvs[0], q_all)
+    zero, *long_part = near(kvs[0], q_all, 10**9)
     shifted, zero = lax.optimization_barrier((shifted, zero))
     own_q = jnp.concatenate(shifted)
     far_q = [yz_move(own_q, dy, 0) for dy in dys[1:]]
-    (odd,) = row(odds, [], kvs[0], *long_part, own_q)
+    (odd,) = row(odds, [], kvs[0], *long_part, own_q, OWN)
     got = seq_pair(odd, 1)
-    even = row([], evens, kvs[0], *long_part, own_q)
-    ins = [zero, got]
-    waiting = [(0, 1, got, even)]
+    even = row([], evens, kvs[0], *long_part, own_q, OWN)
+    first, *rest = joined(0, got, [zero, *even], OWN)
+    own = [first] + [yz_move(x, 0, e) for e, x in zip(evens, rest)]
+    final = []
     for dy in dys[1:]:
         q, even = lax.optimization_barrier((far_all[dy - 1], even))
-        zero, *long_part = near(kvs[dy], q)
-        ins.append(yz_move(zero, -dy, 0))
-        q, _ = lax.optimization_barrier((far_q[dy - 1], zero))
-        odd, one = row(odds[1:], odds[:1], kvs[dy], *long_part, q)
+        zero, *long_part = near(kvs[dy], q, FAR)
+        qs, _ = lax.optimization_barrier((far_q[dy - 1], zero))
+        odd, one = row(odds[1:], odds[:1], kvs[dy], *long_part, qs, FAR)
         got = seq_pair(odd, 1)
-        ins.append(yz_move(one, -dy, 1))
-        even = row([], evens, kvs[dy], *long_part, q)
-        waiting.append((dy, 0, got, even))
-    final = []
-    for at, (dy, skip, got, even) in enumerate(waiting):
-        final += ins[2 * at : 2 * at + 2]
-        for e, x in zip(evens, joined(skip, got, even)):
-            final.append(yz_move(x, -dy, e))
+        even = row([], evens, kvs[dy], *long_part, qs, FAR)
+        rest = joined(0, got, even, FAR)
+        final += [yz_move(zero, -dy, 0), yz_move(one, -dy, 1)]
+        final += [yz_move(x, -dy, e) for e, x in zip(evens, rest)]
+    final = own + final
     partial = call(
         functools.partial(merge_kernel, dys, seqs, groups),
         "merge",

time: 69.6 us -> 68.3 us (0.981)
  waiting for transfers between devices: 22.3 us -> 21.2 us
    ppermute x3, waiting for transfers between devices: 11.1 us -> 10.1 us  [tp_swap(): return lax.ppermute(x, 'tp', [(i, (i + 1) % tps) for i in range(tps)])]
  transfers between devices with their start and end apart: 18 -> 18, of which waited for: 9 -> 9; matrix products, arithmetic and copies ran while one was open for 0% -> 0% of each run, Pallas kernels for 19% -> 20%
where the time goes in v4:
time: 68.3 us; the launch traced here: 68.1 us
  starting transfers between devices  25.7 us (38%)
  waiting for transfers between devices  21.2 us (31%)
  Pallas kernels  19.6 us (29%)
  between operations  1.52 us (2%)
    ppermute x8, starting transfers between devices, seq_pair(): return lax.ppermute(x, 'seq', [(i, i ^ k) for i in range(seqs)])  10.3 us
    ppermute x6, starting transfers between devices, yz_move(): return lax.ppermute(x, both, perm)  10.1 us
    ppermute x3, waiting for transfers between devices, tp_swap(): return lax.ppermute(x, 'tp', [(i, (i + 1) % tps) for i in range(tps)])  10.1 us
    ppermute x6, waiting for transfers between devices, yz_move(): return lax.ppermute(x, both, perm)  6.66 us
    ppermute x3, starting transfers between devices, tp_swap(): return lax.ppermute(x, 'tp', [(i, (i + 1) % tps) for i in range(tps)])  4.71 us
    ppermute x8, waiting for transfers between devices, seq_pair(): return lax.ppermute(x, 'seq', [(i, i ^ k) for i in range(seqs)])  4.42 us
    pallas_call x4, Pallas kernels, row(): call(functools.partial(row_kernel, requests, stacked, single), 'row', sta...  4.16 us
    pallas_call x1, Pallas kernels, local(): call(functools.partial(fetch_kernel, seqs, requests, dys), 'fetch', tuple...  3.41 us
  transfers between devices with their start and end apart: 18, of which 9 were waited for; matrix products, arithmetic and copies ran while one was open for 0% of the time, Pallas kernels for 20%

profile of v4, /device:TPU:0, one launch (start us, length us, event | category | flops | bytes accessed | tf_op | source)
XLA Modules:
  0.0 68.1 jit_solution(5141946992985026223)
XLA Ops:
  0.6 2.0 %first.1 = (bf16[96,512]{1,0:T(8,128)(2,1)S(1)}, bf16[96,1024]{1,0:T(8,128)(2,1)S(1)}, bf16[2,256,512]{2,1,0:T(8,128)(2,1)S(1)}, f32[96,32]{1,0:T(8,128)S(1)}) custom-call(bf16[2,32,1024]{2,1,0:T(8,128)(2,1)} %xs_hbm.1, bf16[1,32,1024]{2,1,0:T(8,128)(2,1)} %xl_hbm.1, bf16[3,1024,512]{2,1,0:T(8,128)(2,1)} %w_ref.1, bf16[1,2,256,512]{3,2,1,0:T(8,128)(2,1)} %kv_hbm.1, ...), custom_call_target="tpu_custom_call" | custom-call | flops 100000000 | bytes 1000000 | tf_op jit(solution)/shard_map/first/pallas_call | solution.py:506
  4.3 2.7 %collective-permute-start = (bf16[32,640]{1,0:T(8,128)(2,1)S(1)}, bf16[32,640]{1,0:T(8,128)(2,1)S(1)}, u32[]{:S(2)}, u32[]{:S(2)}) collective-permute-start(bf16[32,640]{1,0:T(8,128)(2,1)S(1)} %long.1.rest_0_), channel_id=1, source_target_pairs={{0,2},{2,0},{4,6},{6,4},{1,3},{3,1},{5,7},{7,5},{8,10},{10,8},{12,... | collective-permute-start | bytes 122888 | tf_op jit(solution)/shard_map/ppermute | solution.py:491
  6.9 2.6 %collective-permute-start.1 = (bf16[32,640]{1,0:T(8,128)(2,1)S(1)}, bf16[32,640]{1,0:T(8,128)(2,1)S(1)}, u32[]{:S(2)}, u32[]{:S(2)}) collective-permute-start(bf16[32,640]{1,0:T(8,128)(2,1)S(1)} %long.1.rest_0_), channel_id=1, source_target_pairs={{0,4},{2,6},{4,0},{6,2},{1,5},{3,7},{5,1},{7,3},{8,12},{10,14},{12... | collective-permute-start | bytes 122888 | tf_op jit(solution)/shard_map/ppermute | solution.py:491
  9.5 2.3 %attend.1 = (bf16[64,512]{1,0:T(8,128)(2,1)S(1)}, f32[32,512]{1,0:T(8,128)S(1)}, bf16[32,128]{1,0:T(8,128)(2,1)S(1)}) custom-call(bf16[96,512]{1,0:T(8,128)(2,1)S(1)} %get-tuple-element.48.q_ref, bf16[96,1024]{1,0:T(8,128)(2,1)S(1)} %get-tuple-element.46.x_ref, bf16[3,1024,512]{2,1,0:T(8,128)(2,1)S(1)} %copy-done.2, bf16[2,2,512,512]{3,2,1,0:T(8,128)(2,1)S(1)} %copy-done.6, ...), custom_call_target="tpu_custom_call" | custom-call | flops 4000000000 | bytes 1000000 | tf_op jit(solution)/shard_map/attend/pallas_call | solution.py:532
  11.9 0.8 %collective-permute-done.1.rest_2_ = bf16[32,640]{1,0:T(8,128)(2,1)S(1)} collective-permute-done((bf16[32,640]{1,0:T(8,128)(2,1)S(1)}, bf16[32,640]{1,0:T(8,128)(2,1)S(1)}, u32[]{:S(2)}, u32[]{:S(2)}) %collective-permute-start.1) | collective-permute-done | bytes 40992 | tf_op jit(solution)/shard_map/ppermute | solution.py:491
  12.7 2.6 %collective-permute-done.2.rest_3_ = bf16[32,640]{1,0:T(8,128)(2,1)S(1)} collective-permute-done((bf16[32,640]{1,0:T(8,128)(2,1)S(1)}, bf16[32,640]{1,0:T(8,128)(2,1)S(1)}, u32[]{:S(2)}, u32[]{:S(2)}) %collective-permute-start.2) | collective-permute-done | bytes 40992 | tf_op jit(solution)/shard_map/ppermute | solution.py:491
  15.8 1.6 %collective-permute-start.3 = (bf16[96,1024]{1,0:T(8,128)(2,1)S(1)}, bf16[96,1024]{1,0:T(8,128)(2,1)S(1)}, u32[]{:S(2)}, u32[]{:S(2)}) collective-permute-start(bf16[96,1024]{1,0:T(8,128)(2,1)S(1)} %output.1.a_ref), channel_id=1, source_target_pairs={{0,1},{1,0},{2,3},{3,2},{4,5},{5,4},{6,7},{7,6},{8,9},{9,8},{10,11... | collective-permute-start | bytes 589832 | tf_op jit(solution)/shard_map/ppermute | solution.py:503
  17.4 3.4 %fetch.1 = (bf16[9,2,128,512]{3,2,1,0:T(8,128)(2,1)S(1)}, bf16[9,2,128,512]{3,2,1,0:T(8,128)(2,1)S(1)}) custom-call(s32[32]{0:T(128)S(1)} %copy-done.7, s32[4]{0:T(128)S(1)} %copy-done.8, bf16[2,32,64,512]{3,2,1,0:T(8,128)(2,1)} %own_ref, bf16[2,32,64,512]{3,2,1,0:T(8,128)(2,1)S(1)} %collective-permute-done.4.other_ref), custom_call_target="tpu_custom_call" | custom-call | flops 4000000000 | bytes 1000000 | tf_op jit(solution)/shard_map/fetch/pallas_call | solution.py:552
  20.8 0.7 %collective-permute-done.3.b_ref = bf16[96,1024]{1,0:T(8,128)(2,1)S(1)} collective-permute-done((bf16[96,1024]{1,0:T(8,128)(2,1)S(1)}, bf16[96,1024]{1,0:T(8,128)(2,1)S(1)}, u32[]{:S(2)}, u32[]{:S(2)}) %collective-permute-start.3) | collective-permute-done | bytes 196640 | tf_op jit(solution)/shard_map/ppermute | solution.py:503
  22.1 1.9 %collective-permute-start.6 = (bf16[64,512]{1,0:T(8,128)(2,1)S(1)}, bf16[64,512]{1,0:T(8,128)(2,1)S(1)}, u32[]{:S(2)}, u32[]{:S(2)}) collective-permute-start(bf16[64,512]{1,0:T(8,128)(2,1)S(1)} %get-tuple-element.72), channel_id=1, source_target_pairs={{0,4},{2,6},{4,0},{6,2},{1,5},{3,7},{5,1},{7,3},{8,12},{10,14},{12... | collective-permute-start | bytes 196616 | tf_op jit(solution)/shard_map/ppermute | solution.py:491
  24.0 2.5 %collective-permute-start.7 = (bf16[64,512]{1,0:T(8,128)(2,1)S(1)}, bf16[64,512]{1,0:T(8,128)(2,1)S(1)}, u32[]{:S(2)}, u32[]{:S(2)}) collective-permute-start(bf16[64,512]{1,0:T(8,128)(2,1)S(1)} %get-tuple-element.72), channel_id=1, source_target_pairs={{0,6},{2,4},{4,2},{6,0},{1,7},{3,5},{5,3},{7,1},{8,14},{10,12},{12... | collective-permute-start | bytes 196616 | tf_op jit(solution)/shard_map/ppermute | solution.py:491
  26.5 1.5 %collective-permute-start.10 = (bf16[96,512]{1,0:T(8,128)(2,1)S(1)}, bf16[96,512]{1,0:T(8,128)(2,1)S(1)}, u32[]{:S(2)}, u32[]{:S(2)}) collective-permute-start(bf16[96,512]{1,0:T(8,128)(2,1)S(1)} %get-tuple-element.69.q_ref), channel_id=1, source_target_pairs={{0,16},{2,18},{4,20},{6,22},{8,24},{10,26},{12,28},{14,30},{16,0},... | collective-permute-start | bytes 294920 | tf_op jit(solution)/shard_map/ppermute | solution.py:500
  28.0 1.0 %near.2 = (bf16[104,512]{1,0:T(8,128)(2,1)S(1)}, bf16[32,512]{1,0:T(8,128)(2,1)S(1)}, f32[32,128]{1,0:T(8,128)S(1)}) custom-call(bf16[9,2,128,512]{3,2,1,0:T(8,128)(2,1)S(1)} %get-tuple-element.68.kv_ref, bf16[96,512]{1,0:T(8,128)(2,1)S(1)} %get-tuple-element.69.q_ref), custom_call_target="tpu_custom_call" | custom-call | flops 1000000000 | bytes 1000000 | tf_op jit(solution)/shard_map/near/pallas_call | solution.py:575
  29.1 1.0 %collective-permute-done.7 = bf16[64,512]{1,0:T(8,128)(2,1)S(1)} collective-permute-done((bf16[64,512]{1,0:T(8,128)(2,1)S(1)}, bf16[64,512]{1,0:T(8,128)(2,1)S(1)}, u32[]{:S(2)}, u32[]{:S(2)}) %collective-permute-start.7) | collective-permute-done | bytes 65568 | tf_op jit(solution)/shard_map/ppermute | solution.py:491
  30.1 1.6 %collective-permute-start.12 = (bf16[192,512]{1,0:T(8,128)(2,1)S(1)}, bf16[192,512]{1,0:T(8,128)(2,1)S(1)}, u32[]{:S(2)}, u32[]{:S(2)}) collective-permute-start(bf16[192,512]{1,0:T(8,128)(2,1)S(1)} %constant_dynamic-update-slice_fusion.q_ref), channel_id=1, source_target_pairs={{0,16},{2,18},{4,20},{6,22},{8,24},{10,26},{12,28},{14,30},{16,0},... | collective-permute-start | bytes 589832 | tf_op jit(solution)/shard_map/ppermute | solution.py:500
  31.7 1.3 %row.4 = bf16[2,104,512]{2,1,0:T(8,128)(2,1)S(1)} custom-call(bf16[9,2,128,512]{3,2,1,0:T(8,128)(2,1)S(1)} %get-tuple-element.68.kv_ref, bf16[32,512]{1,0:T(8,128)(2,1)S(1)} %get-tuple-element.70.o_ref, f32[32,128]{1,0:T(8,128)S(1)} %get-tuple-element.71.stat_ref, bf16[192,512]{1,0:T(8,128)(2,1)S(1)} %constant_dynamic-update-slice_fusion.q_ref), custom_call_target="tpu_custom_call" | custom-call | flops 1000000 | bytes 1000000 | tf_op jit(solution)/shard_map/row/pallas_call | solution.py:585
  33.1 0.7 %row.5.rest_1_ = bf16[104,512]{1,0:T(8,128)(2,1)S(1)} custom-call(bf16[9,2,128,512]{3,2,1,0:T(8,128)(2,1)S(1)} %get-tuple-element.68.kv_ref, bf16[32,512]{1,0:T(8,128)(2,1)S(1)} %get-tuple-element.70.o_ref, f32[32,128]{1,0:T(8,128)S(1)} %get-tuple-element.71.stat_ref, bf16[192,512]{1,0:T(8,128)(2,1)S(1)} %constant_dynamic-update-slice_fusion.q_ref), custom_call_target="tpu_custom_call" | custom-call | flops 1000000 | bytes 1000000 | tf_op jit(solution)/shard_map/row/pallas_call | solution.py:585
  33.9 1.0 %near.3 = (bf16[104,512]{1,0:T(8,128)(2,1)S(1)}, bf16[32,512]{1,0:T(8,128)(2,1)S(1)}, f32[32,128]{1,0:T(8,128)S(1)}) custom-call(bf16[9,2,128,512]{3,2,1,0:T(8,128)(2,1)S(1)} %get-tuple-element.80.kv_ref, bf16[96,512]{1,0:T(8,128)(2,1)S(1)} %collective-permute-done.10.q_ref), custom_call_target="tpu_custom_call" | custom-call | flops 10000000000 | bytes 1000000 | tf_op jit(solution)/shard_map/near/pallas_call | solution.py:575
  35.5 1.5 %collective-permute-done.12.q_ref = bf16[192,512]{1,0:T(8,128)(2,1)S(1)} collective-permute-done((bf16[192,512]{1,0:T(8,128)(2,1)S(1)}, bf16[192,512]{1,0:T(8,128)(2,1)S(1)}, u32[]{:S(2)}, u32[]{:S(2)}) %collective-permute-start.12) | collective-permute-done | bytes 196640 | tf_op jit(solution)/shard_map/ppermute | solution.py:500
  37.0 1.3 %row.6 = (bf16[1,104,512]{2,1,0:T(8,128)(2,1)S(1)}, bf16[104,512]{1,0:T(8,128)(2,1)S(1)}) custom-call(bf16[9,2,128,512]{3,2,1,0:T(8,128)(2,1)S(1)} %get-tuple-element.80.kv_ref, bf16[32,512]{1,0:T(8,128)(2,1)S(1)} %get-tuple-element.83.o_ref, f32[32,128]{1,0:T(8,128)S(1)} %get-tuple-element.84.stat_ref, bf16[192,512]{1,0:T(8,128)(2,1)S(1)} %collective-permute-done.12.q_ref), custom_call_target="tpu_custom_call" | custom-call | flops 10000000000 | bytes 1000000 | tf_op jit(solution)/shard_map/row/pallas_call | solution.py:585
  39.7 1.9 %collective-permute-start.13 = (bf16[104,512]{1,0:T(8,128)(2,1)S(1)}, bf16[104,512]{1,0:T(8,128)(2,1)S(1)}, u32[]{:S(2)}, u32[]{:S(2)}) collective-permute-start(bf16[104,512]{1,0:T(8,128)(2,1)S(1)} %get-tuple-element.86), channel_id=1, source_target_pairs={{0,18},{2,16},{4,22},{6,20},{8,26},{10,24},{12,30},{14,28},{16,2},... | collective-permute-start | bytes 319496 | tf_op jit(solution)/shard_map/ppermute | solution.py:500
  42.1 2.2 %collective-permute-start.9 = (bf16[104,512]{1,0:T(8,128)(2,1)S(1)}, bf16[104,512]{1,0:T(8,128)(2,1)S(1)}, u32[]{:S(2)}, u32[]{:S(2)}) collective-permute-start(bf16[104,512]{1,0:T(8,128)(2,1)S(1)} %get-tuple-element.79), channel_id=1, source_target_pairs={{0,4},{2,6},{4,0},{6,2},{8,12},{10,14},{12,8},{14,10},{16,20},{18,... | collective-permute-start | bytes 319496 | tf_op jit(solution)/shard_map/ppermute | solution.py:500
  44.6 2.3 %collective-permute-start.15 = (bf16[104,512]{1,0:T(8,128)(2,1)S(1)}, bf16[104,512]{1,0:T(8,128)(2,1)S(1)}, u32[]{:S(2)}, u32[]{:S(2)}) collective-permute-start(bf16[104,512]{1,0:T(8,128)(2,1)S(1)} %join.3), channel_id=1, source_target_pairs={{0,20},{2,22},{4,16},{6,18},{8,28},{10,30},{12,24},{14,26},{16,4},... | collective-permute-start | bytes 319496 | tf_op jit(solution)/shard_map/ppermute | solution.py:500
  46.9 1.9 %collective-permute-done.9.rest_1_ = bf16[104,512]{1,0:T(8,128)(2,1)S(1)} collective-permute-done((bf16[104,512]{1,0:T(8,128)(2,1)S(1)}, bf16[104,512]{1,0:T(8,128)(2,1)S(1)}, u32[]{:S(2)}, u32[]{:S(2)}) %collective-permute-start.9) | collective-permute-done | bytes 106528 | tf_op jit(solution)/shard_map/ppermute | solution.py:500
  48.9 3.2 %collective-permute-done.15.rest_4_ = bf16[104,512]{1,0:T(8,128)(2,1)S(1)} collective-permute-done((bf16[104,512]{1,0:T(8,128)(2,1)S(1)}, bf16[104,512]{1,0:T(8,128)(2,1)S(1)}, u32[]{:S(2)}, u32[]{:S(2)}) %collective-permute-start.15) | collective-permute-done | bytes 106528 | tf_op jit(solution)/shard_map/ppermute | solution.py:500
  52.1 0.9 %merge.1.a_ref = bf16[96,1024]{1,0:T(8,128)(2,1)S(1)} custom-call(bf16[512,1024]{1,0:T(8,128)(2,1)S(1)} %copy-done.3, bf16[104,512]{1,0:T(8,128)(2,1)S(1)} %get-tuple-element.78.rest_0_, bf16[104,512]{1,0:T(8,128)(2,1)S(1)} %collective-permute-done.9.rest_1_, bf16[104,512]{1,0:T(8,128)(2,1)S(1)} %collective-permute-done.11.rest_2_, ...), custom_call_target="tpu_custom_call" | custom-call | flops 100000000 | bytes 1000000 | tf_op jit(solution)/shard_map/merge/pallas_call | solution.py:626
  53.0 1.6 %collective-permute-start.16 = (bf16[96,1024]{1,0:T(8,128)(2,1)S(1)}, bf16[96,1024]{1,0:T(8,128)(2,1)S(1)}, u32[]{:S(2)}, u32[]{:S(2)}) collective-permute-start(bf16[96,1024]{1,0:T(8,128)(2,1)S(1)} %merge.1.a_ref), channel_id=1, source_target_pairs={{0,1},{1,0},{2,3},{3,2},{4,5},{5,4},{6,7},{7,6},{8,9},{9,8},{10,11... | collective-permute-start | bytes 589832 | tf_op jit(solution)/shard_map/ppermute | solution.py:503
  54.5 5.2 %collective-permute-done.16.b_ref = bf16[96,1024]{1,0:T(8,128)(2,1)S(1)} collective-permute-done((bf16[96,1024]{1,0:T(8,128)(2,1)S(1)}, bf16[96,1024]{1,0:T(8,128)(2,1)S(1)}, u32[]{:S(2)}, u32[]{:S(2)}) %collective-permute-start.16) | collective-permute-done | bytes 196640 | tf_op jit(solution)/shard_map/ppermute | solution.py:503
  59.7 1.7 %ffn.1 = (bf16[96,1024]{1,0:T(8,128)(2,1)S(1)}, bf16[96,1024]{1,0:T(8,128)(2,1)S(1)}) custom-call(bf16[96,1024]{1,0:T(8,128)(2,1)S(1)} %get-tuple-element.67.h_ref, bf16[96,1024]{1,0:T(8,128)(2,1)S(1)} %merge.1.a_ref, bf16[96,1024]{1,0:T(8,128)(2,1)S(1)} %collective-permute-done.16.b_ref, bf16[1024,2048]{1,0:T(8,128)(2,1)S(1)} %copy-done, ...), custom_call_target="tpu_custom_call" | custom-call | flops 100000000 | bytes 1000000 | tf_op jit(solution)/shard_map/ffn/pallas_call | solution.py:638
  61.5 1.6 %collective-permute-start.17 = (bf16[96,1024]{1,0:T(8,128)(2,1)S(1)}, bf16[96,1024]{1,0:T(8,128)(2,1)S(1)}, u32[]{:S(2)}, u32[]{:S(2)}) collective-permute-start(bf16[96,1024]{1,0:T(8,128)(2,1)S(1)} %get-tuple-element.89.a_ref), channel_id=1, source_target_pairs={{0,1},{1,0},{2,3},{3,2},{4,5},{5,4},{6,7},{7,6},{8,9},{9,8},{10,11... | collective-permute-start | bytes 589832 | tf_op jit(solution)/shard_map/ppermute | solution.py:503
  63.1 4.1 %collective-permute-done.17.b_ref = bf16[96,1024]{1,0:T(8,128)(2,1)S(1)} collective-permute-done((bf16[96,1024]{1,0:T(8,128)(2,1)S(1)}, bf16[96,1024]{1,0:T(8,128)(2,1)S(1)}, u32[]{:S(2)}, u32[]{:S(2)}) %collective-permute-start.17) | collective-permute-done | bytes 196640 | tf_op jit(solution)/shard_map/ppermute | solution.py:503
  67.2 0.9 %final.1 = (bf16[2,32,1024]{2,1,0:T(8,128)(2,1)}, bf16[1,32,1024]{2,1,0:T(8,128)(2,1)}) custom-call(bf16[96,1024]{1,0:T(8,128)(2,1)S(1)} %get-tuple-element.88.h_ref, bf16[96,1024]{1,0:T(8,128)(2,1)S(1)} %get-tuple-element.89.a_ref, bf16[96,1024]{1,0:T(8,128)(2,1)S(1)} %collective-permute-done.17.b_ref), custom_call_target="tpu_custom_call" | custom-call | flops 100000000 | bytes 1000000 | tf_op jit(solution)/shard_map/final/pallas_call | solution.py:642
  (43 shorter events, 4.8 us)
Async XLA Ops:
  2.6 14.8 %collective-permute-start.4 = (bf16[2,32,64,512]{3,2,1,0:T(8,128)(2,1)}, bf16[2,32,64,512]{3,2,1,0:T(8,128)(2,1)S(1)}, u32[]{:S(2)}, u32[]{:S(2)}) collective-permute-start(bf16[2,32,64,512]{3,2,1,0:T(8,128)(2,1)} %own_ref), channel_id=1, source_target_pairs={{0,8},{8,0},{16,24},{24,16},{1,9},{9,1},{17,25},{25,17},{2,10},{10... | collective-permute-start | bytes 12582920 | tf_op jit(solution)/shard_map/ppermute | solution.py:530
  3.8 5.7 %copy-start.2 = (bf16[3,1024,512]{2,1,0:T(8,128)(2,1)S(1)}, bf16[3,1024,512]{2,1,0:T(8,128)(2,1)}, u32[]{:S(2)}) copy-start(bf16[3,1024,512]{2,1,0:T(8,128)(2,1)} %w_ref.1) | copy-start | bytes 9437188
  3.8 5.7 %copy-start.6 = (bf16[2,2,512,512]{3,2,1,0:T(8,128)(2,1)S(1)}, bf16[2,2,512,512]{3,2,1,0:T(8,128)(2,1)}, u32[]{:S(2)}) copy-start(bf16[2,2,512,512]{3,2,1,0:T(8,128)(2,1)} %skv_ref) | copy-start | bytes 6291460
  4.3 7.6 %collective-permute-start = (bf16[32,640]{1,0:T(8,128)(2,1)S(1)}, bf16[32,640]{1,0:T(8,128)(2,1)S(1)}, u32[]{:S(2)}, u32[]{:S(2)}) collective-permute-start(bf16[32,640]{1,0:T(8,128)(2,1)S(1)} %long.1.rest_0_), channel_id=1, source_target_pairs={{0,2},{2,0},{4,6},{6,4},{1,3},{3,1},{5,7},{7,5},{8,10},{10,8},{12,... | collective-permute-start | bytes 122888 | tf_op jit(solution)/shard_map/ppermute | solution.py:491
  6.9 5.8 %collective-permute-start.1 = (bf16[32,640]{1,0:T(8,128)(2,1)S(1)}, bf16[32,640]{1,0:T(8,128)(2,1)S(1)}, u32[]{:S(2)}, u32[]{:S(2)}) collective-permute-start(bf16[32,640]{1,0:T(8,128)(2,1)S(1)} %long.1.rest_0_), channel_id=1, source_target_pairs={{0,4},{2,6},{4,0},{6,2},{1,5},{3,7},{5,1},{7,3},{8,12},{10,14},{12... | collective-permute-start | bytes 122888 | tf_op jit(solution)/shard_map/ppermute | solution.py:491
  9.5 5.8 %collective-permute-start.2 = (bf16[32,640]{1,0:T(8,128)(2,1)S(1)}, bf16[32,640]{1,0:T(8,128)(2,1)S(1)}, u32[]{:S(2)}, u32[]{:S(2)}) collective-permute-start(bf16[32,640]{1,0:T(8,128)(2,1)S(1)} %long.1.rest_0_), channel_id=1, source_target_pairs={{0,6},{2,4},{4,2},{6,0},{1,7},{3,5},{5,3},{7,1},{8,14},{10,12},{12... | collective-permute-start | bytes 122888 | tf_op jit(solution)/shard_map/ppermute | solution.py:491
  9.5 5.8 %copy-start.4 = (bf16[512,1024]{1,0:T(8,128)(2,1)S(1)}, bf16[512,1024]{1,0:T(8,128)(2,1)}, u32[]{:S(2)}) copy-start(bf16[512,1024]{1,0:T(8,128)(2,1)} %wo_ref) | copy-start | bytes 3145732
  9.5 7.8 %copy-start.7 = (s32[32]{0:T(128)S(1)}, s32[32]{0:T(128)}, u32[]{:S(2)}) copy-start(s32[32]{0:T(128)} %doc_ref) | copy-start | bytes 388
  9.5 7.8 %copy-start.8 = (s32[4]{0:T(128)S(1)}, s32[4]{0:T(128)}, u32[]{:S(2)}) copy-start(s32[4]{0:T(128)} %long_ref.1) | copy-start | bytes 52
  15.8 5.8 %copy-start.5 = (bf16[1024,512]{1,0:T(8,128)(2,1)S(1)}, bf16[1024,512]{1,0:T(8,128)(2,1)}, u32[]{:S(2)}) copy-start(bf16[1024,512]{1,0:T(8,128)(2,1)} %w_ref.2) | copy-start | bytes 3145732
  15.8 5.7 %collective-permute-start.3 = (bf16[96,1024]{1,0:T(8,128)(2,1)S(1)}, bf16[96,1024]{1,0:T(8,128)(2,1)S(1)}, u32[]{:S(2)}, u32[]{:S(2)}) collective-permute-start(bf16[96,1024]{1,0:T(8,128)(2,1)S(1)} %output.1.a_ref), channel_id=1, source_target_pairs={{0,1},{1,0},{2,3},{3,2},{4,5},{5,4},{6,7},{7,6},{8,9},{9,8},{10,11... | collective-permute-start | bytes 589832 | tf_op jit(solution)/shard_map/ppermute | solution.py:503
  22.0 7.0 %collective-permute-start.5 = (bf16[64,512]{1,0:T(8,128)(2,1)S(1)}, bf16[64,512]{1,0:T(8,128)(2,1)S(1)}, u32[]{:S(2)}, u32[]{:S(2)}) collective-permute-start(bf16[64,512]{1,0:T(8,128)(2,1)S(1)} %get-tuple-element.72), channel_id=1, source_target_pairs={{0,2},{2,0},{4,6},{6,4},{1,3},{3,1},{5,7},{7,5},{8,10},{10,8},{12,... | collective-permute-start | bytes 196616 | tf_op jit(solution)/shard_map/ppermute | solution.py:491
  22.1 7.0 %collective-permute-start.6 = (bf16[64,512]{1,0:T(8,128)(2,1)S(1)}, bf16[64,512]{1,0:T(8,128)(2,1)S(1)}, u32[]{:S(2)}, u32[]{:S(2)}) collective-permute-start(bf16[64,512]{1,0:T(8,128)(2,1)S(1)} %get-tuple-element.72), channel_id=1, source_target_pairs={{0,4},{2,6},{4,0},{6,2},{1,5},{3,7},{5,1},{7,3},{8,12},{10,14},{12... | collective-permute-start | bytes 196616 | tf_op jit(solution)/shard_map/ppermute | solution.py:491
  24.0 6.1 %collective-permute-start.7 = (bf16[64,512]{1,0:T(8,128)(2,1)S(1)}, bf16[64,512]{1,0:T(8,128)(2,1)S(1)}, u32[]{:S(2)}, u32[]{:S(2)}) collective-permute-start(bf16[64,512]{1,0:T(8,128)(2,1)S(1)} %get-tuple-element.72), channel_id=1, source_target_pairs={{0,6},{2,4},{4,2},{6,0},{1,7},{3,5},{5,3},{7,1},{8,14},{10,12},{12... | collective-permute-start | bytes 196616 | tf_op jit(solution)/shard_map/ppermute | solution.py:491
  26.5 7.4 %collective-permute-start.10 = (bf16[96,512]{1,0:T(8,128)(2,1)S(1)}, bf16[96,512]{1,0:T(8,128)(2,1)S(1)}, u32[]{:S(2)}, u32[]{:S(2)}) collective-permute-start(bf16[96,512]{1,0:T(8,128)(2,1)S(1)} %get-tuple-element.69.q_ref), channel_id=1, source_target_pairs={{0,16},{2,18},{4,20},{6,22},{8,24},{10,26},{12,28},{14,30},{16,0},... | collective-permute-start | bytes 294920 | tf_op jit(solution)/shard_map/ppermute | solution.py:500
  30.1 6.9 %collective-permute-start.12 = (bf16[192,512]{1,0:T(8,128)(2,1)S(1)}, bf16[192,512]{1,0:T(8,128)(2,1)S(1)}, u32[]{:S(2)}, u32[]{:S(2)}) collective-permute-start(bf16[192,512]{1,0:T(8,128)(2,1)S(1)} %constant_dynamic-update-slice_fusion.q_ref), channel_id=1, source_target_pairs={{0,16},{2,18},{4,20},{6,22},{8,24},{10,26},{12,28},{14,30},{16,0},... | collective-permute-start | bytes 589832 | tf_op jit(solution)/shard_map/ppermute | solution.py:500
  33.1 8.5 %collective-permute-start.8 = (bf16[2,104,512]{2,1,0:T(8,128)(2,1)S(1)}, bf16[2,104,512]{2,1,0:T(8,128)(2,1)S(1)}, u32[]{:S(2)}, u32[]{:S(2)}) collective-permute-start(bf16[2,104,512]{2,1,0:T(8,128)(2,1)S(1)} %row.4), channel_id=1, source_target_pairs={{0,2},{2,0},{4,6},{6,4},{1,3},{3,1},{5,7},{7,5},{8,10},{10,8},{12,... | collective-permute-start | bytes 638984 | tf_op jit(solution)/shard_map/ppermute | solution.py:491
  34.9 12.0 %collective-permute-start.11 = (bf16[104,512]{1,0:T(8,128)(2,1)S(1)}, bf16[104,512]{1,0:T(8,128)(2,1)S(1)}, u32[]{:S(2)}, u32[]{:S(2)}) collective-permute-start(bf16[104,512]{1,0:T(8,128)(2,1)S(1)} %get-tuple-element.82), channel_id=1, source_target_pairs={{0,16},{2,18},{4,20},{6,22},{8,24},{10,26},{12,28},{14,30},{16,0},... | collective-permute-start | bytes 319496 | tf_op jit(solution)/shard_map/ppermute | solution.py:500
  38.3 5.9 %collective-permute-start.14 = (bf16[1,104,512]{2,1,0:T(8,128)(2,1)S(1)}, bf16[1,104,512]{2,1,0:T(8,128)(2,1)S(1)}, u32[]{:S(2)}, u32[]{:S(2)}) collective-permute-start(bf16[1,104,512]{2,1,0:T(8,128)(2,1)S(1)} %get-tuple-element.87), channel_id=1, source_target_pairs={{0,2},{2,0},{4,6},{6,4},{1,3},{3,1},{5,7},{7,5},{8,10},{10,8},{12,... | collective-permute-start | bytes 319496 | tf_op jit(solution)/shard_map/ppermute | solution.py:491
  39.7 7.2 %collective-permute-start.13 = (bf16[104,512]{1,0:T(8,128)(2,1)S(1)}, bf16[104,512]{1,0:T(8,128)(2,1)S(1)}, u32[]{:S(2)}, u32[]{:S(2)}) collective-permute-start(bf16[104,512]{1,0:T(8,128)(2,1)S(1)} %get-tuple-element.86), channel_id=1, source_target_pairs={{0,18},{2,16},{4,22},{6,20},{8,26},{10,24},{12,30},{14,28},{16,2},... | collective-permute-start | bytes 319496 | tf_op jit(solution)/shard_map/ppermute | solution.py:500
  42.0 10.0 %copy-start.3 = (bf16[512,1024]{1,0:T(8,128)(2,1)S(1)}, bf16[512,1024]{1,0:T(8,128)(2,1)}, u32[]{:S(2)}) copy-start(bf16[512,1024]{1,0:T(8,128)(2,1)} %w_ref.3) | copy-start | bytes 3145732
  42.1 6.8 %collective-permute-start.9 = (bf16[104,512]{1,0:T(8,128)(2,1)S(1)}, bf16[104,512]{1,0:T(8,128)(2,1)S(1)}, u32[]{:S(2)}, u32[]{:S(2)}) collective-permute-start(bf16[104,512]{1,0:T(8,128)(2,1)S(1)} %get-tuple-element.79), channel_id=1, source_target_pairs={{0,4},{2,6},{4,0},{6,2},{8,12},{10,14},{12,8},{14,10},{16,20},{18,... | collective-permute-start | bytes 319496 | tf_op jit(solution)/shard_map/ppermute | solution.py:500
  44.3 15.5 %copy-start = (bf16[1024,2048]{1,0:T(8,128)(2,1)S(1)}, bf16[1024,2048]{1,0:T(8,128)(2,1)}, u32[]{:S(2)}) copy-start(bf16[1024,2048]{1,0:T(8,128)(2,1)} %up_ref.1) | copy-start | bytes 12582916
  44.3 15.5 %copy-start.1 = (bf16[2048,1024]{1,0:T(8,128)(2,1)S(1)}, bf16[2048,1024]{1,0:T(8,128)(2,1)}, u32[]{:S(2)}) copy-start(bf16[2048,1024]{1,0:T(8,128)(2,1)} %down_ref.1) | copy-start | bytes 12582916
  44.6 7.5 %collective-permute-start.15 = (bf16[104,512]{1,0:T(8,128)(2,1)S(1)}, bf16[104,512]{1,0:T(8,128)(2,1)S(1)}, u32[]{:S(2)}, u32[]{:S(2)}) collective-permute-start(bf16[104,512]{1,0:T(8,128)(2,1)S(1)} %join.3), channel_id=1, source_target_pairs={{0,20},{2,22},{4,16},{6,18},{8,28},{10,30},{12,24},{14,26},{16,4},... | collective-permute-start | bytes 319496 | tf_op jit(solution)/shard_map/ppermute | solution.py:500
  53.0 6.8 %collective-permute-start.16 = (bf16[96,1024]{1,0:T(8,128)(2,1)S(1)}, bf16[96,1024]{1,0:T(8,128)(2,1)S(1)}, u32[]{:S(2)}, u32[]{:S(2)}) collective-permute-start(bf16[96,1024]{1,0:T(8,128)(2,1)S(1)} %merge.1.a_ref), channel_id=1, source_target_pairs={{0,1},{1,0},{2,3},{3,2},{4,5},{5,4},{6,7},{7,6},{8,9},{9,8},{10,11... | collective-permute-start | bytes 589832 | tf_op jit(solution)/shard_map/ppermute | solution.py:503
  61.5 5.7 %collective-permute-start.17 = (bf16[96,1024]{1,0:T(8,128)(2,1)S(1)}, bf16[96,1024]{1,0:T(8,128)(2,1)S(1)}, u32[]{:S(2)}, u32[]{:S(2)}) collective-permute-start(bf16[96,1024]{1,0:T(8,128)(2,1)S(1)} %get-tuple-element.89.a_ref), channel_id=1, source_target_pairs={{0,1},{1,0},{2,3},{3,2},{4,5},{5,4},{6,7},{7,6},{8,9},{9,8},{10,11... | collective-permute-start | bytes 589832 | tf_op jit(solution)/shard_map/ppermute | solution.py:503

commit v5 on v4

--- a/solution.py
+++ b/solution.py
@@ -618,6 +618,7 @@
         qs, _ = lax.optimization_barrier((far_q[dy - 1], zero))
         odd, one = row(odds[1:], odds[:1], kvs[dy], *long_part, qs, FAR)
         got = seq_pair(odd, 1)
+        qs, rest = lax.optimization_barrier((qs, rest))
         even = row([], evens, kvs[dy], *long_part, qs, FAR)
         rest = joined(0, got, even, FAR)
         final += [yz_move(zero, -dy, 0), yz_move(one, -dy, 1)]

time: 68.3 us -> 68.3 us (level)
  starting transfers between devices: 25.7 us -> 24.2 us
  waiting for transfers between devices: 21.2 us -> 22.7 us
    ppermute x6, starting transfers between devices: 10.1 us -> 8.59 us  [yz_move(): return lax.ppermute(x, both, perm)]
    ppermute x8, waiting for transfers between devices: 4.42 us -> 5.95 us  [seq_pair(): return lax.ppermute(x, 'seq', [(i, i ^ k) for i in range(seqs)])]
  transfers between devices with their start and end apart: 18 -> 18, of which waited for: 9 -> 10; matrix products, arithmetic and copies ran while one was open for 0% -> 0% of each run, Pallas kernels for 20% -> 20%
where the time goes in v5:
time: 68.3 us; the launch traced here: 68.1 us
  starting transfers between devices  24.2 us (35%)
  waiting for transfers between devices  22.7 us (33%)
  Pallas kernels  19.6 us (29%)
  between operations  1.54 us (2%)
    ppermute x8, starting transfers between devices, seq_pair(): return lax.ppermute(x, 'seq', [(i, i ^ k) for i in range(seqs)])  10.3 us
    ppermute x3, waiting for transfers between devices, tp_swap(): return lax.ppermute(x, 'tp', [(i, (i + 1) % tps) for i in range(tps)])  9.96 us
    ppermute x6, starting transfers between devices, yz_move(): return lax.ppermute(x, both, perm)  8.59 us
    ppermute x6, waiting for transfers between devices, yz_move(): return lax.ppermute(x, both, perm)  6.8 us
    ppermute x8, waiting for transfers between devices, seq_pair(): return lax.ppermute(x, 'seq', [(i, i ^ k) for i in range(seqs)])  5.95 us
    ppermute x3, starting transfers between devices, tp_swap(): return lax.ppermute(x, 'tp', [(i, (i + 1) % tps) for i in range(tps)])  4.7 us
    pallas_call x4, Pallas kernels, row(): call(functools.partial(row_kernel, requests, stacked, single), 'row', sta...  4.16 us
    pallas_call x1, Pallas kernels, local(): call(functools.partial(fetch_kernel, seqs, requests, dys), 'fetch', tuple...  3.41 us
  transfers between devices with their start and end apart: 18, of which 10 were waited for; matrix products, arithmetic and copies ran while one was open for 0% of the time, Pallas kernels for 20%

profile of v5, /device:TPU:0, one launch (start us, length us, event | category | flops | bytes accessed | tf_op | source)
XLA Modules:
  0.0 68.1 jit_solution(11808413076322372168)
XLA Ops:
  0.6 2.0 %first.1 = (bf16[96,512]{1,0:T(8,128)(2,1)S(1)}, bf16[96,1024]{1,0:T(8,128)(2,1)S(1)}, bf16[2,256,512]{2,1,0:T(8,128)(2,1)S(1)}, f32[96,32]{1,0:T(8,128)S(1)}) custom-call(bf16[2,32,1024]{2,1,0:T(8,128)(2,1)} %xs_hbm.1, bf16[1,32,1024]{2,1,0:T(8,128)(2,1)} %xl_hbm.1, bf16[3,1024,512]{2,1,0:T(8,128)(2,1)} %w_ref.1, bf16[1,2,256,512]{3,2,1,0:T(8,128)(2,1)} %kv_hbm.1, ...), custom_call_target="tpu_custom_call" | custom-call | flops 100000000 | bytes 1000000 | tf_op jit(solution)/shard_map/first/pallas_call | solution.py:506
  4.3 2.7 %collective-permute-start = (bf16[32,640]{1,0:T(8,128)(2,1)S(1)}, bf16[32,640]{1,0:T(8,128)(2,1)S(1)}, u32[]{:S(2)}, u32[]{:S(2)}) collective-permute-start(bf16[32,640]{1,0:T(8,128)(2,1)S(1)} %long.1.rest_0_), channel_id=1, source_target_pairs={{0,2},{2,0},{4,6},{6,4},{1,3},{3,1},{5,7},{7,5},{8,10},{10,8},{12,... | collective-permute-start | bytes 122888 | tf_op jit(solution)/shard_map/ppermute | solution.py:491
  6.9 2.6 %collective-permute-start.1 = (bf16[32,640]{1,0:T(8,128)(2,1)S(1)}, bf16[32,640]{1,0:T(8,128)(2,1)S(1)}, u32[]{:S(2)}, u32[]{:S(2)}) collective-permute-start(bf16[32,640]{1,0:T(8,128)(2,1)S(1)} %long.1.rest_0_), channel_id=1, source_target_pairs={{0,4},{2,6},{4,0},{6,2},{1,5},{3,7},{5,1},{7,3},{8,12},{10,14},{12... | collective-permute-start | bytes 122888 | tf_op jit(solution)/shard_map/ppermute | solution.py:491
  9.5 2.3 %attend.1 = (bf16[64,512]{1,0:T(8,128)(2,1)S(1)}, f32[32,512]{1,0:T(8,128)S(1)}, bf16[32,128]{1,0:T(8,128)(2,1)S(1)}) custom-call(bf16[96,512]{1,0:T(8,128)(2,1)S(1)} %get-tuple-element.49.q_ref, bf16[96,1024]{1,0:T(8,128)(2,1)S(1)} %get-tuple-element.47.x_ref, bf16[3,1024,512]{2,1,0:T(8,128)(2,1)S(1)} %copy-done.2, bf16[2,2,512,512]{3,2,1,0:T(8,128)(2,1)S(1)} %copy-done.6, ...), custom_call_target="tpu_custom_call" | custom-call | flops 4000000000 | bytes 1000000 | tf_op jit(solution)/shard_map/attend/pallas_call | solution.py:532
  11.9 0.8 %collective-permute-done.1.rest_2_ = bf16[32,640]{1,0:T(8,128)(2,1)S(1)} collective-permute-done((bf16[32,640]{1,0:T(8,128)(2,1)S(1)}, bf16[32,640]{1,0:T(8,128)(2,1)S(1)}, u32[]{:S(2)}, u32[]{:S(2)}) %collective-permute-start.1) | collective-permute-done | bytes 40992 | tf_op jit(solution)/shard_map/ppermute | solution.py:491
  12.7 2.6 %collective-permute-done.2.rest_3_ = bf16[32,640]{1,0:T(8,128)(2,1)S(1)} collective-permute-done((bf16[32,640]{1,0:T(8,128)(2,1)S(1)}, bf16[32,640]{1,0:T(8,128)(2,1)S(1)}, u32[]{:S(2)}, u32[]{:S(2)}) %collective-permute-start.2) | collective-permute-done | bytes 40992 | tf_op jit(solution)/shard_map/ppermute | solution.py:491
  15.8 1.6 %collective-permute-start.3 = (bf16[96,1024]{1,0:T(8,128)(2,1)S(1)}, bf16[96,1024]{1,0:T(8,128)(2,1)S(1)}, u32[]{:S(2)}, u32[]{:S(2)}) collective-permute-start(bf16[96,1024]{1,0:T(8,128)(2,1)S(1)} %output.1.a_ref), channel_id=1, source_target_pairs={{0,1},{1,0},{2,3},{3,2},{4,5},{5,4},{6,7},{7,6},{8,9},{9,8},{10,11... | collective-permute-start | bytes 589832 | tf_op jit(solution)/shard_map/ppermute | solution.py:503
  17.4 3.4 %fetch.1 = (bf16[9,2,128,512]{3,2,1,0:T(8,128)(2,1)S(1)}, bf16[9,2,128,512]{3,2,1,0:T(8,128)(2,1)S(1)}) custom-call(s32[32]{0:T(128)S(1)} %copy-done.7, s32[4]{0:T(128)S(1)} %copy-done.8, bf16[2,32,64,512]{3,2,1,0:T(8,128)(2,1)} %own_ref, bf16[2,32,64,512]{3,2,1,0:T(8,128)(2,1)S(1)} %collective-permute-done.4.other_ref), custom_call_target="tpu_custom_call" | custom-call | flops 4000000000 | bytes 1000000 | tf_op jit(solution)/shard_map/fetch/pallas_call | solution.py:552
  20.8 0.7 %collective-permute-done.3.b_ref = bf16[96,1024]{1,0:T(8,128)(2,1)S(1)} collective-permute-done((bf16[96,1024]{1,0:T(8,128)(2,1)S(1)}, bf16[96,1024]{1,0:T(8,128)(2,1)S(1)}, u32[]{:S(2)}, u32[]{:S(2)}) %collective-permute-start.3) | collective-permute-done | bytes 196640 | tf_op jit(solution)/shard_map/ppermute | solution.py:503
  22.1 1.9 %collective-permute-start.6 = (bf16[64,512]{1,0:T(8,128)(2,1)S(1)}, bf16[64,512]{1,0:T(8,128)(2,1)S(1)}, u32[]{:S(2)}, u32[]{:S(2)}) collective-permute-start(bf16[64,512]{1,0:T(8,128)(2,1)S(1)} %get-tuple-element.73), channel_id=1, source_target_pairs={{0,4},{2,6},{4,0},{6,2},{1,5},{3,7},{5,1},{7,3},{8,12},{10,14},{12... | collective-permute-start | bytes 196616 | tf_op jit(solution)/shard_map/ppermute | solution.py:491
  24.0 2.5 %collective-permute-start.7 = (bf16[64,512]{1,0:T(8,128)(2,1)S(1)}, bf16[64,512]{1,0:T(8,128)(2,1)S(1)}, u32[]{:S(2)}, u32[]{:S(2)}) collective-permute-start(bf16[64,512]{1,0:T(8,128)(2,1)S(1)} %get-tuple-element.73), channel_id=1, source_target_pairs={{0,6},{2,4},{4,2},{6,0},{1,7},{3,5},{5,3},{7,1},{8,14},{10,12},{12... | collective-permute-start | bytes 196616 | tf_op jit(solution)/shard_map/ppermute | solution.py:491
  26.5 1.5 %collective-permute-start.10 = (bf16[96,512]{1,0:T(8,128)(2,1)S(1)}, bf16[96,512]{1,0:T(8,128)(2,1)S(1)}, u32[]{:S(2)}, u32[]{:S(2)}) collective-permute-start(bf16[96,512]{1,0:T(8,128)(2,1)S(1)} %get-tuple-element.70.q_ref), channel_id=1, source_target_pairs={{0,16},{2,18},{4,20},{6,22},{8,24},{10,26},{12,28},{14,30},{16,0},... | collective-permute-start | bytes 294920 | tf_op jit(solution)/shard_map/ppermute | solution.py:500
  28.0 1.0 %near.2 = (bf16[104,512]{1,0:T(8,128)(2,1)S(1)}, bf16[32,512]{1,0:T(8,128)(2,1)S(1)}, f32[32,128]{1,0:T(8,128)S(1)}) custom-call(bf16[9,2,128,512]{3,2,1,0:T(8,128)(2,1)S(1)} %get-tuple-element.69.kv_ref, bf16[96,512]{1,0:T(8,128)(2,1)S(1)} %get-tuple-element.70.q_ref), custom_call_target="tpu_custom_call" | custom-call | flops 1000000000 | bytes 1000000 | tf_op jit(solution)/shard_map/near/pallas_call | solution.py:575
  29.1 1.0 %collective-permute-done.7 = bf16[64,512]{1,0:T(8,128)(2,1)S(1)} collective-permute-done((bf16[64,512]{1,0:T(8,128)(2,1)S(1)}, bf16[64,512]{1,0:T(8,128)(2,1)S(1)}, u32[]{:S(2)}, u32[]{:S(2)}) %collective-permute-start.7) | collective-permute-done | bytes 65568 | tf_op jit(solution)/shard_map/ppermute | solution.py:491
  30.1 1.6 %collective-permute-start.12 = (bf16[192,512]{1,0:T(8,128)(2,1)S(1)}, bf16[192,512]{1,0:T(8,128)(2,1)S(1)}, u32[]{:S(2)}, u32[]{:S(2)}) collective-permute-start(bf16[192,512]{1,0:T(8,128)(2,1)S(1)} %constant_dynamic-update-slice_fusion.q_ref), channel_id=1, source_target_pairs={{0,16},{2,18},{4,20},{6,22},{8,24},{10,26},{12,28},{14,30},{16,0},... | collective-permute-start | bytes 589832 | tf_op jit(solution)/shard_map/ppermute | solution.py:500
  31.7 1.3 %row.4 = bf16[2,104,512]{2,1,0:T(8,128)(2,1)S(1)} custom-call(bf16[9,2,128,512]{3,2,1,0:T(8,128)(2,1)S(1)} %get-tuple-element.69.kv_ref, bf16[32,512]{1,0:T(8,128)(2,1)S(1)} %get-tuple-element.71.o_ref, f32[32,128]{1,0:T(8,128)S(1)} %get-tuple-element.72.stat_ref, bf16[192,512]{1,0:T(8,128)(2,1)S(1)} %constant_dynamic-update-slice_fusion.q_ref), custom_call_target="tpu_custom_call" | custom-call | flops 1000000 | bytes 1000000 | tf_op jit(solution)/shard_map/row/pallas_call | solution.py:585
  33.1 0.7 %row.5.rest_1_ = bf16[104,512]{1,0:T(8,128)(2,1)S(1)} custom-call(bf16[9,2,128,512]{3,2,1,0:T(8,128)(2,1)S(1)} %get-tuple-element.69.kv_ref, bf16[32,512]{1,0:T(8,128)(2,1)S(1)} %get-tuple-element.71.o_ref, f32[32,128]{1,0:T(8,128)S(1)} %get-tuple-element.72.stat_ref, bf16[192,512]{1,0:T(8,128)(2,1)S(1)} %constant_dynamic-update-slice_fusion.q_ref), custom_call_target="tpu_custom_call" | custom-call | flops 1000000 | bytes 1000000 | tf_op jit(solution)/shard_map/row/pallas_call | solution.py:585
  33.9 1.0 %near.3 = (bf16[104,512]{1,0:T(8,128)(2,1)S(1)}, bf16[32,512]{1,0:T(8,128)(2,1)S(1)}, f32[32,128]{1,0:T(8,128)S(1)}) custom-call(bf16[9,2,128,512]{3,2,1,0:T(8,128)(2,1)S(1)} %get-tuple-element.81.kv_ref, bf16[96,512]{1,0:T(8,128)(2,1)S(1)} %collective-permute-done.10.q_ref), custom_call_target="tpu_custom_call" | custom-call | flops 10000000000 | bytes 1000000 | tf_op jit(solution)/shard_map/near/pallas_call | solution.py:575
  35.5 1.5 %collective-permute-done.12.q_ref = bf16[192,512]{1,0:T(8,128)(2,1)S(1)} collective-permute-done((bf16[192,512]{1,0:T(8,128)(2,1)S(1)}, bf16[192,512]{1,0:T(8,128)(2,1)S(1)}, u32[]{:S(2)}, u32[]{:S(2)}) %collective-permute-start.12) | collective-permute-done | bytes 196640 | tf_op jit(solution)/shard_map/ppermute | solution.py:500
  37.0 1.3 %row.6 = (bf16[1,104,512]{2,1,0:T(8,128)(2,1)S(1)}, bf16[104,512]{1,0:T(8,128)(2,1)S(1)}) custom-call(bf16[9,2,128,512]{3,2,1,0:T(8,128)(2,1)S(1)} %get-tuple-element.81.kv_ref, bf16[32,512]{1,0:T(8,128)(2,1)S(1)} %get-tuple-element.84.o_ref, f32[32,128]{1,0:T(8,128)S(1)} %get-tuple-element.85.stat_ref, bf16[192,512]{1,0:T(8,128)(2,1)S(1)} %collective-permute-done.12.q_ref), custom_call_target="tpu_custom_call" | custom-call | flops 10000000000 | bytes 1000000 | tf_op jit(solution)/shard_map/row/pallas_call | solution.py:585
  38.9 1.8 %collective-permute-start.13 = (bf16[104,512]{1,0:T(8,128)(2,1)S(1)}, bf16[104,512]{1,0:T(8,128)(2,1)S(1)}, u32[]{:S(2)}, u32[]{:S(2)}) collective-permute-start(bf16[104,512]{1,0:T(8,128)(2,1)S(1)} %get-tuple-element.87), channel_id=1, source_target_pairs={{0,18},{2,16},{4,22},{6,20},{8,26},{10,24},{12,30},{14,28},{16,2},... | collective-permute-start | bytes 319496 | tf_op jit(solution)/shard_map/ppermute | solution.py:500
  40.8 1.5 %collective-permute-done.8.odd_ref = bf16[2,104,512]{2,1,0:T(8,128)(2,1)S(1)} collective-permute-done((bf16[2,104,512]{2,1,0:T(8,128)(2,1)S(1)}, bf16[2,104,512]{2,1,0:T(8,128)(2,1)S(1)}, u32[]{:S(2)}, u32[]{:S(2)}) %collective-permute-start.8) | collective-permute-done | bytes 213024 | tf_op jit(solution)/shard_map/ppermute | solution.py:491
  44.5 2.4 %collective-permute-start.15 = (bf16[104,512]{1,0:T(8,128)(2,1)S(1)}, bf16[104,512]{1,0:T(8,128)(2,1)S(1)}, u32[]{:S(2)}, u32[]{:S(2)}) collective-permute-start(bf16[104,512]{1,0:T(8,128)(2,1)S(1)} %join.3), channel_id=1, source_target_pairs={{0,20},{2,22},{4,16},{6,18},{8,28},{10,30},{12,24},{14,26},{16,4},... | collective-permute-start | bytes 319496 | tf_op jit(solution)/shard_map/ppermute | solution.py:500
  46.9 1.7 %collective-permute-done.9.rest_1_ = bf16[104,512]{1,0:T(8,128)(2,1)S(1)} collective-permute-done((bf16[104,512]{1,0:T(8,128)(2,1)S(1)}, bf16[104,512]{1,0:T(8,128)(2,1)S(1)}, u32[]{:S(2)}, u32[]{:S(2)}) %collective-permute-start.9) | collective-permute-done | bytes 106528 | tf_op jit(solution)/shard_map/ppermute | solution.py:500
  48.6 3.6 %collective-permute-done.15.rest_4_ = bf16[104,512]{1,0:T(8,128)(2,1)S(1)} collective-permute-done((bf16[104,512]{1,0:T(8,128)(2,1)S(1)}, bf16[104,512]{1,0:T(8,128)(2,1)S(1)}, u32[]{:S(2)}, u32[]{:S(2)}) %collective-permute-start.15) | collective-permute-done | bytes 106528 | tf_op jit(solution)/shard_map/ppermute | solution.py:500
  52.2 0.9 %merge.1.a_ref = bf16[96,1024]{1,0:T(8,128)(2,1)S(1)} custom-call(bf16[512,1024]{1,0:T(8,128)(2,1)S(1)} %copy-done.3, bf16[104,512]{1,0:T(8,128)(2,1)S(1)} %get-tuple-element.79.rest_0_, bf16[104,512]{1,0:T(8,128)(2,1)S(1)} %collective-permute-done.9.rest_1_, bf16[104,512]{1,0:T(8,128)(2,1)S(1)} %collective-permute-done.11.rest_2_, ...), custom_call_target="tpu_custom_call" | custom-call | flops 100000000 | bytes 1000000 | tf_op jit(solution)/shard_map/merge/pallas_call | solution.py:627
  53.1 1.6 %collective-permute-start.16 = (bf16[96,1024]{1,0:T(8,128)(2,1)S(1)}, bf16[96,1024]{1,0:T(8,128)(2,1)S(1)}, u32[]{:S(2)}, u32[]{:S(2)}) collective-permute-start(bf16[96,1024]{1,0:T(8,128)(2,1)S(1)} %merge.1.a_ref), channel_id=1, source_target_pairs={{0,1},{1,0},{2,3},{3,2},{4,5},{5,4},{6,7},{7,6},{8,9},{9,8},{10,11... | collective-permute-start | bytes 589832 | tf_op jit(solution)/shard_map/ppermute | solution.py:503
  54.7 5.1 %collective-permute-done.16.b_ref = bf16[96,1024]{1,0:T(8,128)(2,1)S(1)} collective-permute-done((bf16[96,1024]{1,0:T(8,128)(2,1)S(1)}, bf16[96,1024]{1,0:T(8,128)(2,1)S(1)}, u32[]{:S(2)}, u32[]{:S(2)}) %collective-permute-start.16) | collective-permute-done | bytes 196640 | tf_op jit(solution)/shard_map/ppermute | solution.py:503
  59.7 1.7 %ffn.1 = (bf16[96,1024]{1,0:T(8,128)(2,1)S(1)}, bf16[96,1024]{1,0:T(8,128)(2,1)S(1)}) custom-call(bf16[96,1024]{1,0:T(8,128)(2,1)S(1)} %get-tuple-element.68.h_ref, bf16[96,1024]{1,0:T(8,128)(2,1)S(1)} %merge.1.a_ref, bf16[96,1024]{1,0:T(8,128)(2,1)S(1)} %collective-permute-done.16.b_ref, bf16[1024,2048]{1,0:T(8,128)(2,1)S(1)} %copy-done, ...), custom_call_target="tpu_custom_call" | custom-call | flops 100000000 | bytes 1000000 | tf_op jit(solution)/shard_map/ffn/pallas_call | solution.py:639
  61.5 1.6 %collective-permute-start.17 = (bf16[96,1024]{1,0:T(8,128)(2,1)S(1)}, bf16[96,1024]{1,0:T(8,128)(2,1)S(1)}, u32[]{:S(2)}, u32[]{:S(2)}) collective-permute-start(bf16[96,1024]{1,0:T(8,128)(2,1)S(1)} %get-tuple-element.91.a_ref), channel_id=1, source_target_pairs={{0,1},{1,0},{2,3},{3,2},{4,5},{5,4},{6,7},{7,6},{8,9},{9,8},{10,11... | collective-permute-start | bytes 589832 | tf_op jit(solution)/shard_map/ppermute | solution.py:503
  63.1 4.1 %collective-permute-done.17.b_ref = bf16[96,1024]{1,0:T(8,128)(2,1)S(1)} collective-permute-done((bf16[96,1024]{1,0:T(8,128)(2,1)S(1)}, bf16[96,1024]{1,0:T(8,128)(2,1)S(1)}, u32[]{:S(2)}, u32[]{:S(2)}) %collective-permute-start.17) | collective-permute-done | bytes 196640 | tf_op jit(solution)/shard_map/ppermute | solution.py:503
  67.2 0.9 %final.1 = (bf16[2,32,1024]{2,1,0:T(8,128)(2,1)}, bf16[1,32,1024]{2,1,0:T(8,128)(2,1)}) custom-call(bf16[96,1024]{1,0:T(8,128)(2,1)S(1)} %get-tuple-element.90.h_ref, bf16[96,1024]{1,0:T(8,128)(2,1)S(1)} %get-tuple-element.91.a_ref, bf16[96,1024]{1,0:T(8,128)(2,1)S(1)} %collective-permute-done.17.b_ref), custom_call_target="tpu_custom_call" | custom-call | flops 100000000 | bytes 1000000 | tf_op jit(solution)/shard_map/final/pallas_call | solution.py:643
  (43 shorter events, 5.5 us)
Async XLA Ops:
  2.6 14.8 %collective-permute-start.4 = (bf16[2,32,64,512]{3,2,1,0:T(8,128)(2,1)}, bf16[2,32,64,512]{3,2,1,0:T(8,128)(2,1)S(1)}, u32[]{:S(2)}, u32[]{:S(2)}) collective-permute-start(bf16[2,32,64,512]{3,2,1,0:T(8,128)(2,1)} %own_ref), channel_id=1, source_target_pairs={{0,8},{8,0},{16,24},{24,16},{1,9},{9,1},{17,25},{25,17},{2,10},{10... | collective-permute-start | bytes 12582920 | tf_op jit(solution)/shard_map/ppermute | solution.py:530
  3.8 5.7 %copy-start.2 = (bf16[3,1024,512]{2,1,0:T(8,128)(2,1)S(1)}, bf16[3,1024,512]{2,1,0:T(8,128)(2,1)}, u32[]{:S(2)}) copy-start(bf16[3,1024,512]{2,1,0:T(8,128)(2,1)} %w_ref.1) | copy-start | bytes 9437188
  3.8 5.7 %copy-start.6 = (bf16[2,2,512,512]{3,2,1,0:T(8,128)(2,1)S(1)}, bf16[2,2,512,512]{3,2,1,0:T(8,128)(2,1)}, u32[]{:S(2)}) copy-start(bf16[2,2,512,512]{3,2,1,0:T(8,128)(2,1)} %skv_ref) | copy-start | bytes 6291460
  4.3 7.6 %collective-permute-start = (bf16[32,640]{1,0:T(8,128)(2,1)S(1)}, bf16[32,640]{1,0:T(8,128)(2,1)S(1)}, u32[]{:S(2)}, u32[]{:S(2)}) collective-permute-start(bf16[32,640]{1,0:T(8,128)(2,1)S(1)} %long.1.rest_0_), channel_id=1, source_target_pairs={{0,2},{2,0},{4,6},{6,4},{1,3},{3,1},{5,7},{7,5},{8,10},{10,8},{12,... | collective-permute-start | bytes 122888 | tf_op jit(solution)/shard_map/ppermute | solution.py:491
  6.9 5.8 %collective-permute-start.1 = (bf16[32,640]{1,0:T(8,128)(2,1)S(1)}, bf16[32,640]{1,0:T(8,128)(2,1)S(1)}, u32[]{:S(2)}, u32[]{:S(2)}) collective-permute-start(bf16[32,640]{1,0:T(8,128)(2,1)S(1)} %long.1.rest_0_), channel_id=1, source_target_pairs={{0,4},{2,6},{4,0},{6,2},{1,5},{3,7},{5,1},{7,3},{8,12},{10,14},{12... | collective-permute-start | bytes 122888 | tf_op jit(solution)/shard_map/ppermute | solution.py:491
  9.5 5.8 %collective-permute-start.2 = (bf16[32,640]{1,0:T(8,128)(2,1)S(1)}, bf16[32,640]{1,0:T(8,128)(2,1)S(1)}, u32[]{:S(2)}, u32[]{:S(2)}) collective-permute-start(bf16[32,640]{1,0:T(8,128)(2,1)S(1)} %long.1.rest_0_), channel_id=1, source_target_pairs={{0,6},{2,4},{4,2},{6,0},{1,7},{3,5},{5,3},{7,1},{8,14},{10,12},{12... | collective-permute-start | bytes 122888 | tf_op jit(solution)/shard_map/ppermute | solution.py:491
  9.5 5.8 %copy-start.4 = (bf16[512,1024]{1,0:T(8,128)(2,1)S(1)}, bf16[512,1024]{1,0:T(8,128)(2,1)}, u32[]{:S(2)}) copy-start(bf16[512,1024]{1,0:T(8,128)(2,1)} %wo_ref) | copy-start | bytes 3145732
  9.5 7.8 %copy-start.7 = (s32[32]{0:T(128)S(1)}, s32[32]{0:T(128)}, u32[]{:S(2)}) copy-start(s32[32]{0:T(128)} %doc_ref) | copy-start | bytes 388
  9.5 7.8 %copy-start.8 = (s32[4]{0:T(128)S(1)}, s32[4]{0:T(128)}, u32[]{:S(2)}) copy-start(s32[4]{0:T(128)} %long_ref.1) | copy-start | bytes 52
  15.8 5.8 %copy-start.5 = (bf16[1024,512]{1,0:T(8,128)(2,1)S(1)}, bf16[1024,512]{1,0:T(8,128)(2,1)}, u32[]{:S(2)}) copy-start(bf16[1024,512]{1,0:T(8,128)(2,1)} %w_ref.2) | copy-start | bytes 3145732
  15.8 5.7 %collective-permute-start.3 = (bf16[96,1024]{1,0:T(8,128)(2,1)S(1)}, bf16[96,1024]{1,0:T(8,128)(2,1)S(1)}, u32[]{:S(2)}, u32[]{:S(2)}) collective-permute-start(bf16[96,1024]{1,0:T(8,128)(2,1)S(1)} %output.1.a_ref), channel_id=1, source_target_pairs={{0,1},{1,0},{2,3},{3,2},{4,5},{5,4},{6,7},{7,6},{8,9},{9,8},{10,11... | collective-permute-start | bytes 589832 | tf_op jit(solution)/shard_map/ppermute | solution.py:503
  22.0 7.0 %collective-permute-start.5 = (bf16[64,512]{1,0:T(8,128)(2,1)S(1)}, bf16[64,512]{1,0:T(8,128)(2,1)S(1)}, u32[]{:S(2)}, u32[]{:S(2)}) collective-permute-start(bf16[64,512]{1,0:T(8,128)(2,1)S(1)} %get-tuple-element.73), channel_id=1, source_target_pairs={{0,2},{2,0},{4,6},{6,4},{1,3},{3,1},{5,7},{7,5},{8,10},{10,8},{12,... | collective-permute-start | bytes 196616 | tf_op jit(solution)/shard_map/ppermute | solution.py:491
  22.1 7.0 %collective-permute-start.6 = (bf16[64,512]{1,0:T(8,128)(2,1)S(1)}, bf16[64,512]{1,0:T(8,128)(2,1)S(1)}, u32[]{:S(2)}, u32[]{:S(2)}) collective-permute-start(bf16[64,512]{1,0:T(8,128)(2,1)S(1)} %get-tuple-element.73), channel_id=1, source_target_pairs={{0,4},{2,6},{4,0},{6,2},{1,5},{3,7},{5,1},{7,3},{8,12},{10,14},{12... | collective-permute-start | bytes 196616 | tf_op jit(solution)/shard_map/ppermute | solution.py:491
  24.0 6.1 %collective-permute-start.7 = (bf16[64,512]{1,0:T(8,128)(2,1)S(1)}, bf16[64,512]{1,0:T(8,128)(2,1)S(1)}, u32[]{:S(2)}, u32[]{:S(2)}) collective-permute-start(bf16[64,512]{1,0:T(8,128)(2,1)S(1)} %get-tuple-element.73), channel_id=1, source_target_pairs={{0,6},{2,4},{4,2},{6,0},{1,7},{3,5},{5,3},{7,1},{8,14},{10,12},{12... | collective-permute-start | bytes 196616 | tf_op jit(solution)/shard_map/ppermute | solution.py:491
  26.5 7.4 %collective-permute-start.10 = (bf16[96,512]{1,0:T(8,128)(2,1)S(1)}, bf16[96,512]{1,0:T(8,128)(2,1)S(1)}, u32[]{:S(2)}, u32[]{:S(2)}) collective-permute-start(bf16[96,512]{1,0:T(8,128)(2,1)S(1)} %get-tuple-element.70.q_ref), channel_id=1, source_target_pairs={{0,16},{2,18},{4,20},{6,22},{8,24},{10,26},{12,28},{14,30},{16,0},... | collective-permute-start | bytes 294920 | tf_op jit(solution)/shard_map/ppermute | solution.py:500
  30.1 6.9 %collective-permute-start.12 = (bf16[192,512]{1,0:T(8,128)(2,1)S(1)}, bf16[192,512]{1,0:T(8,128)(2,1)S(1)}, u32[]{:S(2)}, u32[]{:S(2)}) collective-permute-start(bf16[192,512]{1,0:T(8,128)(2,1)S(1)} %constant_dynamic-update-slice_fusion.q_ref), channel_id=1, source_target_pairs={{0,16},{2,18},{4,20},{6,22},{8,24},{10,26},{12,28},{14,30},{16,0},... | collective-permute-start | bytes 589832 | tf_op jit(solution)/shard_map/ppermute | solution.py:500
  33.1 9.2 %collective-permute-start.8 = (bf16[2,104,512]{2,1,0:T(8,128)(2,1)S(1)}, bf16[2,104,512]{2,1,0:T(8,128)(2,1)S(1)}, u32[]{:S(2)}, u32[]{:S(2)}) collective-permute-start(bf16[2,104,512]{2,1,0:T(8,128)(2,1)S(1)} %row.4), channel_id=1, source_target_pairs={{0,2},{2,0},{4,6},{6,4},{1,3},{3,1},{5,7},{7,5},{8,10},{10,8},{12,... | collective-permute-start | bytes 638984 | tf_op jit(solution)/shard_map/ppermute | solution.py:491
  34.9 12.0 %collective-permute-start.11 = (bf16[104,512]{1,0:T(8,128)(2,1)S(1)}, bf16[104,512]{1,0:T(8,128)(2,1)S(1)}, u32[]{:S(2)}, u32[]{:S(2)}) collective-permute-start(bf16[104,512]{1,0:T(8,128)(2,1)S(1)} %get-tuple-element.83), channel_id=1, source_target_pairs={{0,16},{2,18},{4,20},{6,22},{8,24},{10,26},{12,28},{14,30},{16,0},... | collective-permute-start | bytes 319496 | tf_op jit(solution)/shard_map/ppermute | solution.py:500
  38.3 5.9 %collective-permute-start.14 = (bf16[1,104,512]{2,1,0:T(8,128)(2,1)S(1)}, bf16[1,104,512]{2,1,0:T(8,128)(2,1)S(1)}, u32[]{:S(2)}, u32[]{:S(2)}) collective-permute-start(bf16[1,104,512]{2,1,0:T(8,128)(2,1)S(1)} %get-tuple-element.88), channel_id=1, source_target_pairs={{0,2},{2,0},{4,6},{6,4},{1,3},{3,1},{5,7},{7,5},{8,10},{10,8},{12,... | collective-permute-start | bytes 319496 | tf_op jit(solution)/shard_map/ppermute | solution.py:491
  38.9 8.0 %collective-permute-start.13 = (bf16[104,512]{1,0:T(8,128)(2,1)S(1)}, bf16[104,512]{1,0:T(8,128)(2,1)S(1)}, u32[]{:S(2)}, u32[]{:S(2)}) collective-permute-start(bf16[104,512]{1,0:T(8,128)(2,1)S(1)} %get-tuple-element.87), channel_id=1, source_target_pairs={{0,18},{2,16},{4,22},{6,20},{8,26},{10,24},{12,30},{14,28},{16,2},... | collective-permute-start | bytes 319496 | tf_op jit(solution)/shard_map/ppermute | solution.py:500
  42.8 5.9 %collective-permute-start.9 = (bf16[104,512]{1,0:T(8,128)(2,1)S(1)}, bf16[104,512]{1,0:T(8,128)(2,1)S(1)}, u32[]{:S(2)}, u32[]{:S(2)}) collective-permute-start(bf16[104,512]{1,0:T(8,128)(2,1)S(1)} %get-tuple-element.80), channel_id=1, source_target_pairs={{0,4},{2,6},{4,0},{6,2},{8,12},{10,14},{12,8},{14,10},{16,20},{18,... | collective-permute-start | bytes 319496 | tf_op jit(solution)/shard_map/ppermute | solution.py:500
  44.2 8.0 %copy-start.3 = (bf16[512,1024]{1,0:T(8,128)(2,1)S(1)}, bf16[512,1024]{1,0:T(8,128)(2,1)}, u32[]{:S(2)}) copy-start(bf16[512,1024]{1,0:T(8,128)(2,1)} %w_ref.3) | copy-start | bytes 3145732
  44.2 15.5 %copy-start = (bf16[1024,2048]{1,0:T(8,128)(2,1)S(1)}, bf16[1024,2048]{1,0:T(8,128)(2,1)}, u32[]{:S(2)}) copy-start(bf16[1024,2048]{1,0:T(8,128)(2,1)} %up_ref.1) | copy-start | bytes 12582916
  44.2 15.5 %copy-start.1 = (bf16[2048,1024]{1,0:T(8,128)(2,1)S(1)}, bf16[2048,1024]{1,0:T(8,128)(2,1)}, u32[]{:S(2)}) copy-start(bf16[2048,1024]{1,0:T(8,128)(2,1)} %down_ref.1) | copy-start | bytes 12582916
  44.5 7.7 %collective-permute-start.15 = (bf16[104,512]{1,0:T(8,128)(2,1)S(1)}, bf16[104,512]{1,0:T(8,128)(2,1)S(1)}, u32[]{:S(2)}, u32[]{:S(2)}) collective-permute-start(bf16[104,512]{1,0:T(8,128)(2,1)S(1)} %join.3), channel_id=1, source_target_pairs={{0,20},{2,22},{4,16},{6,18},{8,28},{10,30},{12,24},{14,26},{16,4},... | collective-permute-start | bytes 319496 | tf_op jit(solution)/shard_map/ppermute | solution.py:500
  53.1 6.6 %collective-permute-start.16 = (bf16[96,1024]{1,0:T(8,128)(2,1)S(1)}, bf16[96,1024]{1,0:T(8,128)(2,1)S(1)}, u32[]{:S(2)}, u32[]{:S(2)}) collective-permute-start(bf16[96,1024]{1,0:T(8,128)(2,1)S(1)} %merge.1.a_ref), channel_id=1, source_target_pairs={{0,1},{1,0},{2,3},{3,2},{4,5},{5,4},{6,7},{7,6},{8,9},{9,8},{10,11... | collective-permute-start | bytes 589832 | tf_op jit(solution)/shard_map/ppermute | solution.py:503
  61.5 5.7 %collective-permute-start.17 = (bf16[96,1024]{1,0:T(8,128)(2,1)S(1)}, bf16[96,1024]{1,0:T(8,128)(2,1)S(1)}, u32[]{:S(2)}, u32[]{:S(2)}) collective-permute-start(bf16[96,1024]{1,0:T(8,128)(2,1)S(1)} %get-tuple-element.91.a_ref), channel_id=1, source_target_pairs={{0,1},{1,0},{2,3},{3,2},{4,5},{5,4},{6,7},{7,6},{8,9},{9,8},{10,11... | collective-permute-start | bytes 589832 | tf_op jit(solution)/shard_map/ppermute | solution.py:503

commit v6 on v5

--- a/solution.py
+++ b/solution.py
@@ -12,7 +12,7 @@
 CORES = 2
 PIECES = 3
 SLOTS = 4
-CHUNK = 1024
+CHUNK = 2048
 OWN = 10**6
 FAR = 10**10
 MASKED = -1e30

time: 68.3 us -> 68.3 us (level)
  no operation moved by 1% of the time
where the time goes in v6:
time: 68.3 us; the launch traced here: 68.1 us
  starting transfers between devices  24.2 us (35%)
  waiting for transfers between devices  22.7 us (33%)
  Pallas kernels  19.6 us (29%)
  between operations  1.54 us (2%)
    ppermute x8, starting transfers between devices, seq_pair(): return lax.ppermute(x, 'seq', [(i, i ^ k) for i in range(seqs)])  10.3 us
    ppermute x3, waiting for transfers between devices, tp_swap(): return lax.ppermute(x, 'tp', [(i, (i + 1) % tps) for i in range(tps)])  9.94 us
    ppermute x6, starting transfers between devices, yz_move(): return lax.ppermute(x, both, perm)  8.59 us
    ppermute x6, waiting for transfers between devices, yz_move(): return lax.ppermute(x, both, perm)  6.8 us
    ppermute x8, waiting for transfers between devices, seq_pair(): return lax.ppermute(x, 'seq', [(i, i ^ k) for i in range(seqs)])  5.95 us
    ppermute x3, starting transfers between devices, tp_swap(): return lax.ppermute(x, 'tp', [(i, (i + 1) % tps) for i in range(tps)])  4.7 us
    pallas_call x4, Pallas kernels, row(): call(functools.partial(row_kernel, requests, stacked, single), 'row', sta...  4.16 us
    pallas_call x1, Pallas kernels, local(): call(functools.partial(fetch_kernel, seqs, requests, dys), 'fetch', tuple...  3.41 us
  transfers between devices with their start and end apart: 18, of which 10 were waited for; matrix products, arithmetic and copies ran while one was open for 0% of the time, Pallas kernels for 20%

profile of v6, /device:TPU:0, one launch (start us, length us, event | category | flops | bytes accessed | tf_op | source)
XLA Modules:
  0.0 68.1 jit_solution(15943491565808775695)
XLA Ops:
  0.6 2.0 %first.1 = (bf16[96,512]{1,0:T(8,128)(2,1)S(1)}, bf16[96,1024]{1,0:T(8,128)(2,1)S(1)}, bf16[2,256,512]{2,1,0:T(8,128)(2,1)S(1)}, f32[96,32]{1,0:T(8,128)S(1)}) custom-call(bf16[2,32,1024]{2,1,0:T(8,128)(2,1)} %xs_hbm.1, bf16[1,32,1024]{2,1,0:T(8,128)(2,1)} %xl_hbm.1, bf16[3,1024,512]{2,1,0:T(8,128)(2,1)} %w_ref.1, bf16[1,2,256,512]{3,2,1,0:T(8,128)(2,1)} %kv_hbm.1, ...), custom_call_target="tpu_custom_call" | custom-call | flops 100000000 | bytes 1000000 | tf_op jit(solution)/shard_map/first/pallas_call | solution.py:506
  4.3 2.7 %collective-permute-start = (bf16[32,640]{1,0:T(8,128)(2,1)S(1)}, bf16[32,640]{1,0:T(8,128)(2,1)S(1)}, u32[]{:S(2)}, u32[]{:S(2)}) collective-permute-start(bf16[32,640]{1,0:T(8,128)(2,1)S(1)} %long.1.rest_0_), channel_id=1, source_target_pairs={{0,2},{2,0},{4,6},{6,4},{1,3},{3,1},{5,7},{7,5},{8,10},{10,8},{12,... | collective-permute-start | bytes 122888 | tf_op jit(solution)/shard_map/ppermute | solution.py:491
  6.9 2.6 %collective-permute-start.1 = (bf16[32,640]{1,0:T(8,128)(2,1)S(1)}, bf16[32,640]{1,0:T(8,128)(2,1)S(1)}, u32[]{:S(2)}, u32[]{:S(2)}) collective-permute-start(bf16[32,640]{1,0:T(8,128)(2,1)S(1)} %long.1.rest_0_), channel_id=1, source_target_pairs={{0,4},{2,6},{4,0},{6,2},{1,5},{3,7},{5,1},{7,3},{8,12},{10,14},{12... | collective-permute-start | bytes 122888 | tf_op jit(solution)/shard_map/ppermute | solution.py:491
  9.5 2.3 %attend.1 = (bf16[64,512]{1,0:T(8,128)(2,1)S(1)}, f32[32,512]{1,0:T(8,128)S(1)}, bf16[32,128]{1,0:T(8,128)(2,1)S(1)}) custom-call(bf16[96,512]{1,0:T(8,128)(2,1)S(1)} %get-tuple-element.49.q_ref, bf16[96,1024]{1,0:T(8,128)(2,1)S(1)} %get-tuple-element.47.x_ref, bf16[3,1024,512]{2,1,0:T(8,128)(2,1)S(1)} %copy-done.2, bf16[2,2,512,512]{3,2,1,0:T(8,128)(2,1)S(1)} %copy-done.6, ...), custom_call_target="tpu_custom_call" | custom-call | flops 4000000000 | bytes 1000000 | tf_op jit(solution)/shard_map/attend/pallas_call | solution.py:532
  11.9 0.8 %collective-permute-done.1.rest_2_ = bf16[32,640]{1,0:T(8,128)(2,1)S(1)} collective-permute-done((bf16[32,640]{1,0:T(8,128)(2,1)S(1)}, bf16[32,640]{1,0:T(8,128)(2,1)S(1)}, u32[]{:S(2)}, u32[]{:S(2)}) %collective-permute-start.1) | collective-permute-done | bytes 40992 | tf_op jit(solution)/shard_map/ppermute | solution.py:491
  12.7 2.6 %collective-permute-done.2.rest_3_ = bf16[32,640]{1,0:T(8,128)(2,1)S(1)} collective-permute-done((bf16[32,640]{1,0:T(8,128)(2,1)S(1)}, bf16[32,640]{1,0:T(8,128)(2,1)S(1)}, u32[]{:S(2)}, u32[]{:S(2)}) %collective-permute-start.2) | collective-permute-done | bytes 40992 | tf_op jit(solution)/shard_map/ppermute | solution.py:491
  15.8 1.6 %collective-permute-start.3 = (bf16[96,1024]{1,0:T(8,128)(2,1)S(1)}, bf16[96,1024]{1,0:T(8,128)(2,1)S(1)}, u32[]{:S(2)}, u32[]{:S(2)}) collective-permute-start(bf16[96,1024]{1,0:T(8,128)(2,1)S(1)} %output.1.a_ref), channel_id=1, source_target_pairs={{0,1},{1,0},{2,3},{3,2},{4,5},{5,4},{6,7},{7,6},{8,9},{9,8},{10,11... | collective-permute-start | bytes 589832 | tf_op jit(solution)/shard_map/ppermute | solution.py:503
  17.4 3.4 %fetch.1 = (bf16[9,2,128,512]{3,2,1,0:T(8,128)(2,1)S(1)}, bf16[9,2,128,512]{3,2,1,0:T(8,128)(2,1)S(1)}) custom-call(s32[32]{0:T(128)S(1)} %copy-done.7, s32[4]{0:T(128)S(1)} %copy-done.8, bf16[2,32,64,512]{3,2,1,0:T(8,128)(2,1)} %own_ref, bf16[2,32,64,512]{3,2,1,0:T(8,128)(2,1)S(1)} %collective-permute-done.4.other_ref), custom_call_target="tpu_custom_call" | custom-call | flops 4000000000 | bytes 1000000 | tf_op jit(solution)/shard_map/fetch/pallas_call | solution.py:552
  20.8 0.7 %collective-permute-done.3.b_ref = bf16[96,1024]{1,0:T(8,128)(2,1)S(1)} collective-permute-done((bf16[96,1024]{1,0:T(8,128)(2,1)S(1)}, bf16[96,1024]{1,0:T(8,128)(2,1)S(1)}, u32[]{:S(2)}, u32[]{:S(2)}) %collective-permute-start.3) | collective-permute-done | bytes 196640 | tf_op jit(solution)/shard_map/ppermute | solution.py:503
  22.1 1.9 %collective-permute-start.6 = (bf16[64,512]{1,0:T(8,128)(2,1)S(1)}, bf16[64,512]{1,0:T(8,128)(2,1)S(1)}, u32[]{:S(2)}, u32[]{:S(2)}) collective-permute-start(bf16[64,512]{1,0:T(8,128)(2,1)S(1)} %get-tuple-element.73), channel_id=1, source_target_pairs={{0,4},{2,6},{4,0},{6,2},{1,5},{3,7},{5,1},{7,3},{8,12},{10,14},{12... | collective-permute-start | bytes 196616 | tf_op jit(solution)/shard_map/ppermute | solution.py:491
  24.0 2.5 %collective-permute-start.7 = (bf16[64,512]{1,0:T(8,128)(2,1)S(1)}, bf16[64,512]{1,0:T(8,128)(2,1)S(1)}, u32[]{:S(2)}, u32[]{:S(2)}) collective-permute-start(bf16[64,512]{1,0:T(8,128)(2,1)S(1)} %get-tuple-element.73), channel_id=1, source_target_pairs={{0,6},{2,4},{4,2},{6,0},{1,7},{3,5},{5,3},{7,1},{8,14},{10,12},{12... | collective-permute-start | bytes 196616 | tf_op jit(solution)/shard_map/ppermute | solution.py:491
  26.5 1.5 %collective-permute-start.10 = (bf16[96,512]{1,0:T(8,128)(2,1)S(1)}, bf16[96,512]{1,0:T(8,128)(2,1)S(1)}, u32[]{:S(2)}, u32[]{:S(2)}) collective-permute-start(bf16[96,512]{1,0:T(8,128)(2,1)S(1)} %get-tuple-element.70.q_ref), channel_id=1, source_target_pairs={{0,16},{2,18},{4,20},{6,22},{8,24},{10,26},{12,28},{14,30},{16,0},... | collective-permute-start | bytes 294920 | tf_op jit(solution)/shard_map/ppermute | solution.py:500
  28.0 1.0 %near.2 = (bf16[104,512]{1,0:T(8,128)(2,1)S(1)}, bf16[32,512]{1,0:T(8,128)(2,1)S(1)}, f32[32,128]{1,0:T(8,128)S(1)}) custom-call(bf16[9,2,128,512]{3,2,1,0:T(8,128)(2,1)S(1)} %get-tuple-element.69.kv_ref, bf16[96,512]{1,0:T(8,128)(2,1)S(1)} %get-tuple-element.70.q_ref), custom_call_target="tpu_custom_call" | custom-call | flops 1000000000 | bytes 1000000 | tf_op jit(solution)/shard_map/near/pallas_call | solution.py:575
  29.1 1.0 %collective-permute-done.7 = bf16[64,512]{1,0:T(8,128)(2,1)S(1)} collective-permute-done((bf16[64,512]{1,0:T(8,128)(2,1)S(1)}, bf16[64,512]{1,0:T(8,128)(2,1)S(1)}, u32[]{:S(2)}, u32[]{:S(2)}) %collective-permute-start.7) | collective-permute-done | bytes 65568 | tf_op jit(solution)/shard_map/ppermute | solution.py:491
  30.1 1.6 %collective-permute-start.12 = (bf16[192,512]{1,0:T(8,128)(2,1)S(1)}, bf16[192,512]{1,0:T(8,128)(2,1)S(1)}, u32[]{:S(2)}, u32[]{:S(2)}) collective-permute-start(bf16[192,512]{1,0:T(8,128)(2,1)S(1)} %constant_dynamic-update-slice_fusion.q_ref), channel_id=1, source_target_pairs={{0,16},{2,18},{4,20},{6,22},{8,24},{10,26},{12,28},{14,30},{16,0},... | collective-permute-start | bytes 589832 | tf_op jit(solution)/shard_map/ppermute | solution.py:500
  31.7 1.3 %row.4 = bf16[2,104,512]{2,1,0:T(8,128)(2,1)S(1)} custom-call(bf16[9,2,128,512]{3,2,1,0:T(8,128)(2,1)S(1)} %get-tuple-element.69.kv_ref, bf16[32,512]{1,0:T(8,128)(2,1)S(1)} %get-tuple-element.71.o_ref, f32[32,128]{1,0:T(8,128)S(1)} %get-tuple-element.72.stat_ref, bf16[192,512]{1,0:T(8,128)(2,1)S(1)} %constant_dynamic-update-slice_fusion.q_ref), custom_call_target="tpu_custom_call" | custom-call | flops 1000000 | bytes 1000000 | tf_op jit(solution)/shard_map/row/pallas_call | solution.py:585
  33.1 0.7 %row.5.rest_1_ = bf16[104,512]{1,0:T(8,128)(2,1)S(1)} custom-call(bf16[9,2,128,512]{3,2,1,0:T(8,128)(2,1)S(1)} %get-tuple-element.69.kv_ref, bf16[32,512]{1,0:T(8,128)(2,1)S(1)} %get-tuple-element.71.o_ref, f32[32,128]{1,0:T(8,128)S(1)} %get-tuple-element.72.stat_ref, bf16[192,512]{1,0:T(8,128)(2,1)S(1)} %constant_dynamic-update-slice_fusion.q_ref), custom_call_target="tpu_custom_call" | custom-call | flops 1000000 | bytes 1000000 | tf_op jit(solution)/shard_map/row/pallas_call | solution.py:585
  33.9 1.0 %near.3 = (bf16[104,512]{1,0:T(8,128)(2,1)S(1)}, bf16[32,512]{1,0:T(8,128)(2,1)S(1)}, f32[32,128]{1,0:T(8,128)S(1)}) custom-call(bf16[9,2,128,512]{3,2,1,0:T(8,128)(2,1)S(1)} %get-tuple-element.81.kv_ref, bf16[96,512]{1,0:T(8,128)(2,1)S(1)} %collective-permute-done.10.q_ref), custom_call_target="tpu_custom_call" | custom-call | flops 10000000000 | bytes 1000000 | tf_op jit(solution)/shard_map/near/pallas_call | solution.py:575
  35.5 1.5 %collective-permute-done.12.q_ref = bf16[192,512]{1,0:T(8,128)(2,1)S(1)} collective-permute-done((bf16[192,512]{1,0:T(8,128)(2,1)S(1)}, bf16[192,512]{1,0:T(8,128)(2,1)S(1)}, u32[]{:S(2)}, u32[]{:S(2)}) %collective-permute-start.12) | collective-permute-done | bytes 196640 | tf_op jit(solution)/shard_map/ppermute | solution.py:500
  37.0 1.3 %row.6 = (bf16[1,104,512]{2,1,0:T(8,128)(2,1)S(1)}, bf16[104,512]{1,0:T(8,128)(2,1)S(1)}) custom-call(bf16[9,2,128,512]{3,2,1,0:T(8,128)(2,1)S(1)} %get-tuple-element.81.kv_ref, bf16[32,512]{1,0:T(8,128)(2,1)S(1)} %get-tuple-element.84.o_ref, f32[32,128]{1,0:T(8,128)S(1)} %get-tuple-element.85.stat_ref, bf16[192,512]{1,0:T(8,128)(2,1)S(1)} %collective-permute-done.12.q_ref), custom_call_target="tpu_custom_call" | custom-call | flops 10000000000 | bytes 1000000 | tf_op jit(solution)/shard_map/row/pallas_call | solution.py:585
  38.9 1.8 %collective-permute-start.13 = (bf16[104,512]{1,0:T(8,128)(2,1)S(1)}, bf16[104,512]{1,0:T(8,128)(2,1)S(1)}, u32[]{:S(2)}, u32[]{:S(2)}) collective-permute-start(bf16[104,512]{1,0:T(8,128)(2,1)S(1)} %get-tuple-element.87), channel_id=1, source_target_pairs={{0,18},{2,16},{4,22},{6,20},{8,26},{10,24},{12,30},{14,28},{16,2},... | collective-permute-start | bytes 319496 | tf_op jit(solution)/shard_map/ppermute | solution.py:500
  40.8 1.5 %collective-permute-done.8.odd_ref = bf16[2,104,512]{2,1,0:T(8,128)(2,1)S(1)} collective-permute-done((bf16[2,104,512]{2,1,0:T(8,128)(2,1)S(1)}, bf16[2,104,512]{2,1,0:T(8,128)(2,1)S(1)}, u32[]{:S(2)}, u32[]{:S(2)}) %collective-permute-start.8) | collective-permute-done | bytes 213024 | tf_op jit(solution)/shard_map/ppermute | solution.py:491
  44.5 2.4 %collective-permute-start.15 = (bf16[104,512]{1,0:T(8,128)(2,1)S(1)}, bf16[104,512]{1,0:T(8,128)(2,1)S(1)}, u32[]{:S(2)}, u32[]{:S(2)}) collective-permute-start(bf16[104,512]{1,0:T(8,128)(2,1)S(1)} %join.3), channel_id=1, source_target_pairs={{0,20},{2,22},{4,16},{6,18},{8,28},{10,30},{12,24},{14,26},{16,4},... | collective-permute-start | bytes 319496 | tf_op jit(solution)/shard_map/ppermute | solution.py:500
  46.9 1.7 %collective-permute-done.9.rest_1_ = bf16[104,512]{1,0:T(8,128)(2,1)S(1)} collective-permute-done((bf16[104,512]{1,0:T(8,128)(2,1)S(1)}, bf16[104,512]{1,0:T(8,128)(2,1)S(1)}, u32[]{:S(2)}, u32[]{:S(2)}) %collective-permute-start.9) | collective-permute-done | bytes 106528 | tf_op jit(solution)/shard_map/ppermute | solution.py:500
  48.6 3.6 %collective-permute-done.15.rest_4_ = bf16[104,512]{1,0:T(8,128)(2,1)S(1)} collective-permute-done((bf16[104,512]{1,0:T(8,128)(2,1)S(1)}, bf16[104,512]{1,0:T(8,128)(2,1)S(1)}, u32[]{:S(2)}, u32[]{:S(2)}) %collective-permute-start.15) | collective-permute-done | bytes 106528 | tf_op jit(solution)/shard_map/ppermute | solution.py:500
  52.2 0.9 %merge.1.a_ref = bf16[96,1024]{1,0:T(8,128)(2,1)S(1)} custom-call(bf16[512,1024]{1,0:T(8,128)(2,1)S(1)} %copy-done.3, bf16[104,512]{1,0:T(8,128)(2,1)S(1)} %get-tuple-element.79.rest_0_, bf16[104,512]{1,0:T(8,128)(2,1)S(1)} %collective-permute-done.9.rest_1_, bf16[104,512]{1,0:T(8,128)(2,1)S(1)} %collective-permute-done.11.rest_2_, ...), custom_call_target="tpu_custom_call" | custom-call | flops 100000000 | bytes 1000000 | tf_op jit(solution)/shard_map/merge/pallas_call | solution.py:627
  53.1 1.6 %collective-permute-start.16 = (bf16[96,1024]{1,0:T(8,128)(2,1)S(1)}, bf16[96,1024]{1,0:T(8,128)(2,1)S(1)}, u32[]{:S(2)}, u32[]{:S(2)}) collective-permute-start(bf16[96,1024]{1,0:T(8,128)(2,1)S(1)} %merge.1.a_ref), channel_id=1, source_target_pairs={{0,1},{1,0},{2,3},{3,2},{4,5},{5,4},{6,7},{7,6},{8,9},{9,8},{10,11... | collective-permute-start | bytes 589832 | tf_op jit(solution)/shard_map/ppermute | solution.py:503
  54.7 5.0 %collective-permute-done.16.b_ref = bf16[96,1024]{1,0:T(8,128)(2,1)S(1)} collective-permute-done((bf16[96,1024]{1,0:T(8,128)(2,1)S(1)}, bf16[96,1024]{1,0:T(8,128)(2,1)S(1)}, u32[]{:S(2)}, u32[]{:S(2)}) %collective-permute-start.16) | collective-permute-done | bytes 196640 | tf_op jit(solution)/shard_map/ppermute | solution.py:503
  59.7 1.7 %ffn.1 = (bf16[96,1024]{1,0:T(8,128)(2,1)S(1)}, bf16[96,1024]{1,0:T(8,128)(2,1)S(1)}) custom-call(bf16[96,1024]{1,0:T(8,128)(2,1)S(1)} %get-tuple-element.68.h_ref, bf16[96,1024]{1,0:T(8,128)(2,1)S(1)} %merge.1.a_ref, bf16[96,1024]{1,0:T(8,128)(2,1)S(1)} %collective-permute-done.16.b_ref, bf16[1024,2048]{1,0:T(8,128)(2,1)S(1)} %copy-done, ...), custom_call_target="tpu_custom_call" | custom-call | flops 100000000 | bytes 1000000 | tf_op jit(solution)/shard_map/ffn/pallas_call | solution.py:639
  61.5 1.6 %collective-permute-start.17 = (bf16[96,1024]{1,0:T(8,128)(2,1)S(1)}, bf16[96,1024]{1,0:T(8,128)(2,1)S(1)}, u32[]{:S(2)}, u32[]{:S(2)}) collective-permute-start(bf16[96,1024]{1,0:T(8,128)(2,1)S(1)} %get-tuple-element.91.a_ref), channel_id=1, source_target_pairs={{0,1},{1,0},{2,3},{3,2},{4,5},{5,4},{6,7},{7,6},{8,9},{9,8},{10,11... | collective-permute-start | bytes 589832 | tf_op jit(solution)/shard_map/ppermute | solution.py:503
  63.0 4.1 %collective-permute-done.17.b_ref = bf16[96,1024]{1,0:T(8,128)(2,1)S(1)} collective-permute-done((bf16[96,1024]{1,0:T(8,128)(2,1)S(1)}, bf16[96,1024]{1,0:T(8,128)(2,1)S(1)}, u32[]{:S(2)}, u32[]{:S(2)}) %collective-permute-start.17) | collective-permute-done | bytes 196640 | tf_op jit(solution)/shard_map/ppermute | solution.py:503
  67.2 0.9 %final.1 = (bf16[2,32,1024]{2,1,0:T(8,128)(2,1)}, bf16[1,32,1024]{2,1,0:T(8,128)(2,1)}) custom-call(bf16[96,1024]{1,0:T(8,128)(2,1)S(1)} %get-tuple-element.90.h_ref, bf16[96,1024]{1,0:T(8,128)(2,1)S(1)} %get-tuple-element.91.a_ref, bf16[96,1024]{1,0:T(8,128)(2,1)S(1)} %collective-permute-done.17.b_ref), custom_call_target="tpu_custom_call" | custom-call | flops 100000000 | bytes 1000000 | tf_op jit(solution)/shard_map/final/pallas_call | solution.py:643
  (43 shorter events, 5.5 us)
Async XLA Ops:
  2.6 14.8 %collective-permute-start.4 = (bf16[2,32,64,512]{3,2,1,0:T(8,128)(2,1)}, bf16[2,32,64,512]{3,2,1,0:T(8,128)(2,1)S(1)}, u32[]{:S(2)}, u32[]{:S(2)}) collective-permute-start(bf16[2,32,64,512]{3,2,1,0:T(8,128)(2,1)} %own_ref), channel_id=1, source_target_pairs={{0,8},{8,0},{16,24},{24,16},{1,9},{9,1},{17,25},{25,17},{2,10},{10... | collective-permute-start | bytes 12582920 | tf_op jit(solution)/shard_map/ppermute | solution.py:530
  3.8 5.7 %copy-start.2 = (bf16[3,1024,512]{2,1,0:T(8,128)(2,1)S(1)}, bf16[3,1024,512]{2,1,0:T(8,128)(2,1)}, u32[]{:S(2)}) copy-start(bf16[3,1024,512]{2,1,0:T(8,128)(2,1)} %w_ref.1) | copy-start | bytes 9437188
  3.8 5.7 %copy-start.6 = (bf16[2,2,512,512]{3,2,1,0:T(8,128)(2,1)S(1)}, bf16[2,2,512,512]{3,2,1,0:T(8,128)(2,1)}, u32[]{:S(2)}) copy-start(bf16[2,2,512,512]{3,2,1,0:T(8,128)(2,1)} %skv_ref) | copy-start | bytes 6291460
  4.3 7.6 %collective-permute-start = (bf16[32,640]{1,0:T(8,128)(2,1)S(1)}, bf16[32,640]{1,0:T(8,128)(2,1)S(1)}, u32[]{:S(2)}, u32[]{:S(2)}) collective-permute-start(bf16[32,640]{1,0:T(8,128)(2,1)S(1)} %long.1.rest_0_), channel_id=1, source_target_pairs={{0,2},{2,0},{4,6},{6,4},{1,3},{3,1},{5,7},{7,5},{8,10},{10,8},{12,... | collective-permute-start | bytes 122888 | tf_op jit(solution)/shard_map/ppermute | solution.py:491
  6.9 5.8 %collective-permute-start.1 = (bf16[32,640]{1,0:T(8,128)(2,1)S(1)}, bf16[32,640]{1,0:T(8,128)(2,1)S(1)}, u32[]{:S(2)}, u32[]{:S(2)}) collective-permute-start(bf16[32,640]{1,0:T(8,128)(2,1)S(1)} %long.1.rest_0_), channel_id=1, source_target_pairs={{0,4},{2,6},{4,0},{6,2},{1,5},{3,7},{5,1},{7,3},{8,12},{10,14},{12... | collective-permute-start | bytes 122888 | tf_op jit(solution)/shard_map/ppermute | solution.py:491
  9.5 5.8 %collective-permute-start.2 = (bf16[32,640]{1,0:T(8,128)(2,1)S(1)}, bf16[32,640]{1,0:T(8,128)(2,1)S(1)}, u32[]{:S(2)}, u32[]{:S(2)}) collective-permute-start(bf16[32,640]{1,0:T(8,128)(2,1)S(1)} %long.1.rest_0_), channel_id=1, source_target_pairs={{0,6},{2,4},{4,2},{6,0},{1,7},{3,5},{5,3},{7,1},{8,14},{10,12},{12... | collective-permute-start | bytes 122888 | tf_op jit(solution)/shard_map/ppermute | solution.py:491
  9.5 5.8 %copy-start.4 = (bf16[512,1024]{1,0:T(8,128)(2,1)S(1)}, bf16[512,1024]{1,0:T(8,128)(2,1)}, u32[]{:S(2)}) copy-start(bf16[512,1024]{1,0:T(8,128)(2,1)} %wo_ref) | copy-start | bytes 3145732
  9.5 7.8 %copy-start.7 = (s32[32]{0:T(128)S(1)}, s32[32]{0:T(128)}, u32[]{:S(2)}) copy-start(s32[32]{0:T(128)} %doc_ref) | copy-start | bytes 388
  9.5 7.8 %copy-start.8 = (s32[4]{0:T(128)S(1)}, s32[4]{0:T(128)}, u32[]{:S(2)}) copy-start(s32[4]{0:T(128)} %long_ref.1) | copy-start | bytes 52
  15.8 5.8 %copy-start.5 = (bf16[1024,512]{1,0:T(8,128)(2,1)S(1)}, bf16[1024,512]{1,0:T(8,128)(2,1)}, u32[]{:S(2)}) copy-start(bf16[1024,512]{1,0:T(8,128)(2,1)} %w_ref.2) | copy-start | bytes 3145732
  15.8 5.7 %collective-permute-start.3 = (bf16[96,1024]{1,0:T(8,128)(2,1)S(1)}, bf16[96,1024]{1,0:T(8,128)(2,1)S(1)}, u32[]{:S(2)}, u32[]{:S(2)}) collective-permute-start(bf16[96,1024]{1,0:T(8,128)(2,1)S(1)} %output.1.a_ref), channel_id=1, source_target_pairs={{0,1},{1,0},{2,3},{3,2},{4,5},{5,4},{6,7},{7,6},{8,9},{9,8},{10,11... | collective-permute-start | bytes 589832 | tf_op jit(solution)/shard_map/ppermute | solution.py:503
  22.0 7.0 %collective-permute-start.5 = (bf16[64,512]{1,0:T(8,128)(2,1)S(1)}, bf16[64,512]{1,0:T(8,128)(2,1)S(1)}, u32[]{:S(2)}, u32[]{:S(2)}) collective-permute-start(bf16[64,512]{1,0:T(8,128)(2,1)S(1)} %get-tuple-element.73), channel_id=1, source_target_pairs={{0,2},{2,0},{4,6},{6,4},{1,3},{3,1},{5,7},{7,5},{8,10},{10,8},{12,... | collective-permute-start | bytes 196616 | tf_op jit(solution)/shard_map/ppermute | solution.py:491
  22.1 7.0 %collective-permute-start.6 = (bf16[64,512]{1,0:T(8,128)(2,1)S(1)}, bf16[64,512]{1,0:T(8,128)(2,1)S(1)}, u32[]{:S(2)}, u32[]{:S(2)}) collective-permute-start(bf16[64,512]{1,0:T(8,128)(2,1)S(1)} %get-tuple-element.73), channel_id=1, source_target_pairs={{0,4},{2,6},{4,0},{6,2},{1,5},{3,7},{5,1},{7,3},{8,12},{10,14},{12... | collective-permute-start | bytes 196616 | tf_op jit(solution)/shard_map/ppermute | solution.py:491
  24.0 6.1 %collective-permute-start.7 = (bf16[64,512]{1,0:T(8,128)(2,1)S(1)}, bf16[64,512]{1,0:T(8,128)(2,1)S(1)}, u32[]{:S(2)}, u32[]{:S(2)}) collective-permute-start(bf16[64,512]{1,0:T(8,128)(2,1)S(1)} %get-tuple-element.73), channel_id=1, source_target_pairs={{0,6},{2,4},{4,2},{6,0},{1,7},{3,5},{5,3},{7,1},{8,14},{10,12},{12... | collective-permute-start | bytes 196616 | tf_op jit(solution)/shard_map/ppermute | solution.py:491
  26.5 7.4 %collective-permute-start.10 = (bf16[96,512]{1,0:T(8,128)(2,1)S(1)}, bf16[96,512]{1,0:T(8,128)(2,1)S(1)}, u32[]{:S(2)}, u32[]{:S(2)}) collective-permute-start(bf16[96,512]{1,0:T(8,128)(2,1)S(1)} %get-tuple-element.70.q_ref), channel_id=1, source_target_pairs={{0,16},{2,18},{4,20},{6,22},{8,24},{10,26},{12,28},{14,30},{16,0},... | collective-permute-start | bytes 294920 | tf_op jit(solution)/shard_map/ppermute | solution.py:500
  30.1 6.9 %collective-permute-start.12 = (bf16[192,512]{1,0:T(8,128)(2,1)S(1)}, bf16[192,512]{1,0:T(8,128)(2,1)S(1)}, u32[]{:S(2)}, u32[]{:S(2)}) collective-permute-start(bf16[192,512]{1,0:T(8,128)(2,1)S(1)} %constant_dynamic-update-slice_fusion.q_ref), channel_id=1, source_target_pairs={{0,16},{2,18},{4,20},{6,22},{8,24},{10,26},{12,28},{14,30},{16,0},... | collective-permute-start | bytes 589832 | tf_op jit(solution)/shard_map/ppermute | solution.py:500
  33.1 9.2 %collective-permute-start.8 = (bf16[2,104,512]{2,1,0:T(8,128)(2,1)S(1)}, bf16[2,104,512]{2,1,0:T(8,128)(2,1)S(1)}, u32[]{:S(2)}, u32[]{:S(2)}) collective-permute-start(bf16[2,104,512]{2,1,0:T(8,128)(2,1)S(1)} %row.4), channel_id=1, source_target_pairs={{0,2},{2,0},{4,6},{6,4},{1,3},{3,1},{5,7},{7,5},{8,10},{10,8},{12,... | collective-permute-start | bytes 638984 | tf_op jit(solution)/shard_map/ppermute | solution.py:491
  34.9 12.0 %collective-permute-start.11 = (bf16[104,512]{1,0:T(8,128)(2,1)S(1)}, bf16[104,512]{1,0:T(8,128)(2,1)S(1)}, u32[]{:S(2)}, u32[]{:S(2)}) collective-permute-start(bf16[104,512]{1,0:T(8,128)(2,1)S(1)} %get-tuple-element.83), channel_id=1, source_target_pairs={{0,16},{2,18},{4,20},{6,22},{8,24},{10,26},{12,28},{14,30},{16,0},... | collective-permute-start | bytes 319496 | tf_op jit(solution)/shard_map/ppermute | solution.py:500
  38.3 5.9 %collective-permute-start.14 = (bf16[1,104,512]{2,1,0:T(8,128)(2,1)S(1)}, bf16[1,104,512]{2,1,0:T(8,128)(2,1)S(1)}, u32[]{:S(2)}, u32[]{:S(2)}) collective-permute-start(bf16[1,104,512]{2,1,0:T(8,128)(2,1)S(1)} %get-tuple-element.88), channel_id=1, source_target_pairs={{0,2},{2,0},{4,6},{6,4},{1,3},{3,1},{5,7},{7,5},{8,10},{10,8},{12,... | collective-permute-start | bytes 319496 | tf_op jit(solution)/shard_map/ppermute | solution.py:491
  38.9 8.0 %collective-permute-start.13 = (bf16[104,512]{1,0:T(8,128)(2,1)S(1)}, bf16[104,512]{1,0:T(8,128)(2,1)S(1)}, u32[]{:S(2)}, u32[]{:S(2)}) collective-permute-start(bf16[104,512]{1,0:T(8,128)(2,1)S(1)} %get-tuple-element.87), channel_id=1, source_target_pairs={{0,18},{2,16},{4,22},{6,20},{8,26},{10,24},{12,30},{14,28},{16,2},... | collective-permute-start | bytes 319496 | tf_op jit(solution)/shard_map/ppermute | solution.py:500
  42.8 5.9 %collective-permute-start.9 = (bf16[104,512]{1,0:T(8,128)(2,1)S(1)}, bf16[104,512]{1,0:T(8,128)(2,1)S(1)}, u32[]{:S(2)}, u32[]{:S(2)}) collective-permute-start(bf16[104,512]{1,0:T(8,128)(2,1)S(1)} %get-tuple-element.80), channel_id=1, source_target_pairs={{0,4},{2,6},{4,0},{6,2},{8,12},{10,14},{12,8},{14,10},{16,20},{18,... | collective-permute-start | bytes 319496 | tf_op jit(solution)/shard_map/ppermute | solution.py:500
  44.2 8.0 %copy-start.3 = (bf16[512,1024]{1,0:T(8,128)(2,1)S(1)}, bf16[512,1024]{1,0:T(8,128)(2,1)}, u32[]{:S(2)}) copy-start(bf16[512,1024]{1,0:T(8,128)(2,1)} %w_ref.3) | copy-start | bytes 3145732
  44.2 15.5 %copy-start = (bf16[1024,2048]{1,0:T(8,128)(2,1)S(1)}, bf16[1024,2048]{1,0:T(8,128)(2,1)}, u32[]{:S(2)}) copy-start(bf16[1024,2048]{1,0:T(8,128)(2,1)} %up_ref.1) | copy-start | bytes 12582916
  44.2 15.5 %copy-start.1 = (bf16[2048,1024]{1,0:T(8,128)(2,1)S(1)}, bf16[2048,1024]{1,0:T(8,128)(2,1)}, u32[]{:S(2)}) copy-start(bf16[2048,1024]{1,0:T(8,128)(2,1)} %down_ref.1) | copy-start | bytes 12582916
  44.5 7.7 %collective-permute-start.15 = (bf16[104,512]{1,0:T(8,128)(2,1)S(1)}, bf16[104,512]{1,0:T(8,128)(2,1)S(1)}, u32[]{:S(2)}, u32[]{:S(2)}) collective-permute-start(bf16[104,512]{1,0:T(8,128)(2,1)S(1)} %join.3), channel_id=1, source_target_pairs={{0,20},{2,22},{4,16},{6,18},{8,28},{10,30},{12,24},{14,26},{16,4},... | collective-permute-start | bytes 319496 | tf_op jit(solution)/shard_map/ppermute | solution.py:500
  53.1 6.6 %collective-permute-start.16 = (bf16[96,1024]{1,0:T(8,128)(2,1)S(1)}, bf16[96,1024]{1,0:T(8,128)(2,1)S(1)}, u32[]{:S(2)}, u32[]{:S(2)}) collective-permute-start(bf16[96,1024]{1,0:T(8,128)(2,1)S(1)} %merge.1.a_ref), channel_id=1, source_target_pairs={{0,1},{1,0},{2,3},{3,2},{4,5},{5,4},{6,7},{7,6},{8,9},{9,8},{10,11... | collective-permute-start | bytes 589832 | tf_op jit(solution)/shard_map/ppermute | solution.py:503
  61.5 5.7 %collective-permute-start.17 = (bf16[96,1024]{1,0:T(8,128)(2,1)S(1)}, bf16[96,1024]{1,0:T(8,128)(2,1)S(1)}, u32[]{:S(2)}, u32[]{:S(2)}) collective-permute-start(bf16[96,1024]{1,0:T(8,128)(2,1)S(1)} %get-tuple-element.91.a_ref), channel_id=1, source_target_pairs={{0,1},{1,0},{2,3},{3,2},{4,5},{5,4},{6,7},{7,6},{8,9},{9,8},{10,11... | collective-permute-start | bytes 589832 | tf_op jit(solution)/shard_map/ppermute | solution.py:503
